TPU v7x, 256 devices: a whole 4x4x8 slice. The times are simulated.
256 devices in a mesh: dp: 16 (over z_lo, y, core), mp: 16 (over x, z_hi).
Axes of the slice: x: 4, y: 4, z: 8 (z_hi: 4, z_lo: 2; z = z_hi * 2 + z_lo), core: 2. Of those that a mesh axis runs over, the one named last changes fastest.
Arguments:
- tokens: bfloat16 [2048, 4096], P('dp', 'mp'), may hold values from -6 to 6
- cotangent: bfloat16 [2048, 4096], P('dp', 'mp'), may hold values from -6 to 6
- block_cols: int32 [64, 32], replicated, may hold values from 0 to 255, as said below
- in_weights: bfloat16 [4096, 4096], P('mp'), may hold values from -0.25 to 0.25
- out_weights: bfloat16 [4096, 4096], P('mp'), may hold values from -0.125 to 0.125
Outputs:
- layer_out: bfloat16 [2048, 4096], P('dp', 'mp')
- token_grad: bfloat16 [2048, 4096], P('dp', 'mp')
- in_weight_grad: float32 [4096, 4096], P(('mp', 'dp'))
- out_weight_grad: float32 [4096, 4096], P(('mp', 'dp'))
Inputs may be any that keep to these rules, and one draw needn't show every extreme that they name: `block_cols`: each row lists 32 different hidden blocks in increasing order. The entries naming hidden blocks of one hidden group number at most 256, and exactly 256 for one group in every draw; one row has at most 4 entries in one hidden group.
All inputs are finite; a program needn't handle non-finite values.
Results may differ from a plain program's by a relative error of at most 0.017.
Values may be sent and summed in bfloat16 or wider, within the bound.
No kernel may reach another device: no remote copies, remote signals or barrier semaphores. Data moves between devices by JAX's collectives and lax.ppermute only.
A program may use at most 128 MiB of HBM per device.

v0:
```python
import jax
import jax.numpy as jnp
from jax import lax
from jax.sharding import PartitionSpec as P

D = 4096
FF = 16384
BLK = 64


def sent_together(arrays, axis, dim, along):
    ends, at = ([], 0)
    for a in arrays[:-1]:
        at += a.shape[along]
        ends.append(at)
    both = jnp.concatenate(arrays, axis=along)
    return tuple(jnp.split(lax.all_gather(both, axis, axis=dim, tiled=True), ends, axis=along))


def cut_along(value, dim, length):
    shape = value.shape
    blocks = value.reshape(*shape[:dim], length, shape[dim] // length, *shape[dim + 1 :])
    return jnp.moveaxis(blocks, dim, 0)


def sum_at_owner(value, axis, dim):
    length = lax.axis_size(axis)
    blocks = lax.all_to_all(cut_along(value, dim, length), axis, 0, 0, tiled=True)
    return jnp.sum(blocks.astype(jnp.float32), axis=0)


def sent_together_2(arrays, axis, dim, along):
    ends, at = ([], 0)
    for a in arrays[:-1]:
        at += a.shape[along]
        ends.append(at)
    both = jnp.concatenate(arrays, axis=along)
    return tuple(
        jnp.split(lax.psum_scatter(both, axis, scatter_dimension=dim, tiled=True), ends, axis=along)
    )


def slot_tables(block_cols, my_shard, slot_count, local_blocks):
    row_count = block_cols.shape[0]
    per_row = block_cols.shape[1]
    flat_cols = block_cols.reshape(-1)
    is_mine = flat_cols // local_blocks == my_shard
    ranks = jnp.cumsum(is_mine.astype(jnp.int32), dtype=jnp.int32) - 1
    targets = jnp.where(is_mine, ranks, slot_count)
    row_ids = jnp.arange(flat_cols.shape[0], dtype=jnp.int32) // per_row
    slot_row = jnp.full((slot_count,), row_count, jnp.int32).at[targets].set(row_ids, mode="drop")
    local_cols = flat_cols - my_shard * local_blocks
    slot_col = (
        jnp.full((slot_count,), local_blocks, jnp.int32).at[targets].set(local_cols, mode="drop")
    )
    return (slot_row, slot_col)


def take_blocks(blocked, indices):
    return jnp.take(blocked, indices, axis=0, mode="fill", fill_value=0)


def sum_slots(slot_terms, indices, block_count):
    return jax.ops.segment_sum(slot_terms, indices, num_segments=block_count)


def gelu_tanh(values):
    return jax.nn.gelu(values, approximate=True)


def on_device(tokens, cotangent, block_cols, in_weights, out_weights):
    model_parts = lax.axis_size("mp")
    my_shard = lax.axis_index("mp")
    local_blocks = FF // BLK // model_parts
    model_blocks = D // BLK
    slot_count = in_weights.shape[0]
    tok_count = tokens.shape[0]
    slot_row, slot_col = slot_tables(block_cols, my_shard, slot_count, local_blocks)
    in_blocks = in_weights.reshape(slot_count, BLK, BLK)
    out_blocks = out_weights.reshape(slot_count, BLK, BLK)
    grad_scale = float(tok_count * lax.axis_size("dp")) ** (-0.5)
    feature_cols, grad_cols = sent_together((tokens.T, cotangent.T), "mp", 0, 1)
    token_blocks = take_blocks(feature_cols.reshape(model_blocks, BLK, tok_count), slot_row)
    pre_terms = jnp.einsum(
        "sit,sij->sjt", token_blocks, in_blocks, preferred_element_type=jnp.float32
    )
    hidden = sum_slots(pre_terms, slot_col, local_blocks)
    activated = gelu_tanh(hidden).astype(jnp.bfloat16)
    act_blocks = take_blocks(activated, slot_col)
    out_terms = jnp.einsum(
        "sjt,sjm->smt", act_blocks, out_blocks, preferred_element_type=jnp.float32
    )
    out_part = sum_slots(out_terms, slot_row, model_blocks).reshape(model_blocks * BLK, tok_count)
    layer_out = sum_at_owner(out_part.astype(jnp.bfloat16), "mp", 0).astype(jnp.bfloat16).T
    grad_blocks = take_blocks(grad_cols.reshape(model_blocks, BLK, tok_count), slot_row)
    back_terms = jnp.einsum(
        "smt,sjm->sjt", grad_blocks, out_blocks, preferred_element_type=jnp.float32
    )
    act_grad = sum_slots(back_terms, slot_col, local_blocks)
    pullback = jax.vjp(gelu_tanh, hidden)[1]
    pre_grad = pullback(act_grad)[0].astype(jnp.bfloat16)
    pre_blocks = take_blocks(pre_grad, slot_col)
    input_terms = jnp.einsum(
        "sjt,sij->sit", pre_blocks, in_blocks, preferred_element_type=jnp.float32
    )
    in_part = sum_slots(input_terms, slot_row, model_blocks).reshape(model_blocks * BLK, tok_count)
    token_grad = sum_at_owner(in_part.astype(jnp.bfloat16), "mp", 0).astype(jnp.bfloat16).T
    in_term = jnp.einsum(
        "sit,sjt->sij", token_blocks, pre_blocks, preferred_element_type=jnp.float32
    )
    in_flat = (grad_scale * in_term).reshape(slot_count, BLK * BLK)
    out_term = jnp.einsum(
        "sjt,smt->sjm", act_blocks, grad_blocks, preferred_element_type=jnp.float32
    )
    out_flat = (grad_scale * out_term).reshape(slot_count, BLK * BLK)
    in_weight_grad, out_weight_grad = tuple(
        (
            part.astype(jnp.float32)
            for part in sent_together_2(
                (in_flat.astype(jnp.bfloat16), out_flat.astype(jnp.bfloat16)), "dp", 0, 1
            )
        )
    )
    return (layer_out, token_grad, in_weight_grad, out_weight_grad)


def solution(mesh):
    placed = (P("dp", "mp"), P("dp", "mp"), P(), P("mp", None), P("mp", None))
    return jax.shard_map(
        on_device,
        mesh=mesh,
        in_specs=placed,
        out_specs=(P("dp", "mp"), P("dp", "mp"), P(("mp", "dp"), None), P(("mp", "dp"), None)),
        check_vma=False,
    )
```

profile of v0, /device:TPU:8, one launch (start us, length us, event | category | flops | bytes accessed | tf_op | source)
XLA Modules:
  0.0 321.1 jit_solution(2677630481925903926)
XLA Ops:
  12.1 3.3 %copy.32 = bf16[256,4096]{0,1:T(8,128)(2,1)S(1)} copy(bf16[256,4096]{1,0:T(8,128)(2,1)} %param.12) | data formatting | bytes 4194304 | tf_op args[3]
  15.4 6.7 %copy.37 = bf16[256,64,64]{2,1,0:T(8,128)(2,1)} copy(bf16[256,64,64]{0,2,1:T(8,128)(2,1)S(1)} %bitcast.29) | data formatting | bytes 4194304 | tf_op jit(solution)/shard_map/reshape | solution.py:79
  22.1 3.3 %copy.34 = bf16[256,4096]{0,1:T(8,128)(2,1)S(1)} copy(bf16[256,4096]{1,0:T(8,128)(2,1)} %param.13) | data formatting | bytes 4194304 | tf_op args[4]
  25.3 6.6 %copy.36 = bf16[256,64,64]{2,1,0:T(8,128)(2,1)} copy(bf16[256,64,64]{0,2,1:T(8,128)(2,1)S(1)} %bitcast.30) | data formatting | bytes 4194304 | tf_op jit(solution)/shard_map/reshape | solution.py:80
  32.2 8.0 %scatter_custom_fusion.1 = s32[256]{0:T(256)S(1)} fusion(s32[2048]{0:T(1024)S(1)} %bitcast.38, s32[2048]{0:T(1024)S(1)} %reshape.228, s32[]{:T(128)} %constant.78.clone.1), kind=kCustom, calls=%fused_computation.63 | custom fusion | bytes 1028 | tf_op jit(solution)/shard_map/scatter | solution.py:54
  40.3 8.0 %scatter_custom_fusion = s32[256]{0:T(256)S(1)} fusion(s32[2048]{0:T(1024)S(1)} %bitcast.39, s32[2048]{0:T(1024)S(1)} %add_select_fusion, s32[]{:T(128)} %constant.68.clone.1), kind=kCustom, calls=%fused_computation.65 | custom fusion | bytes 1028 | tf_op jit(solution)/shard_map/scatter | solution.py:51
  48.4 24.6 %all-gather.2.cloned.1.call-done = bf16[4096,256]{1,0:T(8,128)(2,1)} async-done(((bf16[256,256]{1,0:T(8,128)(2,1)}), bf16[4096,256]{1,0:T(8,128)(2,1)}) %all-gather.2.cloned.1.call-update) | async-done | bytes 2097168 | tf_op jit(solution)/shard_map/all_gather | solution.py:17
  73.0 1.7 fusion.24
  74.7 3.0 gather_fusion
  77.7 3.1 gather_fusion.2
  80.8 8.5 %convolution_bitcast_fusion.3 = f32[256,64,128]{2,1,0:T(8,128)} fusion(bf16[256,64,64]{2,1,0:T(8,128)(2,1)} %copy.37, bf16[256,64,128]{2,1,0:T(8,128)(2,1)} %gather_fusion, pred[256]{0:T(512)(128)(4,1)S(1)} %get-tuple-element.21), kind=kOutput, calls=%fused_computation.20 | convolution fusion | flops 270532608 | bytes 14680320 | tf_op jit(solution)/shard_map/sit,sij->sjt/dot_general | solution.py:84
  89.3 26.4 %scatter_fusion = f32[16,64,128]{2,1,0:T(8,128)S(1)} fusion(f32[16,64,128]{2,1,0:T(8,128)S(1)} %broadcast.154.clone, s32[256]{0:T(256)S(1)} %scatter_custom_fusion.1, f32[256,64,128]{2,1,0:T(8,128)} %convolution_bitcast_fusion.3), kind=kCustom, calls=%fused_computation.6 | custom fusion | flops 2097152 | bytes 25166848 | tf_op jit(solution)/shard_map/scatter-add | solution.py:64
  115.8 8.0 %convolution_bitcast_fusion.1 = f32[256,64,128]{2,1,0:T(8,128)} fusion(bf16[256,64,64]{2,1,0:T(8,128)(2,1)} %copy.36, bf16[256,64,128]{2,1,0:T(8,128)(2,1)} %gather_fusion.2, pred[256]{0:T(512)(128)(4,1)S(1)} %get-tuple-element.21), kind=kOutput, calls=%fused_computation.18 | convolution fusion | flops 270532608 | bytes 14680320 | tf_op jit(solution)/shard_map/smt,sjm->sjt/dot_general | solution.py:96
  123.8 26.3 %scatter_fusion.2 = f32[16,64,128]{2,1,0:T(8,128)S(1)} fusion(f32[16,64,128]{2,1,0:T(8,128)S(1)} %broadcast.154.clone.1, s32[256]{0:T(256)S(1)} %scatter_custom_fusion.1, f32[256,64,128]{2,1,0:T(8,128)} %convolution_bitcast_fusion.1), kind=kCustom, calls=%fused_computation.8 | custom fusion | flops 2097152 | bytes 25166848 | tf_op jit(solution)/shard_map/scatter-add | solution.py:64
  150.5 3.1 gather_fusion.3
  153.6 7.8 %multiply_convert_fusion.1 = bf16[256,64,64]{2,1,0:T(8,128)(2,1)} fusion(bf16[256,64,128]{2,1,0:T(8,128)(2,1)} %gather_fusion, pred[256]{0:T(512)(128)(4,1)S(1)} %get-tuple-element.21, bf16[256,64,128]{2,1,0:T(8,128)(2,1)} %gather_fusion.3, pred[256]{0:T(512)(128)(4,1)S(1)} %get-tuple-element.20), kind=kOutput, calls=%fused_computation.11 | convolution fusion | flops 274726912 | bytes 10486272 | tf_op jit(solution)/shard_map/sit,sjt->sij/dot_general | solution.py:108
  161.4 4.9 %copy.38 = bf16[256,64,64]{0,2,1:T(8,128)(2,1)S(1)} copy(bf16[256,64,64]{2,1,0:T(8,128)(2,1)} %multiply_convert_fusion.1) | data formatting | bytes 4194304 | tf_op jit(solution)/shard_map/convert_element_type | solution.py:120
  166.3 3.0 gather_fusion.1
  169.3 7.8 %multiply_convert_fusion = bf16[256,64,64]{2,1,0:T(8,128)(2,1)} fusion(bf16[256,64,128]{2,1,0:T(8,128)(2,1)} %gather_fusion.2, pred[256]{0:T(512)(128)(4,1)S(1)} %get-tuple-element.21, bf16[256,64,128]{2,1,0:T(8,128)(2,1)} %gather_fusion.1, pred[256]{0:T(512)(128)(4,1)S(1)} %get-tuple-element.20), kind=kOutput, calls=%fused_computation.10 | convolution fusion | flops 274726912 | bytes 10486272 | tf_op jit(solution)/shard_map/sjt,smt->sjm/dot_general | solution.py:112
  177.1 5.9 %copy.39 = bf16[256,64,64]{0,2,1:T(8,128)(2,1)} copy(bf16[256,64,64]{2,1,0:T(8,128)(2,1)} %multiply_convert_fusion) | data formatting | bytes 4194304 | tf_op jit(solution)/shard_map/convert_element_type | solution.py:120
  183.0 3.8 %pad_maximum_fusion = bf16[256,8192]{0,1:T(8,128)(2,1)} fusion(bf16[256,4096]{0,1:T(8,128)(2,1)} %bitcast.32, bf16[256,4096]{0,1:T(8,128)(2,1)S(1)} %bitcast.31), kind=kLoop, calls=%fused_computation.12 | loop fusion | flops 8388608 | bytes 8388608 | tf_op jit(solution)/shard_map/concatenate | solution.py:37
  186.8 6.4 %copy.44 = bf16[256,8192]{1,0:T(8,128)(2,1)} copy(bf16[256,8192]{0,1:T(8,128)(2,1)} %pad_maximum_fusion) | data formatting | bytes 8388608
  193.2 8.0 %convolution_bitcast_fusion = f32[256,64,128]{2,1,0:T(8,128)} fusion(bf16[256,64,64]{2,1,0:T(8,128)(2,1)} %copy.37, bf16[256,64,128]{2,1,0:T(8,128)(2,1)} %gather_fusion.3, pred[256]{0:T(512)(128)(4,1)S(1)} %get-tuple-element.20), kind=kOutput, calls=%fused_computation.17 | convolution fusion | flops 270532608 | bytes 14680320 | tf_op jit(solution)/shard_map/sjt,sij->sit/dot_general | solution.py:103
  201.4 26.4 %scatter_fusion.3 = f32[64,64,128]{2,1,0:T(8,128)S(1)} fusion(f32[64,64,128]{2,1,0:T(8,128)S(1)} %broadcast.147.clone.1, s32[256]{0:T(256)S(1)} %scatter_custom_fusion, f32[256,64,128]{2,1,0:T(8,128)} %convolution_bitcast_fusion), kind=kCustom, calls=%fused_computation.9 | custom fusion | flops 2097152 | bytes 25166848 | tf_op jit(solution)/shard_map/scatter-add | solution.py:64
  227.9 1.3 convert_element_type.51
  229.1 6.3 %all-to-all-start.1 = ((bf16[16,256,128]{2,1,0:T(8,128)(2,1)}), bf16[16,256,128]{2,1,0:T(8,128)(2,1)S(1)}, u32[]{:S(2)}, u32[]{:S(2)}) async-start(bf16[16,256,128]{2,1,0:T(8,128)(2,1)} %bitcast.14), calls=%async_computation.1 | async-start | bytes 2097152 | tf_op jit(solution)/shard_map/all_to_all | solution.py:28
  235.5 8.6 %convolution_bitcast_fusion.2 = f32[256,64,128]{2,1,0:T(8,128)} fusion(bf16[256,64,64]{2,1,0:T(8,128)(2,1)} %copy.36, bf16[256,64,128]{2,1,0:T(8,128)(2,1)} %gather_fusion.1, pred[256]{0:T(512)(128)(4,1)S(1)} %get-tuple-element.20), kind=kOutput, calls=%fused_computation.19 | convolution fusion | flops 270532608 | bytes 14680320 | tf_op jit(solution)/shard_map/sjt,sjm->smt/dot_general | solution.py:90
  244.4 26.3 %scatter_fusion.1 = f32[64,64,128]{2,1,0:T(8,128)S(1)} fusion(f32[64,64,128]{2,1,0:T(8,128)S(1)} %broadcast.147.clone, s32[256]{0:T(256)S(1)} %scatter_custom_fusion, f32[256,64,128]{2,1,0:T(8,128)} %convolution_bitcast_fusion.2), kind=kCustom, calls=%fused_computation.7 | custom fusion | flops 2097152 | bytes 25166848 | tf_op jit(solution)/shard_map/scatter-add | solution.py:64
  270.7 1.2 convert_element_type.48
  271.9 9.6 %all-to-all-start = ((bf16[16,256,128]{2,1,0:T(8,128)(2,1)}), bf16[16,256,128]{2,1,0:T(8,128)(2,1)S(1)}, u32[]{:S(2)}, u32[]{:S(2)}) async-start(bf16[16,256,128]{2,1,0:T(8,128)(2,1)} %bitcast.9), calls=%async_computation | async-start | bytes 2097152 | tf_op jit(solution)/shard_map/all_to_all | solution.py:28
  282.4 27.0 %all-to-all-done = bf16[16,256,128]{2,1,0:T(8,128)(2,1)S(1)} async-done(((bf16[16,256,128]{2,1,0:T(8,128)(2,1)}), bf16[16,256,128]{2,1,0:T(8,128)(2,1)S(1)}, u32[]{:S(2)}, u32[]{:S(2)}) %all-to-all-start) | async-done | bytes 1048608 | tf_op jit(solution)/shard_map/all_to_all | solution.py:28
  311.7 1.0 copy.42
  (41 shorter events, 10.9 us)
Async XLA Ops:
  7.2 65.9 %all-gather.2.cloned.1.call-start = ((), (), s32[]{:S(2)}) async-start(), calls=%async_computation.3 | async-start | bytes 2228224 | tf_op jit(solution)/shard_map/all_gather | solution.py:17
  9.8 300.4 %reduce-scatter.4.cloned.1.call-start = ((), (), s32[]{:S(2)}) async-start(), calls=%async_computation.4 | async-start | bytes 4456448
  229.1 42.7 %all-to-all-start.1 = ((bf16[16,256,128]{2,1,0:T(8,128)(2,1)}), bf16[16,256,128]{2,1,0:T(8,128)(2,1)S(1)}, u32[]{:S(2)}, u32[]{:S(2)}) async-start(bf16[16,256,128]{2,1,0:T(8,128)(2,1)} %bitcast.14), calls=%async_computation.1 | async-start | bytes 2097152 | tf_op jit(solution)/shard_map/all_to_all | solution.py:28
  271.9 37.5 %all-to-all-start = ((bf16[16,256,128]{2,1,0:T(8,128)(2,1)}), bf16[16,256,128]{2,1,0:T(8,128)(2,1)S(1)}, u32[]{:S(2)}, u32[]{:S(2)}) async-start(bf16[16,256,128]{2,1,0:T(8,128)(2,1)} %bitcast.9), calls=%async_computation | async-start | bytes 2097152 | tf_op jit(solution)/shard_map/all_to_all | solution.py:28
Sparse Core Ops, SparseCore 0:
  11.0 61.9 all-gather.1
  193.3 77.0 reduce-scatter.3
where the time goes:
time: 325 us; the launch traced here: 321 us
  other arithmetic  114 us (35%)
  local copies, waits for them, and re-layouts  76.2 us (23%)
  waiting for transfers between devices  51.6 us (16%)
  matrix products  48.7 us (15%)
  starting transfers between devices  16 us (5%)
  between operations  14.3 us (4%)
    scatter-add x4, other arithmetic, sum_slots(): return jax.ops.segment_sum(slot_terms, indices, num_segments=block_count)  105 us
    all_to_all x2, waiting for transfers between devices, sum_at_owner(): lax.all_to_all(cut_along(value, dim, length), axis, 0, 0, tiled=True)  27 us
    all_gather x1, waiting for transfers between devices, sent_together(): lax.all_gather(both, axis, axis=dim, tiled=True)  24.6 us
    unnamed x12, local copies, waits for them, and re-layouts  20.1 us
    all_to_all x2, starting transfers between devices, sum_at_owner(): lax.all_to_all(cut_along(value, dim, length), axis, 0, 0, tiled=True)  15.9 us
    gather x4, local copies, waits for them, and re-layouts, take_blocks(): return jnp.take(blocked, indices, axis=0, mode='fill', fill_value=0)  12.2 us
    dot_general x1, matrix products, on_device(): jnp.einsum('sjt,sjm->smt', act_blocks, out_blocks, preferred_element_type...  8.61 us
    dot_general x1, matrix products, on_device(): jnp.einsum('sit,sij->sjt', token_blocks, in_blocks, preferred_element_typ...  8.5 us
  transfers between devices with their start and end apart: 4, of which 2 were waited for; matrix products, arithmetic and copies ran while one was open for 35% of the time, Pallas kernels for 0%

commit v1 on v0

v1 whole, which is shorter than its diff:
```python
import functools

import jax
import jax.numpy as jnp
from jax import lax
from jax.experimental import pallas as pl
from jax.experimental.pallas import tpu as pltpu
from jax.sharding import PartitionSpec as P

D = 4096
FF = 16384
BLK = 64
HBL = 16
VMEM_LIMIT = 60 * 1024 * 1024


def place_of(steps):
    d = steps % 4
    return jnp.where(d == 0, 0, jnp.where(d == 3, 1, jnp.where(d == 1, 2, 3)))


def steps_of(place):
    return jnp.where(place == 0, 0, jnp.where(place == 1, 3, jnp.where(place == 2, 1, 2)))


def slot_tables(block_cols, mp_at, dp_at, slot_count):
    row_count, per_row = block_cols.shape
    flat_cols = block_cols.reshape(1, -1)
    is_mine = flat_cols // HBL == mp_at
    ranks = jnp.cumsum(is_mine.astype(jnp.int32), axis=1, dtype=jnp.int32) - 1
    targets = jnp.where(is_mine, ranks, slot_count)
    row_ids = lax.broadcasted_iota(jnp.int32, flat_cols.shape, 1) // per_row
    packed = row_ids * HBL + flat_cols - mp_at * HBL + 1
    slots = lax.broadcasted_iota(jnp.int32, (slot_count, 1), 0)
    found = jnp.sum(jnp.where(targets == slots, packed, 0), axis=1, dtype=jnp.int32)
    entry = jnp.where(found > 0, found - 1, row_count * HBL)
    run = lax.broadcasted_iota(jnp.int32, (16, 1), 0)
    owner = (mp_at // 4 + steps_of(run // 4)) % 4 * 4 + (mp_at % 4 + steps_of(run % 4)) % 4
    first = jnp.sum((entry[None, :] < owner * (4 * HBL)).astype(jnp.int32), axis=1, dtype=jnp.int32)
    last = jnp.sum((entry[None, :] < (owner + 1) * (4 * HBL)).astype(jnp.int32), axis=1, dtype=jnp.int32)
    row = entry // HBL
    at = place_of(row // 16 - mp_at // 4) * 4 + place_of(row // 4 - mp_at % 4)
    dest = jnp.where(entry < row_count * HBL, (at * 4 + row % 4) * HBL + entry % HBL, row_count * HBL)
    slot = slots[:, 0]
    to = slot // 16
    core, across, deep = (to + dp_at) % 2, place_of(to // 2 - dp_at // 2 % 4), (to // 8 + dp_at // 8) % 2
    send = ((core * 4 + across) * 2 + deep) * 16 + slot % 16
    return dest, send, first, last


def dense_kernel(turned, dest, w_ref, d_ref, lines):
    d_ref[...] = jnp.zeros_like(d_ref)
    at_once = 16
    count = at_once // 2 if turned else at_once
    low = lax.broadcasted_iota(jnp.int32, (count, 2 * BLK), 1) < BLK
    upper = lax.broadcasted_iota(jnp.int32, (BLK, 2 * BLK), 1) >= BLK

    def place(e, block):
        c = e % HBL
        here = d_ref.at[c // 2, pl.ds(pl.multiple_of(e // HBL * BLK, BLK), BLK), :]
        here[...] = jnp.where(upper == (c % 2 == 1), block.astype(jnp.bfloat16), here[...])

    def some(k, carry):
        start = pl.multiple_of(k * at_once, at_once)
        for t in range(BLK // 2):
            two = w_ref[pl.ds(start, at_once), 2 * BLK * t : 2 * BLK * (t + 1)].astype(jnp.float32)
            swapped = pltpu.roll(two, BLK, 1)
            if turned:
                even = jnp.where(low, two[:count], swapped[count:])
                odd = jnp.where(low, swapped[:count], two[count:])
            else:
                even, odd = jnp.where(low, two, swapped), jnp.where(low, swapped, two)
            lines[pl.ds(2 * t, count, stride=BLK), :] = even
            lines[pl.ds(2 * t + 1, count, stride=BLK), :] = odd
        for u in range(count):
            block = lines[u * BLK : (u + 1) * BLK, :]
            if turned:
                both = jnp.concatenate([block, block], axis=0).T
                place(dest[start + u], both[:BLK])
                place(dest[start + u + count], both[BLK:])
            else:
                place(dest[start + u], block)
        return carry

    lax.fori_loop(0, dest.shape[0] // at_once, some, 0)


def dense_weights(dest, weights, turned):
    whole = pl.BlockSpec(memory_space=pltpu.VMEM)
    return pl.pallas_call(
        functools.partial(dense_kernel, turned),
        out_shape=jax.ShapeDtypeStruct((8, D + BLK, 2 * BLK), jnp.bfloat16),
        in_specs=[pl.BlockSpec(memory_space=pltpu.SMEM), whole],
        out_specs=whole,
        scratch_shapes=[pltpu.VMEM((16 * BLK, 2 * BLK), jnp.float32)],
        compiler_params=pltpu.CompilerParams(vmem_limit_bytes=VMEM_LIMIT),
        cost_estimate=pl.CostEstimate(flops=0, transcendentals=0, bytes_accessed=20 << 20),
        name="dense_out" if turned else "dense_in",
    )(dest, weights)


def hidden_kernel(xc_ref, din_ref, dout_ref, act_ref, pre_ref):
    tok = xc_ref.shape[1] // 2
    x = jnp.concatenate([xc_ref[j, :tok, :] for j in range(16)], axis=1)
    c = jnp.concatenate([xc_ref[j, tok:, :] for j in range(16)], axis=1)
    win = jnp.concatenate([din_ref[0], din_ref[1]], axis=1)
    wout = jnp.concatenate([dout_ref[0], dout_ref[1]], axis=1)
    v = jnp.dot(x, win, preferred_element_type=jnp.float32)
    g = jnp.dot(c, wout, preferred_element_type=jnp.float32)
    k0 = 0.7978845608028654
    t = jnp.tanh(k0 * (v + 0.044715 * (v * v * v)))
    act_ref[...] = (0.5 * v * (1.0 + t)).T.astype(jnp.bfloat16)
    slope = 0.5 * (1.0 + t) + 0.5 * v * (1.0 - t * t) * (k0 * (1.0 + 3 * 0.044715 * (v * v)))
    pre_ref[...] = (g * slope).T.astype(jnp.bfloat16)


def hidden_stage(xc, din, dout, tok):
    cost = pl.CostEstimate(flops=4 * tok * D * 1024, transcendentals=tok * 1024, bytes_accessed=18 << 20)
    wide = pl.BlockSpec((2, D, 2 * BLK), lambda q: (q, 0, 0))
    tall = pl.BlockSpec((4 * BLK, tok), lambda q: (q, 0))
    shape = jax.ShapeDtypeStruct((1024, tok), jnp.bfloat16)
    return pl.pallas_call(
        hidden_kernel,
        grid=(4,),
        out_shape=(shape, shape),
        in_specs=[pl.BlockSpec(xc.shape, lambda q: (0, 0, 0)), wide, wide],
        out_specs=(tall, tall),
        compiler_params=pltpu.CompilerParams(vmem_limit_bytes=VMEM_LIMIT),
        cost_estimate=cost,
        name="hidden_stage",
    )(xc, din, dout)


def grad_kernel(scale, dest, send, first, last, xc_ref, act_ref, pre_ref, own_ref, other_ref, g_scr, in_scr, out_scr):
    j = pl.program_id(0)
    tok = act_ref.shape[1]
    at_once = 4

    @pl.when(j == 0)
    def _():
        g_scr[...] = jnp.zeros_like(g_scr)

    gin = jnp.dot(pre_ref[...], xc_ref[0, :tok, :], preferred_element_type=jnp.float32)
    gout = jnp.dot(act_ref[...], xc_ref[0, tok:, :], preferred_element_type=jnp.float32)
    for half in range(2):
        in_scr[half] = gin[:, half * 128 : half * 128 + 128]
        out_scr[half] = gout[:, half * 128 : half * 128 + 128]
    upper = lax.broadcasted_iota(jnp.int32, (BLK, 2 * BLK), 1) >= BLK
    begin, end = first[j], last[j]

    def take(i, carry):
        found = []
        for u in range(at_once):
            s = jnp.minimum(begin + i * at_once + u, end - 1)
            e = dest[s]
            r, c = e // HBL % 4, e % HBL
            tile, odd = r // 2, r % 2
            rows = pl.ds(pl.multiple_of(c * BLK, BLK), BLK)
            low = pltpu.roll(out_scr[tile, rows, :], odd * BLK, 1)
            high = pltpu.roll(in_scr[tile, rows, :], (1 - odd) * BLK, 1)
            found.append((send[s], (jnp.where(upper, high, low) * scale).astype(jnp.bfloat16)))
        for to, block in found:
            g_scr[to] = block
        return carry

    lax.fori_loop(0, (end - begin + at_once - 1) // at_once, take, 0)

    @pl.when(j == pl.num_programs(0) - 1)
    def _():
        half = own_ref.shape[0]
        own_ref[...] = g_scr[:half]
        other_ref[...] = g_scr[half:]


def grad_stage(tables, xc, act, pre, slot_count, scale):
    tok = act.shape[1]
    cost = pl.CostEstimate(flops=4 * tok * D * 1024, transcendentals=0, bytes_accessed=7 << 20)
    whole = pl.BlockSpec(act.shape, lambda j: (0, 0))
    smem = pl.BlockSpec(memory_space=pltpu.SMEM)
    half = (slot_count // 2, BLK, 2 * BLK)
    half_spec = pl.BlockSpec(half, lambda j: (0, 0, 0), pipeline_mode=pl.Buffered(1))
    return pl.pallas_call(
        functools.partial(grad_kernel, scale),
        grid=(16,),
        out_shape=(jax.ShapeDtypeStruct(half, jnp.bfloat16),) * 2,
        in_specs=[smem] * 4 + [pl.BlockSpec((1,) + xc.shape[1:], lambda j: (j, 0, 0)), whole, whole],
        out_specs=(half_spec, half_spec),
        scratch_shapes=[pltpu.VMEM((slot_count, BLK, 2 * BLK), jnp.bfloat16)]
        + [pltpu.VMEM((2, 1024, 128), jnp.float32)] * 2,
        compiler_params=pltpu.CompilerParams(vmem_limit_bytes=VMEM_LIMIT),
        cost_estimate=cost,
        name="grad_stage",
    )(*tables, xc, act, pre)


def part_kernel(din_ref, dout_ref, act_ref, pre_ref, *part_refs):
    j = pl.program_id(0)
    win = jnp.concatenate([din_ref[p] for p in range(8)], axis=1)
    wout = jnp.concatenate([dout_ref[p] for p in range(8)], axis=1)
    out = jnp.dot(wout, act_ref[...], preferred_element_type=jnp.float32).astype(jnp.bfloat16)
    back = jnp.dot(win, pre_ref[...], preferred_element_type=jnp.float32).astype(jnp.bfloat16)
    both = jnp.concatenate([out, back], axis=1)
    for n, ref in enumerate(part_refs):

        @pl.when(j // 2 == n)
        def _():
            ref[...] = both


def part_stage(din, dout, act, pre):
    tok = act.shape[1]
    cost = pl.CostEstimate(flops=4 * tok * D * 1024, transcendentals=0, bytes_accessed=18 << 20)
    whole = pl.BlockSpec(act.shape, lambda j: (0, 0))
    wide = pl.BlockSpec((8, 512, 2 * BLK), lambda j: (0, j, 0))
    pieces = tuple(
        pl.BlockSpec((512, 2 * tok), lambda j, n=n: (jnp.clip(j - 2 * n, 0, 1), 0)) for n in range(4)
    )
    return pl.pallas_call(
        part_kernel,
        grid=(D // 512,),
        out_shape=(jax.ShapeDtypeStruct((1024, 2 * tok), jnp.bfloat16),) * 4,
        in_specs=[wide, wide, whole, whole],
        out_specs=pieces,
        compiler_params=pltpu.CompilerParams(vmem_limit_bytes=VMEM_LIMIT),
        cost_estimate=cost,
        name="part_stage",
    )(din, dout, act, pre)


def total_kernel(own_ref, before_ref, after_ref, opposite_ref, out_ref, back_ref):
    refs = (own_ref, before_ref, after_ref, opposite_ref)
    total = sum(ref[...].astype(jnp.float32) for ref in refs)
    tok = out_ref.shape[0]
    out_ref[...] = total[:, :tok].T.astype(jnp.bfloat16)
    back_ref[...] = total[:, tok:].T.astype(jnp.bfloat16)


def total_turned(terms):
    rows, cols = terms[0].shape
    return pl.pallas_call(
        total_kernel,
        out_shape=(jax.ShapeDtypeStruct((cols // 2, rows), jnp.bfloat16),) * 2,
        name="total_turned",
    )(*terms)


def ring(axis, stride):
    def target(i, by):
        return i - i // stride % 4 * stride + (i // stride + by) % 4 * stride

    return tuple(
        functools.partial(lax.ppermute, axis_name=axis, perm=[(i, target(i, by)) for i in range(16)])
        for by in (1, 3, 2)
    )


def spread(block, up, down, over):
    return jnp.stack([block, up(block), down(block), over(block)])


def collect(blocks, up, down, over):
    own, before, after, opposite = blocks
    return own, up(after), down(before), over(opposite)


def added(*terms):
    return sum(term.astype(jnp.float32) for term in terms).astype(jnp.bfloat16)


def on_device(tokens, cotangent, block_cols, in_weights, out_weights):
    mp_at, dp_at = lax.axis_index("mp"), lax.axis_index("dp")
    slot_count = in_weights.shape[0]
    tok = tokens.shape[0]
    scale = float(tok * lax.axis_size("dp")) ** (-0.5)
    along_x, along_z, along_y = ring("mp", 4), ring("mp", 1), ring("dp", 2)
    block = jnp.concatenate([tokens, cotangent], axis=0)
    near = spread(block, *along_z)
    tables = slot_tables(block_cols, mp_at, dp_at, slot_count)
    din = dense_weights(tables[0], in_weights, False)
    near, din = lax.optimization_barrier((near, din))
    xc = spread(near, *along_x).reshape(16, 2 * tok, -1)
    dout = dense_weights(tables[0], out_weights, True)
    act, pre = hidden_stage(xc, din, dout, tok)
    mine, other = grad_stage(tables, xc, act, pre, slot_count, scale)
    from_core = lax.ppermute(other, "dp", [(i, i ^ 1) for i in range(16)])
    parts = part_stage(din, dout, act, pre)
    parts, from_core = lax.optimization_barrier((parts, from_core))
    share = slot_count // 8
    pair = [
        added(mine[n * share : (n + 1) * share], from_core[n * share : (n + 1) * share]) for n in range(4)
    ]
    deep_terms = collect(pair, *along_y)
    across_terms = collect(parts, *along_x)
    deep_terms, across_terms = lax.optimization_barrier((deep_terms, across_terms))
    half = share // 2
    from_deep = lax.ppermute(added(*(term[half:] for term in deep_terms)), "dp", [(i, i ^ 8) for i in range(16)])
    rows = across_terms[0].shape[0] // 4
    across = [added(*(term[n * rows : (n + 1) * rows] for term in across_terms)) for n in range(4)]
    layer_out, token_grad = total_turned(collect(across, *along_z))
    summed = sum(term[:half].astype(jnp.float32) for term in deep_terms) + from_deep.astype(jnp.float32)
    out_grad = summed[:, :, :BLK].reshape(-1, BLK * BLK)
    in_grad = summed[:, :, BLK:].swapaxes(1, 2).reshape(-1, BLK * BLK)
    return (layer_out, token_grad, in_grad, out_grad)


def solution(mesh):
    placed = (P("dp", "mp"), P("dp", "mp"), P(), P("mp", None), P("mp", None))
    return jax.shard_map(
        on_device,
        mesh=mesh,
        in_specs=placed,
        out_specs=(P("dp", "mp"), P("dp", "mp"), P(("mp", "dp"), None), P(("mp", "dp"), None)),
        check_vma=False,
    )
```

time: 325 us -> 156 us (0.48)
  the two profiles are of different devices: /device:TPU:8 before, /device:TPU:38 now
where the time goes in v1:
time: 156 us; the launch traced here: 154 us
  Pallas kernels  67.4 us (43%)
  waiting for transfers between devices  39.8 us (26%)
  starting transfers between devices  32.8 us (21%)
  other arithmetic  7.73 us (5%)
  local copies, waits for them, and re-layouts  5.82 us (4%)
    ppermute x9, waiting for transfers between devices, collect(): return (own, up(after), down(before), over(opposite))  32.8 us
    pallas_call x2, Pallas kernels, dense_weights(): pl.pallas_call(functools.partial(dense_kernel, turned), out_shape=jax.Sha...  27.3 us
    ppermute x9, starting transfers between devices, collect(): return (own, up(after), down(before), over(opposite))  17.7 us
    pallas_call x1, Pallas kernels, grad_stage(): pl.pallas_call(functools.partial(grad_kernel, scale), grid=(16,), out_sha...  17.2 us
    ppermute x6, starting transfers between devices, spread(): return jnp.stack([block, up(block), down(block), over(block)])  13.9 us
    pallas_call x1, Pallas kernels, part_stage(): pl.pallas_call(part_kernel, grid=(D // 512,), out_shape=(jax.ShapeDtypeSt...  12 us
    pallas_call x1, Pallas kernels, hidden_stage(): pl.pallas_call(hidden_kernel, grid=(4,), out_shape=(shape, shape), in_spe...  8.99 us
    ppermute x6, waiting for transfers between devices, spread(): return jnp.stack([block, up(block), down(block), over(block)])  7.04 us
  transfers between devices with their start and end apart: 17, of which 5 were waited for; matrix products, arithmetic and copies ran while one was open for 3% of the time, Pallas kernels for 27%

profile of v1, /device:TPU:38, one launch (start us, length us, event | category | flops | bytes accessed | tf_op | source)
XLA Modules:
  0.0 154.3 jit_solution(4773676525916930294)
XLA Ops:
  0.6 0.8 constant_dynamic-update-slice_fusion.1
  1.5 0.8 constant_dynamic-update-slice_fusion
  2.3 6.3 %collective-permute-start.2 = (bf16[256,256]{1,0:T(8,128)(2,1)S(1)}, bf16[256,256]{1,0:T(8,128)(2,1)S(1)}, u32[]{:S(2)}, u32[]{:S(2)}) collective-permute-start(bf16[256,256]{1,0:T(8,128)(2,1)S(1)} %constant_dynamic-update-slice_fusion), channel_id=1, source_target_pairs={{0,2},{1,3},{2,0},{3,1},{4,6},{5,7},{6,4},{7,5},{8,10},{9,11},{10,... | collective-permute-start | bytes 393224 | tf_op jit(solution)/shard_map/ppermute | solution.py:258
  9.2 2.4 %collective-permute-start = (bf16[256,256]{1,0:T(8,128)(2,1)S(1)}, bf16[256,256]{1,0:T(8,128)(2,1)S(1)}, u32[]{:S(2)}, u32[]{:S(2)}) collective-permute-start(bf16[256,256]{1,0:T(8,128)(2,1)S(1)} %constant_dynamic-update-slice_fusion), channel_id=1, source_target_pairs={{0,1},{1,2},{2,3},{3,0},{4,5},{5,6},{6,7},{7,4},{8,9},{9,10},{10,1... | collective-permute-start | bytes 393224 | tf_op jit(solution)/shard_map/ppermute | solution.py:258
  14.2 14.2 %dense_in.1.din_ref = bf16[8,4160,128]{2,1,0:T(8,128)(2,1)} custom-call(s32[256]{0:T(256)} %get-tuple-element.69.dest, bf16[256,4096]{1,0:T(8,128)(2,1)} %w_ref.2), custom_call_target="tpu_custom_call" | custom-call | bytes 20971520 | tf_op jit(solution)/shard_map/dense_in/pallas_call | solution.py:90
  28.5 1.5 collective-permute-start.5
  30.0 3.2 %collective-permute-start.3 = (bf16[4,256,256]{2,1,0:T(8,128)(2,1)S(1)}, bf16[4,256,256]{2,1,0:T(8,128)(2,1)S(1)}, u32[]{:S(2)}, u32[]{:S(2)}) collective-permute-start(bf16[4,256,256]{2,1,0:T(8,128)(2,1)S(1)} %pad_maximum_fusion.1), channel_id=1, source_target_pairs={{0,4},{1,5},{2,6},{3,7},{4,8},{5,9},{6,10},{7,11},{8,12},{9,13},{1... | collective-permute-start | bytes 1572872 | tf_op jit(solution)/shard_map/ppermute | solution.py:258
  33.2 13.1 %dense_out.1.dout_ref = bf16[8,4160,128]{2,1,0:T(8,128)(2,1)} custom-call(s32[256]{0:T(256)} %get-tuple-element.69.dest, bf16[256,4096]{1,0:T(8,128)(2,1)} %w_ref.3), custom_call_target="tpu_custom_call" | custom-call | bytes 20971520 | tf_op jit(solution)/shard_map/dense_out/pallas_call | solution.py:90
  47.1 7.0 %collective-permute-done.4 = bf16[4,256,256]{2,1,0:T(8,128)(2,1)S(1)} collective-permute-done((bf16[4,256,256]{2,1,0:T(8,128)(2,1)S(1)}, bf16[4,256,256]{2,1,0:T(8,128)(2,1)S(1)}, u32[]{:S(2)}, u32[]{:S(2)}) %collective-permute-start.4) | collective-permute-done | bytes 524320 | tf_op jit(solution)/shard_map/ppermute | solution.py:258
  54.1 1.6 %pad_maximum_fusion = bf16[4,4,256,256]{3,2,1,0:T(8,128)(2,1)} fusion(bf16[1,4,256,256]{3,2,1,0:T(8,128)(2,1)S(1)} %bitcast.24, bf16[1,4,256,256]{3,2,1,0:T(8,128)(2,1)S(1)} %bitcast.25, bf16[1,4,256,256]{3,2,1,0:T(8,128)(2,1)S(1)} %bitcast.26, bf16[1,4,256,256]{3,2,1,0:T(8,128)(2,1)S(1)} %bitcast.23), kind=kLoop, calls=%fused_computation | loop fusion | flops 3145728 | bytes 4194304 | tf_op jit(solution)/shard_map/stack | solution.py:258
  55.8 9.0 %hidden_stage.1 = (bf16[1024,128]{1,0:T(8,128)(2,1)}, bf16[1024,128]{1,0:T(8,128)(2,1)}) custom-call(bf16[16,256,256]{2,1,0:T(8,128)(2,1)} %bitcast.21, bf16[8,4160,128]{2,1,0:T(8,128)(2,1)} %dense_in.1.din_ref, bf16[8,4160,128]{2,1,0:T(8,128)(2,1)} %dense_out.1.dout_ref), custom_call_target="tpu_custom_call" | custom-call | flops 2147483648 | bytes 18874368 | tf_op jit(solution)/shard_map/hidden_stage/pallas_call | solution.py:122
  64.7 17.2 %grad_stage.1 = (bf16[128,64,128]{2,1,0:T(8,128)(2,1)}, bf16[128,64,128]{2,1,0:T(8,128)(2,1)}) custom-call(s32[256]{0:T(256)} %get-tuple-element.69.dest, s32[256]{0:T(256)} %get-tuple-element.72.send, s32[16]{0:T(128)} %get-tuple-element.55.first, s32[16]{0:T(128)} %get-tuple-element.54.last, bf16[16,256,256]{2,1,0:T(8,128)(2,1)} %bitcast.22, ...), custom_call_target="tpu_custom_call" | custom-call | flops 2147483648 | bytes 7340032 | tf_op jit(solution)/shard_map/grad_stage/pallas_call | solution.py:182
  82.0 12.0 %part_stage.1 = (bf16[1024,256]{1,0:T(8,128)(2,1)}, bf16[1024,256]{1,0:T(8,128)(2,1)}, bf16[1024,256]{1,0:T(8,128)(2,1)}, bf16[1024,256]{1,0:T(8,128)(2,1)}) custom-call(bf16[8,4160,128]{2,1,0:T(8,128)(2,1)} %dense_in.1.din_ref, bf16[8,4160,128]{2,1,0:T(8,128)(2,1)} %dense_out.1.dout_ref, bf16[1024,128]{1,0:T(8,128)(2,1)} %get-tuple-element.31.act_ref, ...), custom_call_target="tpu_custom_call" | custom-call | flops 2147483648 | bytes 18874368 | tf_op jit(solution)/shard_map/part_stage/pallas_call | solution.py:218
  94.0 2.5 %add_convert_fusion = (bf16[32,64,128]{2,1,0:T(8,128)(2,1)S(1)}, bf16[32,64,128]{2,1,0:T(8,128)(2,1)S(1)}, bf16[32,64,128]{2,1,0:T(8,128)(2,1)S(1)}, bf16[32,64,128]{2,1,0:T(8,128)(2,1)S(1)}) fusion(bf16[128,64,128]{2,1,0:T(8,128)(2,1)} %collective-permute-done.6, bf16[128,64,128]{2,1,0:T(8,128)(2,1)S(1)} %copy-done), kind=kLoop, calls=%fused_computation.3 | loop fusion | flops 4194304 | bytes 6291456 | tf_op jit(solution)/shard_map/convert_element_type | solution.py:267
  96.5 3.3 %collective-permute-start.9 = (bf16[32,64,128]{2,1,0:T(8,128)(2,1)S(1)}, bf16[32,64,128]{2,1,0:T(8,128)(2,1)S(1)}, u32[]{:S(2)}, u32[]{:S(2)}) collective-permute-start(bf16[32,64,128]{2,1,0:T(8,128)(2,1)S(1)} %get-tuple-element.56), channel_id=1, source_target_pairs={{0,64},{16,80},{32,96},{48,112},{64,0},{80,16},{96,32},{112,48},{1... | collective-permute-start | bytes 1572872 | tf_op jit(solution)/shard_map/ppermute | solution.py:263
  99.8 1.0 collective-permute-start.8
  100.9 1.0 collective-permute-start.7
  101.9 0.9 collective-permute-start.10
  102.8 1.1 collective-permute-start.11
  103.9 9.1 %collective-permute-done.9 = bf16[32,64,128]{2,1,0:T(8,128)(2,1)S(1)} collective-permute-done((bf16[32,64,128]{2,1,0:T(8,128)(2,1)S(1)}, bf16[32,64,128]{2,1,0:T(8,128)(2,1)S(1)}, u32[]{:S(2)}, u32[]{:S(2)}) %collective-permute-start.9) | collective-permute-done | bytes 524320 | tf_op jit(solution)/shard_map/ppermute | solution.py:263
  113.0 2.1 %collective-permute-start.12 = (bf16[1024,256]{1,0:T(8,128)(2,1)S(1)}, bf16[1024,256]{1,0:T(8,128)(2,1)S(1)}, u32[]{:S(2)}, u32[]{:S(2)}) collective-permute-start(bf16[1024,256]{1,0:T(8,128)(2,1)S(1)} %copy-done.5), channel_id=1, source_target_pairs={{0,8},{1,9},{2,10},{3,11},{4,12},{5,13},{6,14},{7,15},{8,0},{9,1},... | collective-permute-start | bytes 1572872 | tf_op jit(solution)/shard_map/ppermute | solution.py:263
  115.0 9.0 %collective-permute-done.8 = bf16[32,64,128]{2,1,0:T(8,128)(2,1)S(1)} collective-permute-done((bf16[32,64,128]{2,1,0:T(8,128)(2,1)S(1)}, bf16[32,64,128]{2,1,0:T(8,128)(2,1)S(1)}, u32[]{:S(2)}, u32[]{:S(2)}) %collective-permute-start.8) | collective-permute-done | bytes 524320 | tf_op jit(solution)/shard_map/ppermute | solution.py:263
  124.0 4.2 %collective-permute-done.12 = bf16[1024,256]{1,0:T(8,128)(2,1)S(1)} collective-permute-done((bf16[1024,256]{1,0:T(8,128)(2,1)S(1)}, bf16[1024,256]{1,0:T(8,128)(2,1)S(1)}, u32[]{:S(2)}, u32[]{:S(2)}) %collective-permute-start.12) | collective-permute-done | bytes 524320 | tf_op jit(solution)/shard_map/ppermute | solution.py:263
  128.4 1.1 collective-permute-start.16
  129.5 0.9 add_convert_fusion.5
  130.5 5.4 %collective-permute-start.15 = (bf16[256,256]{1,0:T(8,128)(2,1)S(1)}, bf16[256,256]{1,0:T(8,128)(2,1)S(1)}, u32[]{:S(2)}, u32[]{:S(2)}) collective-permute-start(bf16[256,256]{1,0:T(8,128)(2,1)S(1)} %get-tuple-element.60), channel_id=1, source_target_pairs={{0,2},{1,3},{2,0},{3,1},{4,6},{5,7},{6,4},{7,5},{8,10},{9,11},{10,... | collective-permute-start | bytes 393224 | tf_op jit(solution)/shard_map/ppermute | solution.py:263
  135.8 0.9 collective-permute-start.14
  136.7 2.0 %collective-permute-start.13 = (bf16[256,256]{1,0:T(8,128)(2,1)S(1)}, bf16[256,256]{1,0:T(8,128)(2,1)S(1)}, u32[]{:S(2)}, u32[]{:S(2)}) collective-permute-start(bf16[256,256]{1,0:T(8,128)(2,1)S(1)} %get-tuple-element.62), channel_id=1, source_target_pairs={{0,1},{1,2},{2,3},{3,0},{4,5},{5,6},{6,7},{7,4},{8,9},{9,10},{10,1... | collective-permute-start | bytes 393224 | tf_op jit(solution)/shard_map/ppermute | solution.py:263
  138.8 10.5 %collective-permute-done.15.opposite_ref = bf16[256,256]{1,0:T(8,128)(2,1)S(1)} collective-permute-done((bf16[256,256]{1,0:T(8,128)(2,1)S(1)}, bf16[256,256]{1,0:T(8,128)(2,1)S(1)}, u32[]{:S(2)}, u32[]{:S(2)}) %collective-permute-start.15) | collective-permute-done | bytes 131104 | tf_op jit(solution)/shard_map/ppermute | solution.py:263
  150.0 1.9 %total_turned.1 = (bf16[128,256]{1,0:T(8,128)(2,1)}, bf16[128,256]{1,0:T(8,128)(2,1)}) custom-call(bf16[256,256]{1,0:T(8,128)(2,1)} %get-tuple-element.63.own_ref, bf16[256,256]{1,0:T(8,128)(2,1)} %copy-done.4, bf16[256,256]{1,0:T(8,128)(2,1)} %copy-done.3, bf16[256,256]{1,0:T(8,128)(2,1)} %copy-done.2), custom_call_target="tpu_custom_call" | custom-call | tf_op jit(solution)/shard_map/total_turned/pallas_call | solution.py:240
  152.3 0.9 reshape.424
  153.4 0.9 reshape.423
  (50 shorter events, 5.6 us)
Async XLA Ops:
  2.3 26.1 %collective-permute-start.2 = (bf16[256,256]{1,0:T(8,128)(2,1)S(1)}, bf16[256,256]{1,0:T(8,128)(2,1)S(1)}, u32[]{:S(2)}, u32[]{:S(2)}) collective-permute-start(bf16[256,256]{1,0:T(8,128)(2,1)S(1)} %constant_dynamic-update-slice_fusion), channel_id=1, source_target_pairs={{0,2},{1,3},{2,0},{3,1},{4,6},{5,7},{6,4},{7,5},{8,10},{9,11},{10,... | collective-permute-start | bytes 393224 | tf_op jit(solution)/shard_map/ppermute | solution.py:258
  8.6 19.8 %collective-permute-start.1 = (bf16[256,256]{1,0:T(8,128)(2,1)S(1)}, bf16[256,256]{1,0:T(8,128)(2,1)S(1)}, u32[]{:S(2)}, u32[]{:S(2)}) collective-permute-start(bf16[256,256]{1,0:T(8,128)(2,1)S(1)} %constant_dynamic-update-slice_fusion), channel_id=1, source_target_pairs={{0,3},{1,0},{2,1},{3,2},{4,7},{5,4},{6,5},{7,6},{8,11},{9,8},{10,9... | collective-permute-start | bytes 393224 | tf_op jit(solution)/shard_map/ppermute | solution.py:258
  9.2 19.2 %collective-permute-start = (bf16[256,256]{1,0:T(8,128)(2,1)S(1)}, bf16[256,256]{1,0:T(8,128)(2,1)S(1)}, u32[]{:S(2)}, u32[]{:S(2)}) collective-permute-start(bf16[256,256]{1,0:T(8,128)(2,1)S(1)} %constant_dynamic-update-slice_fusion), channel_id=1, source_target_pairs={{0,1},{1,2},{2,3},{3,0},{4,5},{5,6},{6,7},{7,4},{8,9},{9,10},{10,1... | collective-permute-start | bytes 393224 | tf_op jit(solution)/shard_map/ppermute | solution.py:258
  28.5 18.6 %collective-permute-start.5 = (bf16[4,256,256]{2,1,0:T(8,128)(2,1)S(1)}, bf16[4,256,256]{2,1,0:T(8,128)(2,1)S(1)}, u32[]{:S(2)}, u32[]{:S(2)}) collective-permute-start(bf16[4,256,256]{2,1,0:T(8,128)(2,1)S(1)} %pad_maximum_fusion.1), channel_id=1, source_target_pairs={{0,8},{1,9},{2,10},{3,11},{4,12},{5,13},{6,14},{7,15},{8,0},{9,1},... | collective-permute-start | bytes 1572872 | tf_op jit(solution)/shard_map/ppermute | solution.py:258
  30.0 24.2 %collective-permute-start.4 = (bf16[4,256,256]{2,1,0:T(8,128)(2,1)S(1)}, bf16[4,256,256]{2,1,0:T(8,128)(2,1)S(1)}, u32[]{:S(2)}, u32[]{:S(2)}) collective-permute-start(bf16[4,256,256]{2,1,0:T(8,128)(2,1)S(1)} %pad_maximum_fusion.1), channel_id=1, source_target_pairs={{0,12},{1,13},{2,14},{3,15},{4,0},{5,1},{6,2},{7,3},{8,4},{9,5},{1... | collective-permute-start | bytes 1572872 | tf_op jit(solution)/shard_map/ppermute | solution.py:258
  30.0 24.2 %collective-permute-start.3 = (bf16[4,256,256]{2,1,0:T(8,128)(2,1)S(1)}, bf16[4,256,256]{2,1,0:T(8,128)(2,1)S(1)}, u32[]{:S(2)}, u32[]{:S(2)}) collective-permute-start(bf16[4,256,256]{2,1,0:T(8,128)(2,1)S(1)} %pad_maximum_fusion.1), channel_id=1, source_target_pairs={{0,4},{1,5},{2,6},{3,7},{4,8},{5,9},{6,10},{7,11},{8,12},{9,13},{1... | collective-permute-start | bytes 1572872 | tf_op jit(solution)/shard_map/ppermute | solution.py:258
  81.9 12.0 %copy-start = (bf16[128,64,128]{2,1,0:T(8,128)(2,1)S(1)}, bf16[128,64,128]{2,1,0:T(8,128)(2,1)}, u32[]{:S(2)}) copy-start(bf16[128,64,128]{2,1,0:T(8,128)(2,1)} %get-tuple-element.33) | copy-start | bytes 6291460
  81.9 12.0 %collective-permute-start.6 = (bf16[128,64,128]{2,1,0:T(8,128)(2,1)}, bf16[128,64,128]{2,1,0:T(8,128)(2,1)}, u32[]{:S(2)}, u32[]{:S(2)}) collective-permute-start(bf16[128,64,128]{2,1,0:T(8,128)(2,1)} %get-tuple-element.38), channel_id=1, source_target_pairs={{0,16},{16,0},{32,48},{48,32},{64,80},{80,64},{96,112},{112,96},{1... | collective-permute-start | bytes 6291464 | tf_op jit(solution)/shard_map/ppermute | solution.py:285
  93.9 7.9 %copy-start.7 = (bf16[1024,256]{1,0:T(8,128)(2,1)S(1)}, bf16[1024,256]{1,0:T(8,128)(2,1)}, u32[]{:S(2)}) copy-start(bf16[1024,256]{1,0:T(8,128)(2,1)} %get-tuple-element.41) | copy-start | bytes 1572868
  94.0 8.8 %copy-start.6 = (bf16[1024,256]{1,0:T(8,128)(2,1)S(1)}, bf16[1024,256]{1,0:T(8,128)(2,1)}, u32[]{:S(2)}) copy-start(bf16[1024,256]{1,0:T(8,128)(2,1)} %get-tuple-element.42) | copy-start | bytes 1572868
  94.0 19.0 %copy-start.5 = (bf16[1024,256]{1,0:T(8,128)(2,1)S(1)}, bf16[1024,256]{1,0:T(8,128)(2,1)}, u32[]{:S(2)}) copy-start(bf16[1024,256]{1,0:T(8,128)(2,1)} %get-tuple-element.43) | copy-start | bytes 1572868
  94.0 35.6 %copy-start.1 = (bf16[1024,256]{1,0:T(8,128)(2,1)S(1)}, bf16[1024,256]{1,0:T(8,128)(2,1)}, u32[]{:S(2)}) copy-start(bf16[1024,256]{1,0:T(8,128)(2,1)} %get-tuple-element.44) | copy-start | bytes 1572868
  96.5 16.4 %collective-permute-start.9 = (bf16[32,64,128]{2,1,0:T(8,128)(2,1)S(1)}, bf16[32,64,128]{2,1,0:T(8,128)(2,1)S(1)}, u32[]{:S(2)}, u32[]{:S(2)}) collective-permute-start(bf16[32,64,128]{2,1,0:T(8,128)(2,1)S(1)} %get-tuple-element.56), channel_id=1, source_target_pairs={{0,64},{16,80},{32,96},{48,112},{64,0},{80,16},{96,32},{112,48},{1... | collective-permute-start | bytes 1572872 | tf_op jit(solution)/shard_map/ppermute | solution.py:263
  99.8 24.2 %collective-permute-start.8 = (bf16[32,64,128]{2,1,0:T(8,128)(2,1)S(1)}, bf16[32,64,128]{2,1,0:T(8,128)(2,1)S(1)}, u32[]{:S(2)}, u32[]{:S(2)}) collective-permute-start(bf16[32,64,128]{2,1,0:T(8,128)(2,1)S(1)} %get-tuple-element.57), channel_id=1, source_target_pairs={{0,96},{16,112},{32,0},{48,16},{64,32},{80,48},{96,64},{112,80},{1... | collective-permute-start | bytes 1572872 | tf_op jit(solution)/shard_map/ppermute | solution.py:263
  100.9 23.1 %collective-permute-start.7 = (bf16[32,64,128]{2,1,0:T(8,128)(2,1)S(1)}, bf16[32,64,128]{2,1,0:T(8,128)(2,1)S(1)}, u32[]{:S(2)}, u32[]{:S(2)}) collective-permute-start(bf16[32,64,128]{2,1,0:T(8,128)(2,1)S(1)} %get-tuple-element.58), channel_id=1, source_target_pairs={{0,32},{16,48},{32,64},{48,80},{64,96},{80,112},{96,0},{112,16},{1... | collective-permute-start | bytes 1572872 | tf_op jit(solution)/shard_map/ppermute | solution.py:263
  101.9 22.2 %collective-permute-start.10 = (bf16[1024,256]{1,0:T(8,128)(2,1)S(1)}, bf16[1024,256]{1,0:T(8,128)(2,1)S(1)}, u32[]{:S(2)}, u32[]{:S(2)}) collective-permute-start(bf16[1024,256]{1,0:T(8,128)(2,1)S(1)} %copy-done.7), channel_id=1, source_target_pairs={{0,4},{1,5},{2,6},{3,7},{4,8},{5,9},{6,10},{7,11},{8,12},{9,13},{1... | collective-permute-start | bytes 1572872 | tf_op jit(solution)/shard_map/ppermute | solution.py:263
  102.8 21.2 %collective-permute-start.11 = (bf16[1024,256]{1,0:T(8,128)(2,1)S(1)}, bf16[1024,256]{1,0:T(8,128)(2,1)S(1)}, u32[]{:S(2)}, u32[]{:S(2)}) collective-permute-start(bf16[1024,256]{1,0:T(8,128)(2,1)S(1)} %copy-done.6), channel_id=1, source_target_pairs={{0,12},{1,13},{2,14},{3,15},{4,0},{5,1},{6,2},{7,3},{8,4},{9,5},{1... | collective-permute-start | bytes 1572872 | tf_op jit(solution)/shard_map/ppermute | solution.py:263
  113.0 15.3 %collective-permute-start.12 = (bf16[1024,256]{1,0:T(8,128)(2,1)S(1)}, bf16[1024,256]{1,0:T(8,128)(2,1)S(1)}, u32[]{:S(2)}, u32[]{:S(2)}) collective-permute-start(bf16[1024,256]{1,0:T(8,128)(2,1)S(1)} %copy-done.5), channel_id=1, source_target_pairs={{0,8},{1,9},{2,10},{3,11},{4,12},{5,13},{6,14},{7,15},{8,0},{9,1},... | collective-permute-start | bytes 1572872 | tf_op jit(solution)/shard_map/ppermute | solution.py:263
  128.4 23.5 %collective-permute-start.16 = (bf16[16,64,128]{2,1,0:T(8,128)(2,1)S(1)}, bf16[16,64,128]{2,1,0:T(8,128)(2,1)S(1)}, u32[]{:S(2)}, u32[]{:S(2)}) collective-permute-start(bf16[16,64,128]{2,1,0:T(8,128)(2,1)S(1)} %add_convert_fusion.4), channel_id=1, source_target_pairs={{0,128},{16,144},{32,160},{48,176},{64,192},{80,208},{96,224},{112... | collective-permute-start | bytes 786440 | tf_op jit(solution)/shard_map/ppermute | solution.py:296
  130.5 18.8 %collective-permute-start.15 = (bf16[256,256]{1,0:T(8,128)(2,1)S(1)}, bf16[256,256]{1,0:T(8,128)(2,1)S(1)}, u32[]{:S(2)}, u32[]{:S(2)}) collective-permute-start(bf16[256,256]{1,0:T(8,128)(2,1)S(1)} %get-tuple-element.60), channel_id=1, source_target_pairs={{0,2},{1,3},{2,0},{3,1},{4,6},{5,7},{6,4},{7,5},{8,10},{9,11},{10,... | collective-permute-start | bytes 393224 | tf_op jit(solution)/shard_map/ppermute | solution.py:263
  135.8 13.4 %collective-permute-start.14 = (bf16[256,256]{1,0:T(8,128)(2,1)S(1)}, bf16[256,256]{1,0:T(8,128)(2,1)S(1)}, u32[]{:S(2)}, u32[]{:S(2)}) collective-permute-start(bf16[256,256]{1,0:T(8,128)(2,1)S(1)} %get-tuple-element.61), channel_id=1, source_target_pairs={{0,3},{1,0},{2,1},{3,2},{4,7},{5,4},{6,5},{7,6},{8,11},{9,8},{10,9... | collective-permute-start | bytes 393224 | tf_op jit(solution)/shard_map/ppermute | solution.py:263
  136.7 12.5 %collective-permute-start.13 = (bf16[256,256]{1,0:T(8,128)(2,1)S(1)}, bf16[256,256]{1,0:T(8,128)(2,1)S(1)}, u32[]{:S(2)}, u32[]{:S(2)}) collective-permute-start(bf16[256,256]{1,0:T(8,128)(2,1)S(1)} %get-tuple-element.62), channel_id=1, source_target_pairs={{0,1},{1,2},{2,3},{3,0},{4,5},{5,6},{6,7},{7,4},{8,9},{9,10},{10,1... | collective-permute-start | bytes 393224 | tf_op jit(solution)/shard_map/ppermute | solution.py:263
  149.3 0.7 copy-start.2
  149.3 0.7 copy-start.3
  149.3 0.7 copy-start.4

commit v2 on v1

v2 whole, which is shorter than its diff:
```python
import functools

import jax
import jax.numpy as jnp
from jax import lax
from jax.experimental import pallas as pl
from jax.experimental.pallas import tpu as pltpu
from jax.sharding import PartitionSpec as P


D = 4096
BLK = 64
HBL = 16
MIB = 1024 * 1024


def place_of(steps):
    d = steps % 4
    return jnp.where(d == 0, 0, jnp.where(d == 3, 1, jnp.where(d == 1, 2, 3)))


def steps_of(place):
    return jnp.where(place == 0, 0, jnp.where(place == 1, 3, jnp.where(place == 2, 1, 2)))


def slot_tables(block_cols, mp_at, dp_at, slot_count):
    row_count, per_row = block_cols.shape
    flat_cols = block_cols.reshape(1, -1)
    is_mine = flat_cols // HBL == mp_at
    ranks = jnp.cumsum(is_mine.astype(jnp.int32), axis=1, dtype=jnp.int32) - 1
    targets = jnp.where(is_mine, ranks, slot_count)
    row_ids = lax.broadcasted_iota(jnp.int32, flat_cols.shape, 1) // per_row
    packed = row_ids * HBL + flat_cols - mp_at * HBL + 1
    slots = lax.broadcasted_iota(jnp.int32, (slot_count, 1), 0)
    found = jnp.sum(jnp.where(targets == slots, packed, 0), axis=1, dtype=jnp.int32)
    entry = jnp.where(found > 0, found - 1, row_count * HBL)
    place = lax.broadcasted_iota(jnp.int32, (row_count, 1), 0)
    owner = (mp_at // 4 + steps_of(place // 16)) % 4 * 4 + (mp_at % 4 + steps_of(place // 4 % 4)) % 4
    begin = (owner * 4 + place % 4) * HBL
    first = jnp.sum((entry[None, :] < begin).astype(jnp.int32), axis=1, dtype=jnp.int32)
    last = jnp.sum((entry[None, :] < begin + HBL).astype(jnp.int32), axis=1, dtype=jnp.int32)
    row = entry // HBL
    at = place_of(row // 16 - mp_at // 4) * 4 + place_of(row // 4 - mp_at % 4)
    dest = jnp.where(entry < row_count * HBL, (at * 4 + row % 4) * HBL + entry % HBL, row_count * HBL)
    slot = slots[:, 0]
    to = slot // 16
    core, across, deep = (to + dp_at) % 2, place_of(to // 2 - dp_at // 2 % 4), (to // 8 + dp_at // 8) % 2
    send = ((core * 4 + across) * 2 + deep) * 16 + slot % 16
    return dest, send, first, last


def dense_kernel(turned, dest, w_ref, d_ref, lines):
    d_ref[...] = jnp.zeros_like(d_ref)
    at_once = 16
    count = at_once // 2 if turned else at_once
    low = lax.broadcasted_iota(jnp.int32, (count, 2 * BLK), 1) < BLK
    upper = lax.broadcasted_iota(jnp.int32, (BLK, 2 * BLK), 1) >= BLK

    def place(e, block):
        c = e % HBL
        here = d_ref.at[c // 2, pl.ds(pl.multiple_of(e // HBL * BLK, BLK), BLK), :]
        here[...] = jnp.where(upper == (c % 2 == 1), block.astype(jnp.bfloat16), here[...])

    def some(k, carry):
        start = pl.multiple_of(k * at_once, at_once)
        for t in range(BLK // 2):
            two = w_ref[pl.ds(start, at_once), 2 * BLK * t : 2 * BLK * (t + 1)].astype(jnp.float32)
            swapped = pltpu.roll(two, BLK, 1)
            if turned:
                even = jnp.where(low, two[:count], swapped[count:])
                odd = jnp.where(low, swapped[:count], two[count:])
            else:
                even, odd = jnp.where(low, two, swapped), jnp.where(low, swapped, two)
            lines[pl.ds(2 * t, count, stride=BLK), :] = even
            lines[pl.ds(2 * t + 1, count, stride=BLK), :] = odd
        for u in range(count):
            block = lines[u * BLK : (u + 1) * BLK, :]
            if turned:
                both = jnp.concatenate([block, block], axis=0).T
                place(dest[start + u], both[:BLK])
                place(dest[start + u + count], both[BLK:])
            else:
                place(dest[start + u], block)
        return carry

    lax.fori_loop(0, dest.shape[0] // at_once, some, 0)


def dense_weights(dest, weights, turned):
    whole = pl.BlockSpec(memory_space=pltpu.VMEM)
    return pl.pallas_call(
        functools.partial(dense_kernel, turned),
        out_shape=jax.ShapeDtypeStruct((8, D + BLK, 2 * BLK), jnp.bfloat16),
        in_specs=[pl.BlockSpec(memory_space=pltpu.SMEM), whole],
        out_specs=whole,
        scratch_shapes=[pltpu.VMEM((16 * BLK, 2 * BLK), jnp.float32)],
        compiler_params=pltpu.CompilerParams(vmem_limit_bytes=14 * MIB),
        cost_estimate=pl.CostEstimate(flops=0, transcendentals=0, bytes_accessed=20 << 20),
        name="dense_out" if turned else "dense_in",
    )(dest, weights)


def hidden_kernel(xc_ref, din_ref, dout_ref, both_ref):
    tok = xc_ref.shape[1] // 2
    x = jnp.concatenate([xc_ref[j, :tok, :] for j in range(16)], axis=1)
    c = jnp.concatenate([xc_ref[j, tok:, :] for j in range(16)], axis=1)
    win = jnp.concatenate([din_ref[0], din_ref[1]], axis=1)
    wout = jnp.concatenate([dout_ref[0], dout_ref[1]], axis=1)
    v = jnp.dot(x, win, preferred_element_type=jnp.float32)
    g = jnp.dot(c, wout, preferred_element_type=jnp.float32)
    k0 = 0.7978845608028654
    t = jnp.tanh(k0 * (v + 0.044715 * (v * v * v)))
    both_ref[:, tok:] = (0.5 * v * (1.0 + t)).T.astype(jnp.bfloat16)
    slope = 0.5 * (1.0 + t) + 0.5 * v * (1.0 - t * t) * (k0 * (1.0 + 3 * 0.044715 * (v * v)))
    both_ref[:, :tok] = (g * slope).T.astype(jnp.bfloat16)


def hidden_stage(xc, din, dout, tok):
    cost = pl.CostEstimate(flops=4 * tok * D * 1024, transcendentals=tok * 1024, bytes_accessed=18 << 20)
    wide = pl.BlockSpec((2, D, 2 * BLK), lambda q: (q, 0, 0))
    return pl.pallas_call(
        hidden_kernel,
        grid=(4,),
        out_shape=jax.ShapeDtypeStruct((1024, 2 * tok), jnp.bfloat16),
        in_specs=[pl.BlockSpec(xc.shape, lambda q: (0, 0, 0)), wide, wide],
        out_specs=pl.BlockSpec((4 * BLK, 2 * tok), lambda q: (q, 0)),
        compiler_params=pltpu.CompilerParams(vmem_limit_bytes=26 * MIB),
        cost_estimate=cost,
        name="hidden_stage",
    )(xc, din, dout)


def grad_kernel(scale, dest, send, first, last, xc_ref, both_ref, own_ref, other_ref, g_scr):
    j = pl.program_id(0)
    tok = both_ref.shape[1] // 2
    unused = g_scr.shape[0] - 1
    most = 4

    @pl.when(j == 0)
    def _():
        g_scr[...] = jnp.zeros_like(g_scr)

    upper = lax.broadcasted_iota(jnp.int32, (tok, 2 * BLK), 1) >= BLK
    for q in range(4):
        begin, end = first[j * 4 + q], last[j * 4 + q]
        tile = xc_ref[0, :, q // 2 * 2 * BLK : (q // 2 + 1) * 2 * BLK].astype(jnp.float32)
        x, c = tile[:tok], tile[tok:]
        if q % 2:
            c = pltpu.roll(c, BLK, 1)
        else:
            x = pltpu.roll(x, BLK, 1)
        sides = jnp.concatenate([jnp.where(upper, x, 0.0), jnp.where(upper, 0.0, c)], axis=0).astype(jnp.bfloat16)
        blocks, targets = [], []
        for u in range(most):
            s = jnp.minimum(begin + u, unused - 1)
            at = pl.multiple_of(dest[s] % HBL * BLK, BLK)
            blocks.append(both_ref[pl.ds(at, BLK), :])
            targets.append(jnp.where(begin + u < end, send[s], unused))
        terms = jnp.dot(jnp.concatenate(blocks, axis=0), sides, preferred_element_type=jnp.float32)
        terms = (terms * scale).astype(jnp.bfloat16)
        for u in range(most):
            g_scr[targets[u]] = terms[u * BLK : (u + 1) * BLK]

    @pl.when(j == pl.num_programs(0) - 1)
    def _():
        half = own_ref.shape[0]
        own_ref[...] = g_scr[:half]
        other_ref[...] = g_scr[half : 2 * half]


def grad_stage(tables, xc, both, slot_count, scale):
    tok = both.shape[1] // 2
    cost = pl.CostEstimate(flops=tok * D * 1024, transcendentals=0, bytes_accessed=7 << 20)
    smem = pl.BlockSpec(memory_space=pltpu.SMEM)
    half = (slot_count // 2, BLK, 2 * BLK)
    half_spec = pl.BlockSpec(half, lambda j: (0, 0, 0), pipeline_mode=pl.Buffered(1))
    return pl.pallas_call(
        functools.partial(grad_kernel, scale),
        grid=(16,),
        out_shape=(jax.ShapeDtypeStruct(half, jnp.bfloat16),) * 2,
        in_specs=[smem] * 4
        + [pl.BlockSpec((1,) + xc.shape[1:], lambda j: (j, 0, 0)), pl.BlockSpec(both.shape, lambda j: (0, 0))],
        out_specs=(half_spec, half_spec),
        scratch_shapes=[pltpu.VMEM((slot_count + 1, BLK, 2 * BLK), jnp.bfloat16)],
        compiler_params=pltpu.CompilerParams(vmem_limit_bytes=14 * MIB),
        cost_estimate=cost,
        name="grad_stage",
    )(*tables, xc, both)


def part_kernel(din_ref, dout_ref, both_ref, *part_refs):
    j = pl.program_id(0)
    tok = both_ref.shape[1] // 2
    win = jnp.concatenate([din_ref[p] for p in range(8)], axis=1)
    wout = jnp.concatenate([dout_ref[p] for p in range(8)], axis=1)
    out = jnp.dot(wout, both_ref[:, tok:], preferred_element_type=jnp.float32).astype(jnp.bfloat16)
    back = jnp.dot(win, both_ref[:, :tok], preferred_element_type=jnp.float32).astype(jnp.bfloat16)
    both = jnp.concatenate([out, back], axis=1)
    for n, ref in enumerate(part_refs):

        @pl.when(j // 2 == n)
        def _():
            ref[...] = both


def part_stage(din, dout, both, quarter, count):
    cost = pl.CostEstimate(
        flops=count * D * 1024 * both.shape[1] // 2, transcendentals=0, bytes_accessed=count * (9 << 19)
    )
    wide = pl.BlockSpec((8, 512, 2 * BLK), lambda j: (0, 2 * quarter + j, 0))
    pieces = tuple(
        pl.BlockSpec((512, both.shape[1]), lambda j, n=n: (jnp.clip(j - 2 * n, 0, 1), 0)) for n in range(count)
    )
    return pl.pallas_call(
        part_kernel,
        grid=(2 * count,),
        out_shape=(jax.ShapeDtypeStruct((1024, both.shape[1]), jnp.bfloat16),) * count,
        in_specs=[wide, wide, pl.BlockSpec(both.shape, lambda j: (0, 0))],
        out_specs=pieces,
        compiler_params=pltpu.CompilerParams(vmem_limit_bytes=16 * MIB),
        cost_estimate=cost,
    )(din, dout, both)


def turn_kernel(own_ref, out_ref, back_ref):
    own = own_ref[...].astype(jnp.float32)
    tok = out_ref.shape[0]
    out_ref[...] = own[:, :tok].T
    back_ref[...] = own[:, tok:].T


def own_turned(own):
    rows, cols = own.shape
    return pl.pallas_call(
        turn_kernel,
        out_shape=(jax.ShapeDtypeStruct((cols // 2, rows), jnp.float32),) * 2,
        compiler_params=pltpu.CompilerParams(vmem_limit_bytes=4 * MIB),
        name="own_turned",
    )(own)


def total_kernel(out_own_ref, back_own_ref, before_ref, after_ref, opposite_ref, out_ref, back_ref):
    refs = (before_ref, after_ref, opposite_ref)
    total = sum(ref[...].astype(jnp.float32) for ref in refs)
    tok = out_ref.shape[0]
    out_ref[...] = (out_own_ref[...] + total[:, :tok].T).astype(jnp.bfloat16)
    back_ref[...] = (back_own_ref[...] + total[:, tok:].T).astype(jnp.bfloat16)


def total_turned(own, terms):
    return pl.pallas_call(
        total_kernel,
        out_shape=tuple(jax.ShapeDtypeStruct(part.shape, jnp.bfloat16) for part in own),
        compiler_params=pltpu.CompilerParams(vmem_limit_bytes=6 * MIB),
        name="total_turned",
    )(*own, *terms)


def ring(axis, stride):
    def target(i, by):
        return i - i // stride % 4 * stride + (i // stride + by) % 4 * stride

    return tuple(
        functools.partial(lax.ppermute, axis_name=axis, perm=[(i, target(i, by)) for i in range(16)])
        for by in (1, 3, 2)
    )


def spread(block, up, down, over):
    return jnp.stack([block, up(block), down(block), over(block)])


def collect(blocks, up, down, over):
    own, before, after, opposite = blocks
    return own, up(after), down(before), over(opposite)


def added(*terms):
    return sum(term.astype(jnp.float32) for term in terms).astype(jnp.bfloat16)


def on_device(tokens, cotangent, block_cols, in_weights, out_weights):
    mp_at, dp_at = lax.axis_index("mp"), lax.axis_index("dp")
    slot_count = in_weights.shape[0]
    tok = tokens.shape[0]
    scale = float(tok * lax.axis_size("dp")) ** (-0.5)
    along_x, along_z, along_y = ring("mp", 4), ring("mp", 1), ring("dp", 2)
    block = jnp.concatenate([tokens, cotangent], axis=0)
    near = spread(block, *along_z)
    tables = slot_tables(block_cols, mp_at, dp_at, slot_count)
    din = dense_weights(tables[0], in_weights, False)
    near, din = lax.optimization_barrier((near, din))
    xc = spread(near, *along_x).reshape(16, 2 * tok, -1)
    dout = dense_weights(tables[0], out_weights, True)
    both = hidden_stage(xc, din, dout, tok)
    (opposite,) = part_stage(din, dout, both, 3, 1)
    opposite, both = lax.optimization_barrier((opposite, both))
    from_opposite = along_x[2](opposite)
    mine, other = grad_stage(tables, xc, both, slot_count, scale)
    other, both = lax.optimization_barrier((other, both))
    from_core = lax.ppermute(other, "dp", [(i, i ^ 1) for i in range(16)])
    own, before, after = part_stage(din, dout, both, 0, 3)
    from_core, _ = lax.optimization_barrier((from_core, before))
    across_terms = own, along_x[0](after), along_x[1](before), from_opposite
    share = slot_count // 8
    pair = [
        added(mine[n * share : (n + 1) * share], from_core[n * share : (n + 1) * share]) for n in range(4)
    ]
    deep_terms = collect(pair, *along_y)
    rows = own.shape[0] // 4
    across = [added(*(term[n * rows : (n + 1) * rows] for term in across_terms)) for n in range(4)]
    deep_terms, _ = lax.optimization_barrier((deep_terms, across[0]))
    half = share // 2
    to_deep = added(*(term[half:] for term in deep_terms))
    from_deep = lax.ppermute(to_deep, "dp", [(i, i ^ 8) for i in range(16)])
    own_part = own_turned(across[0])
    near_terms = collect(across, *along_z)[1:]
    summed = sum(term[:half].astype(jnp.float32) for term in deep_terms) + from_deep.astype(jnp.float32)
    out_grad = summed[:, :, :BLK].reshape(-1, BLK * BLK)
    in_grad = summed[:, :, BLK:].swapaxes(1, 2).reshape(-1, BLK * BLK)
    near_terms, out_grad, in_grad = lax.optimization_barrier((near_terms, out_grad, in_grad))
    layer_out, token_grad = total_turned(own_part, near_terms)
    return (layer_out, token_grad, in_grad, out_grad)


def solution(mesh):
    placed = (P("dp", "mp"), P("dp", "mp"), P(), P("mp", None), P("mp", None))
    return jax.shard_map(
        on_device,
        mesh=mesh,
        in_specs=placed,
        out_specs=(P("dp", "mp"), P("dp", "mp"), P(("mp", "dp"), None), P(("mp", "dp"), None)),
        check_vma=False,
    )
```

time: 156 us -> 129 us (0.83)
  the two profiles are of different devices: /device:TPU:38 before, /device:TPU:8 now
where the time goes in v2:
time: 129 us
  waiting for transfers between devices  43.3 us (34%)
  Pallas kernels  41.6 us (32%)
  starting transfers between devices  33.6 us (26%)
  local copies, waits for them, and re-layouts  6.67 us (5%)
  other arithmetic  2.95 us (2%)
    pallas_call x2, Pallas kernels, dense_weights(): pl.pallas_call(functools.partial(dense_kernel, turned), out_shape=jax.Sha...  18.8 us
    ppermute x6, waiting for transfers between devices, collect(): return (own, up(after), down(before), over(opposite))  18.3 us
    ppermute x6, starting transfers between devices, spread(): return jnp.stack([block, up(block), down(block), over(block)])  15.2 us
    ppermute x6, waiting for transfers between devices, spread(): return jnp.stack([block, up(block), down(block), over(block)])  11.6 us
    ppermute x6, starting transfers between devices, collect(): return (own, up(after), down(before), over(opposite))  10.7 us
    pallas_call x2, Pallas kernels, part_stage(): pl.pallas_call(part_kernel, grid=(2 * count,), out_shape=(jax.ShapeDtypeS...  9.67 us
    ppermute x2, waiting for transfers between devices, on_device(): across_terms = (own, along_x[0](after), along_x[1](before), from_opposite)  8.01 us
    pallas_call x1, Pallas kernels, grad_stage(): pl.pallas_call(functools.partial(grad_kernel, scale), grid=(16,), out_sha...  7.65 us
  transfers between devices with their start and end apart: 17, of which 9 were waited for; matrix products, arithmetic and copies ran while one was open for 5% of the time, Pallas kernels for 20%

profile of v2, /device:TPU:8, one launch (start us, length us, event | category | flops | bytes accessed | tf_op | source)
XLA Modules:
  0.0 128.9 jit_solution(3186826477174910973)
XLA Ops:
  0.6 0.8 constant_dynamic-update-slice_fusion.1
  1.5 0.8 constant_dynamic-update-slice_fusion
  2.3 7.2 %collective-permute-start.2 = (bf16[256,256]{1,0:T(8,128)(2,1)S(1)}, bf16[256,256]{1,0:T(8,128)(2,1)S(1)}, u32[]{:S(2)}, u32[]{:S(2)}) collective-permute-start(bf16[256,256]{1,0:T(8,128)(2,1)S(1)} %constant_dynamic-update-slice_fusion), channel_id=1, source_target_pairs={{0,2},{1,3},{2,0},{3,1},{4,6},{5,7},{6,4},{7,5},{8,10},{9,11},{10,... | collective-permute-start | bytes 393224 | tf_op jit(solution)/shard_map/ppermute | solution.py:270
  9.5 2.9 %collective-permute-start = (bf16[256,256]{1,0:T(8,128)(2,1)S(1)}, bf16[256,256]{1,0:T(8,128)(2,1)S(1)}, u32[]{:S(2)}, u32[]{:S(2)}) collective-permute-start(bf16[256,256]{1,0:T(8,128)(2,1)S(1)} %constant_dynamic-update-slice_fusion), channel_id=1, source_target_pairs={{0,1},{1,2},{2,3},{3,0},{4,5},{5,6},{6,7},{7,4},{8,9},{9,10},{10,1... | collective-permute-start | bytes 393224 | tf_op jit(solution)/shard_map/ppermute | solution.py:270
  12.4 0.8 copy.12
  14.5 1.6 %copy-done = bf16[256,4096]{1,0:T(8,128)(2,1)S(1)} copy-done((bf16[256,4096]{1,0:T(8,128)(2,1)S(1)}, bf16[256,4096]{1,0:T(8,128)(2,1)}, u32[]{:S(2)}) %copy-start) | copy-done | bytes 2097176
  16.1 9.9 %dense_in.1.din_ref = bf16[8,4160,128]{2,1,0:T(8,128)(2,1)S(1)} custom-call(s32[256]{0:T(256)S(1)} %get-tuple-element.71.dest, bf16[256,4096]{1,0:T(8,128)(2,1)S(1)} %copy-done), custom_call_target="tpu_custom_call" | custom-call | bytes 20971520 | tf_op jit(solution)/shard_map/dense_in/pallas_call | solution.py:91
  26.1 3.1 %collective-permute-start.5 = (bf16[4,256,256]{2,1,0:T(8,128)(2,1)S(1)}, bf16[4,256,256]{2,1,0:T(8,128)(2,1)S(1)}, u32[]{:S(2)}, u32[]{:S(2)}) collective-permute-start(bf16[4,256,256]{2,1,0:T(8,128)(2,1)S(1)} %pad_maximum_fusion.1), channel_id=1, source_target_pairs={{0,8},{1,9},{2,10},{3,11},{4,12},{5,13},{6,14},{7,15},{8,0},{9,1},... | collective-permute-start | bytes 1572872 | tf_op jit(solution)/shard_map/ppermute | solution.py:270
  29.2 1.1 collective-permute-start.4
  30.4 0.9 collective-permute-start.3
  31.3 8.9 %dense_out.1.dout_ref = bf16[8,4160,128]{2,1,0:T(8,128)(2,1)S(1)} custom-call(s32[256]{0:T(256)S(1)} %get-tuple-element.71.dest, bf16[256,4096]{1,0:T(8,128)(2,1)S(1)} %copy-done.1), custom_call_target="tpu_custom_call" | custom-call | bytes 20971520 | tf_op jit(solution)/shard_map/dense_out/pallas_call | solution.py:91
  40.3 2.2 %collective-permute-done.5 = bf16[4,256,256]{2,1,0:T(8,128)(2,1)S(1)} collective-permute-done((bf16[4,256,256]{2,1,0:T(8,128)(2,1)S(1)}, bf16[4,256,256]{2,1,0:T(8,128)(2,1)S(1)}, u32[]{:S(2)}, u32[]{:S(2)}) %collective-permute-start.5) | collective-permute-done | bytes 524320 | tf_op jit(solution)/shard_map/ppermute | solution.py:270
  42.6 9.3 %collective-permute-done.4 = bf16[4,256,256]{2,1,0:T(8,128)(2,1)S(1)} collective-permute-done((bf16[4,256,256]{2,1,0:T(8,128)(2,1)S(1)}, bf16[4,256,256]{2,1,0:T(8,128)(2,1)S(1)}, u32[]{:S(2)}, u32[]{:S(2)}) %collective-permute-start.4) | collective-permute-done | bytes 524320 | tf_op jit(solution)/shard_map/ppermute | solution.py:270
  52.2 4.6 %hidden_stage.1.both_ref = bf16[1024,256]{1,0:T(8,128)(2,1)S(1)} custom-call(bf16[16,256,256]{2,1,0:T(8,128)(2,1)S(1)} %bitcast.21, bf16[8,4160,128]{2,1,0:T(8,128)(2,1)S(1)} %dense_in.1.din_ref, bf16[8,4160,128]{2,1,0:T(8,128)(2,1)S(1)} %dense_out.1.dout_ref), custom_call_target="tpu_custom_call" | custom-call | flops 2147483648 | bytes 18874368 | tf_op jit(solution)/shard_map/hidden_stage/pallas_call | solution.py:121
  56.7 2.4 %shard_map.84 = bf16[1024,256]{1,0:T(8,128)(2,1)S(1)} custom-call(bf16[8,4160,128]{2,1,0:T(8,128)(2,1)S(1)} %dense_in.1.din_ref, bf16[8,4160,128]{2,1,0:T(8,128)(2,1)S(1)} %dense_out.1.dout_ref, bf16[1024,256]{1,0:T(8,128)(2,1)S(1)} %hidden_stage.1.both_ref), custom_call_target="tpu_custom_call" | custom-call | flops 536870912 | bytes 4718592 | tf_op jit(solution)/shard_map/pallas_call | solution.py:214
  59.2 7.7 %grad_stage.1 = (bf16[128,64,128]{2,1,0:T(8,128)(2,1)S(1)}, bf16[128,64,128]{2,1,0:T(8,128)(2,1)S(1)}) custom-call(s32[256]{0:T(256)S(1)} %get-tuple-element.71.dest, s32[256]{0:T(256)S(1)} %get-tuple-element.72.send, s32[64]{0:T(128)S(1)} %get-tuple-element.55.first, s32[64]{0:T(128)S(1)} %get-tuple-element.54.last, bf16[16,256,256]{2,1,0:T(8,128)(2,1)S(1)} %bitcast.22, ...), custom_call_target="tpu_custom_call" | custom-call | flops 536870912 | bytes 7340032 | tf_op jit(solution)/shard_map/grad_stage/pallas_call | solution.py:177
  67.0 3.2 %collective-permute-start.8 = (bf16[1024,256]{1,0:T(8,128)(2,1)S(1)}, bf16[1024,256]{1,0:T(8,128)(2,1)S(1)}, u32[]{:S(2)}, u32[]{:S(2)}) collective-permute-start(bf16[1024,256]{1,0:T(8,128)(2,1)S(1)} %shard_map.84), channel_id=1, source_target_pairs={{0,8},{1,9},{2,10},{3,11},{4,12},{5,13},{6,14},{7,15},{8,0},{9,1},... | collective-permute-start | bytes 1572872 | tf_op jit(solution)/shard_map/ppermute | solution.py:298
  70.1 7.2 %shard_map.85 = (bf16[1024,256]{1,0:T(8,128)(2,1)S(1)}, bf16[1024,256]{1,0:T(8,128)(2,1)S(1)}, bf16[1024,256]{1,0:T(8,128)(2,1)S(1)}) custom-call(bf16[8,4160,128]{2,1,0:T(8,128)(2,1)S(1)} %dense_in.1.din_ref, bf16[8,4160,128]{2,1,0:T(8,128)(2,1)S(1)} %dense_out.1.dout_ref, bf16[1024,256]{1,0:T(8,128)(2,1)S(1)} %hidden_stage.1.both_ref), custom_call_target="tpu_custom_call" | custom-call | flops 1610612736 | bytes 14155776 | tf_op jit(solution)/shard_map/pallas_call | solution.py:214
  78.0 2.6 %collective-permute-start.7 = (bf16[1024,256]{1,0:T(8,128)(2,1)S(1)}, bf16[1024,256]{1,0:T(8,128)(2,1)S(1)}, u32[]{:S(2)}, u32[]{:S(2)}) collective-permute-start(bf16[1024,256]{1,0:T(8,128)(2,1)S(1)} %get-tuple-element.36), channel_id=1, source_target_pairs={{0,12},{1,13},{2,14},{3,15},{4,0},{5,1},{6,2},{7,3},{8,4},{9,5},{1... | collective-permute-start | bytes 1572872 | tf_op jit(solution)/shard_map/ppermute | solution.py:304
  80.7 0.9 add_convert_fusion
  81.6 2.4 %collective-permute-start.15 = (bf16[32,64,128]{2,1,0:T(8,128)(2,1)S(1)}, bf16[32,64,128]{2,1,0:T(8,128)(2,1)S(1)}, u32[]{:S(2)}, u32[]{:S(2)}) collective-permute-start(bf16[32,64,128]{2,1,0:T(8,128)(2,1)S(1)} %get-tuple-element.58), channel_id=1, source_target_pairs={{0,64},{16,80},{32,96},{48,112},{64,0},{80,16},{96,32},{112,48},{1... | collective-permute-start | bytes 1572872 | tf_op jit(solution)/shard_map/ppermute | solution.py:275
  84.0 1.3 %collective-permute-start.14 = (bf16[32,64,128]{2,1,0:T(8,128)(2,1)S(1)}, bf16[32,64,128]{2,1,0:T(8,128)(2,1)S(1)}, u32[]{:S(2)}, u32[]{:S(2)}) collective-permute-start(bf16[32,64,128]{2,1,0:T(8,128)(2,1)S(1)} %get-tuple-element.59), channel_id=1, source_target_pairs={{0,96},{16,112},{32,0},{48,16},{64,32},{80,48},{96,64},{112,80},{1... | collective-permute-start | bytes 1572872 | tf_op jit(solution)/shard_map/ppermute | solution.py:275
  86.0 8.0 %collective-permute-done.6 = bf16[1024,256]{1,0:T(8,128)(2,1)S(1)} collective-permute-done((bf16[1024,256]{1,0:T(8,128)(2,1)S(1)}, bf16[1024,256]{1,0:T(8,128)(2,1)S(1)}, u32[]{:S(2)}, u32[]{:S(2)}) %collective-permute-start.6) | collective-permute-done | bytes 524320 | tf_op jit(solution)/shard_map/ppermute | solution.py:304
  94.3 3.7 %collective-permute-done.15 = bf16[32,64,128]{2,1,0:T(8,128)(2,1)S(1)} collective-permute-done((bf16[32,64,128]{2,1,0:T(8,128)(2,1)S(1)}, bf16[32,64,128]{2,1,0:T(8,128)(2,1)S(1)}, u32[]{:S(2)}, u32[]{:S(2)}) %collective-permute-start.15) | collective-permute-done | bytes 524320 | tf_op jit(solution)/shard_map/ppermute | solution.py:275
  98.0 9.6 %collective-permute-done.14 = bf16[32,64,128]{2,1,0:T(8,128)(2,1)S(1)} collective-permute-done((bf16[32,64,128]{2,1,0:T(8,128)(2,1)S(1)}, bf16[32,64,128]{2,1,0:T(8,128)(2,1)S(1)}, u32[]{:S(2)}, u32[]{:S(2)}) %collective-permute-start.14) | collective-permute-done | bytes 524320 | tf_op jit(solution)/shard_map/ppermute | solution.py:275
  108.0 1.1 collective-permute-start.16
  109.2 2.5 %collective-permute-start.11 = (bf16[256,256]{1,0:T(8,128)(2,1)S(1)}, bf16[256,256]{1,0:T(8,128)(2,1)S(1)}, u32[]{:S(2)}, u32[]{:S(2)}) collective-permute-start(bf16[256,256]{1,0:T(8,128)(2,1)S(1)} %get-tuple-element.62), channel_id=1, source_target_pairs={{0,2},{1,3},{2,0},{3,1},{4,6},{5,7},{6,4},{7,5},{8,10},{9,11},{10,... | collective-permute-start | bytes 393224 | tf_op jit(solution)/shard_map/ppermute | solution.py:275
  111.7 3.8 %collective-permute-start.10 = (bf16[256,256]{1,0:T(8,128)(2,1)S(1)}, bf16[256,256]{1,0:T(8,128)(2,1)S(1)}, u32[]{:S(2)}, u32[]{:S(2)}) collective-permute-start(bf16[256,256]{1,0:T(8,128)(2,1)S(1)} %get-tuple-element.63), channel_id=1, source_target_pairs={{0,3},{1,0},{2,1},{3,2},{4,7},{5,4},{6,5},{7,6},{8,11},{9,8},{10,9... | collective-permute-start | bytes 393224 | tf_op jit(solution)/shard_map/ppermute | solution.py:275
  115.5 5.4 %collective-permute-done.16 = bf16[16,64,128]{2,1,0:T(8,128)(2,1)S(1)} collective-permute-done((bf16[16,64,128]{2,1,0:T(8,128)(2,1)S(1)}, bf16[16,64,128]{2,1,0:T(8,128)(2,1)S(1)}, u32[]{:S(2)}, u32[]{:S(2)}) %collective-permute-start.16) | collective-permute-done | bytes 262176 | tf_op jit(solution)/shard_map/ppermute | solution.py:315
  121.5 0.9 reshape.474
  122.4 0.9 reshape.473
  123.5 4.6 %collective-permute-done.9.before_ref = bf16[256,256]{1,0:T(8,128)(2,1)S(1)} collective-permute-done((bf16[256,256]{1,0:T(8,128)(2,1)S(1)}, bf16[256,256]{1,0:T(8,128)(2,1)S(1)}, u32[]{:S(2)}, u32[]{:S(2)}) %collective-permute-start.9) | collective-permute-done | bytes 131104 | tf_op jit(solution)/shard_map/ppermute | solution.py:275
  (40 shorter events, 5.6 us)
Async XLA Ops:
  2.3 23.7 %collective-permute-start.2 = (bf16[256,256]{1,0:T(8,128)(2,1)S(1)}, bf16[256,256]{1,0:T(8,128)(2,1)S(1)}, u32[]{:S(2)}, u32[]{:S(2)}) collective-permute-start(bf16[256,256]{1,0:T(8,128)(2,1)S(1)} %constant_dynamic-update-slice_fusion), channel_id=1, source_target_pairs={{0,2},{1,3},{2,0},{3,1},{4,6},{5,7},{6,4},{7,5},{8,10},{9,11},{10,... | collective-permute-start | bytes 393224 | tf_op jit(solution)/shard_map/ppermute | solution.py:270
  9.5 16.5 %collective-permute-start.1 = (bf16[256,256]{1,0:T(8,128)(2,1)S(1)}, bf16[256,256]{1,0:T(8,128)(2,1)S(1)}, u32[]{:S(2)}, u32[]{:S(2)}) collective-permute-start(bf16[256,256]{1,0:T(8,128)(2,1)S(1)} %constant_dynamic-update-slice_fusion), channel_id=1, source_target_pairs={{0,3},{1,0},{2,1},{3,2},{4,7},{5,4},{6,5},{7,6},{8,11},{9,8},{10,9... | collective-permute-start | bytes 393224 | tf_op jit(solution)/shard_map/ppermute | solution.py:270
  9.5 16.5 %collective-permute-start = (bf16[256,256]{1,0:T(8,128)(2,1)S(1)}, bf16[256,256]{1,0:T(8,128)(2,1)S(1)}, u32[]{:S(2)}, u32[]{:S(2)}) collective-permute-start(bf16[256,256]{1,0:T(8,128)(2,1)S(1)} %constant_dynamic-update-slice_fusion), channel_id=1, source_target_pairs={{0,1},{1,2},{2,3},{3,0},{4,5},{5,6},{6,7},{7,4},{8,9},{9,10},{10,1... | collective-permute-start | bytes 393224 | tf_op jit(solution)/shard_map/ppermute | solution.py:270
  14.5 1.6 %copy-start = (bf16[256,4096]{1,0:T(8,128)(2,1)S(1)}, bf16[256,4096]{1,0:T(8,128)(2,1)}, u32[]{:S(2)}) copy-start(bf16[256,4096]{1,0:T(8,128)(2,1)} %w_ref.2) | copy-start | bytes 6291460
  16.1 15.2 %copy-start.1 = (bf16[256,4096]{1,0:T(8,128)(2,1)S(1)}, bf16[256,4096]{1,0:T(8,128)(2,1)}, u32[]{:S(2)}) copy-start(bf16[256,4096]{1,0:T(8,128)(2,1)} %w_ref.3) | copy-start | bytes 6291460
  26.1 16.4 %collective-permute-start.5 = (bf16[4,256,256]{2,1,0:T(8,128)(2,1)S(1)}, bf16[4,256,256]{2,1,0:T(8,128)(2,1)S(1)}, u32[]{:S(2)}, u32[]{:S(2)}) collective-permute-start(bf16[4,256,256]{2,1,0:T(8,128)(2,1)S(1)} %pad_maximum_fusion.1), channel_id=1, source_target_pairs={{0,8},{1,9},{2,10},{3,11},{4,12},{5,13},{6,14},{7,15},{8,0},{9,1},... | collective-permute-start | bytes 1572872 | tf_op jit(solution)/shard_map/ppermute | solution.py:270
  29.2 22.7 %collective-permute-start.4 = (bf16[4,256,256]{2,1,0:T(8,128)(2,1)S(1)}, bf16[4,256,256]{2,1,0:T(8,128)(2,1)S(1)}, u32[]{:S(2)}, u32[]{:S(2)}) collective-permute-start(bf16[4,256,256]{2,1,0:T(8,128)(2,1)S(1)} %pad_maximum_fusion.1), channel_id=1, source_target_pairs={{0,12},{1,13},{2,14},{3,15},{4,0},{5,1},{6,2},{7,3},{8,4},{9,5},{1... | collective-permute-start | bytes 1572872 | tf_op jit(solution)/shard_map/ppermute | solution.py:270
  30.4 21.5 %collective-permute-start.3 = (bf16[4,256,256]{2,1,0:T(8,128)(2,1)S(1)}, bf16[4,256,256]{2,1,0:T(8,128)(2,1)S(1)}, u32[]{:S(2)}, u32[]{:S(2)}) collective-permute-start(bf16[4,256,256]{2,1,0:T(8,128)(2,1)S(1)} %pad_maximum_fusion.1), channel_id=1, source_target_pairs={{0,4},{1,5},{2,6},{3,7},{4,8},{5,9},{6,10},{7,11},{8,12},{9,13},{1... | collective-permute-start | bytes 1572872 | tf_op jit(solution)/shard_map/ppermute | solution.py:270
  66.9 13.8 %collective-permute-start.12 = (bf16[128,64,128]{2,1,0:T(8,128)(2,1)S(1)}, bf16[128,64,128]{2,1,0:T(8,128)(2,1)S(1)}, u32[]{:S(2)}, u32[]{:S(2)}) collective-permute-start(bf16[128,64,128]{2,1,0:T(8,128)(2,1)S(1)} %get-tuple-element.41), channel_id=1, source_target_pairs={{0,16},{16,0},{32,48},{48,32},{64,80},{80,64},{96,112},{112,96},{1... | collective-permute-start | bytes 6291464 | tf_op jit(solution)/shard_map/ppermute | solution.py:301
  67.0 18.4 %collective-permute-start.8 = (bf16[1024,256]{1,0:T(8,128)(2,1)S(1)}, bf16[1024,256]{1,0:T(8,128)(2,1)S(1)}, u32[]{:S(2)}, u32[]{:S(2)}) collective-permute-start(bf16[1024,256]{1,0:T(8,128)(2,1)S(1)} %shard_map.84), channel_id=1, source_target_pairs={{0,8},{1,9},{2,10},{3,11},{4,12},{5,13},{6,14},{7,15},{8,0},{9,1},... | collective-permute-start | bytes 1572872 | tf_op jit(solution)/shard_map/ppermute | solution.py:298
  77.4 16.7 %collective-permute-start.6 = (bf16[1024,256]{1,0:T(8,128)(2,1)S(1)}, bf16[1024,256]{1,0:T(8,128)(2,1)S(1)}, u32[]{:S(2)}, u32[]{:S(2)}) collective-permute-start(bf16[1024,256]{1,0:T(8,128)(2,1)S(1)} %get-tuple-element.35), channel_id=1, source_target_pairs={{0,4},{1,5},{2,6},{3,7},{4,8},{5,9},{6,10},{7,11},{8,12},{9,13},{1... | collective-permute-start | bytes 1572872 | tf_op jit(solution)/shard_map/ppermute | solution.py:304
  78.0 16.0 %collective-permute-start.7 = (bf16[1024,256]{1,0:T(8,128)(2,1)S(1)}, bf16[1024,256]{1,0:T(8,128)(2,1)S(1)}, u32[]{:S(2)}, u32[]{:S(2)}) collective-permute-start(bf16[1024,256]{1,0:T(8,128)(2,1)S(1)} %get-tuple-element.36), channel_id=1, source_target_pairs={{0,12},{1,13},{2,14},{3,15},{4,0},{5,1},{6,2},{7,3},{8,4},{9,5},{1... | collective-permute-start | bytes 1572872 | tf_op jit(solution)/shard_map/ppermute | solution.py:304
  81.6 16.4 %collective-permute-start.15 = (bf16[32,64,128]{2,1,0:T(8,128)(2,1)S(1)}, bf16[32,64,128]{2,1,0:T(8,128)(2,1)S(1)}, u32[]{:S(2)}, u32[]{:S(2)}) collective-permute-start(bf16[32,64,128]{2,1,0:T(8,128)(2,1)S(1)} %get-tuple-element.58), channel_id=1, source_target_pairs={{0,64},{16,80},{32,96},{48,112},{64,0},{80,16},{96,32},{112,48},{1... | collective-permute-start | bytes 1572872 | tf_op jit(solution)/shard_map/ppermute | solution.py:275
  84.0 23.7 %collective-permute-start.14 = (bf16[32,64,128]{2,1,0:T(8,128)(2,1)S(1)}, bf16[32,64,128]{2,1,0:T(8,128)(2,1)S(1)}, u32[]{:S(2)}, u32[]{:S(2)}) collective-permute-start(bf16[32,64,128]{2,1,0:T(8,128)(2,1)S(1)} %get-tuple-element.59), channel_id=1, source_target_pairs={{0,96},{16,112},{32,0},{48,16},{64,32},{80,48},{96,64},{112,80},{1... | collective-permute-start | bytes 1572872 | tf_op jit(solution)/shard_map/ppermute | solution.py:275
  85.3 22.5 %collective-permute-start.13 = (bf16[32,64,128]{2,1,0:T(8,128)(2,1)S(1)}, bf16[32,64,128]{2,1,0:T(8,128)(2,1)S(1)}, u32[]{:S(2)}, u32[]{:S(2)}) collective-permute-start(bf16[32,64,128]{2,1,0:T(8,128)(2,1)S(1)} %get-tuple-element.60), channel_id=1, source_target_pairs={{0,32},{16,48},{32,64},{48,80},{64,96},{80,112},{96,0},{112,16},{1... | collective-permute-start | bytes 1572872 | tf_op jit(solution)/shard_map/ppermute | solution.py:275
  108.0 12.9 %collective-permute-start.16 = (bf16[16,64,128]{2,1,0:T(8,128)(2,1)S(1)}, bf16[16,64,128]{2,1,0:T(8,128)(2,1)S(1)}, u32[]{:S(2)}, u32[]{:S(2)}) collective-permute-start(bf16[16,64,128]{2,1,0:T(8,128)(2,1)S(1)} %add_convert_fusion.4), channel_id=1, source_target_pairs={{0,128},{16,144},{32,160},{48,176},{64,192},{80,208},{96,224},{112... | collective-permute-start | bytes 786440 | tf_op jit(solution)/shard_map/ppermute | solution.py:315
  109.2 14.3 %collective-permute-start.11 = (bf16[256,256]{1,0:T(8,128)(2,1)S(1)}, bf16[256,256]{1,0:T(8,128)(2,1)S(1)}, u32[]{:S(2)}, u32[]{:S(2)}) collective-permute-start(bf16[256,256]{1,0:T(8,128)(2,1)S(1)} %get-tuple-element.62), channel_id=1, source_target_pairs={{0,2},{1,3},{2,0},{3,1},{4,6},{5,7},{6,4},{7,5},{8,10},{9,11},{10,... | collective-permute-start | bytes 393224 | tf_op jit(solution)/shard_map/ppermute | solution.py:275
  111.7 11.8 %collective-permute-start.10 = (bf16[256,256]{1,0:T(8,128)(2,1)S(1)}, bf16[256,256]{1,0:T(8,128)(2,1)S(1)}, u32[]{:S(2)}, u32[]{:S(2)}) collective-permute-start(bf16[256,256]{1,0:T(8,128)(2,1)S(1)} %get-tuple-element.63), channel_id=1, source_target_pairs={{0,3},{1,0},{2,1},{3,2},{4,7},{5,4},{6,5},{7,6},{8,11},{9,8},{10,9... | collective-permute-start | bytes 393224 | tf_op jit(solution)/shard_map/ppermute | solution.py:275
  115.5 12.6 %collective-permute-start.9 = (bf16[256,256]{1,0:T(8,128)(2,1)S(1)}, bf16[256,256]{1,0:T(8,128)(2,1)S(1)}, u32[]{:S(2)}, u32[]{:S(2)}) collective-permute-start(bf16[256,256]{1,0:T(8,128)(2,1)S(1)} %get-tuple-element.64), channel_id=1, source_target_pairs={{0,1},{1,2},{2,3},{3,0},{4,5},{5,6},{6,7},{7,4},{8,9},{9,10},{10,1... | collective-permute-start | bytes 393224 | tf_op jit(solution)/shard_map/ppermute | solution.py:275

commit v3 on v2

--- a/solution.py
+++ b/solution.py
@@ -45,7 +45,9 @@
     slot = slots[:, 0]
     to = slot // 16
     core, across, deep = (to + dp_at) % 2, place_of(to // 2 - dp_at // 2 % 4), (to // 8 + dp_at // 8) % 2
-    send = ((core * 4 + across) * 2 + deep) * 16 + slot % 16
+    late = slot // 8 % 2
+    owner_at = jnp.where(late == 0, across * 2 + deep, deep * 4 + across)
+    send = ((core * 2 + late) * 8 + owner_at) * 8 + slot % 8
     return dest, send, first, last
 
 
@@ -266,8 +268,8 @@
     )
 
 
-def spread(block, up, down, over):
-    return jnp.stack([block, up(block), down(block), over(block)])
+def sent(block, ways):
+    return [way(block) for way in ways]
 
 
 def collect(blocks, up, down, over):
@@ -286,12 +288,15 @@
     scale = float(tok * lax.axis_size("dp")) ** (-0.5)
     along_x, along_z, along_y = ring("mp", 4), ring("mp", 1), ring("dp", 2)
     block = jnp.concatenate([tokens, cotangent], axis=0)
-    near = spread(block, *along_z)
+    near = jnp.stack(sent(block, along_z))
+    wide_own = sent(block, along_x)
     tables = slot_tables(block_cols, mp_at, dp_at, slot_count)
-    din = dense_weights(tables[0], in_weights, False)
-    near, din = lax.optimization_barrier((near, din))
-    xc = spread(near, *along_x).reshape(16, 2 * tok, -1)
-    dout = dense_weights(tables[0], out_weights, True)
+    wide = sent(near, along_x)
+    pieces = [(own[None], others) for own, others in zip([block] + wide_own, [near] + wide)]
+    xc = jnp.concatenate([piece for both in pieces for piece in both])
+    dest, _ = lax.optimization_barrier((tables[0], near))
+    din = dense_weights(dest, in_weights, False)
+    dout = dense_weights(dest, out_weights, True)
     both = hidden_stage(xc, din, dout, tok)
     (opposite,) = part_stage(din, dout, both, 3, 1)
     opposite, both = lax.optimization_barrier((opposite, both))
@@ -302,20 +307,32 @@
     own, before, after = part_stage(din, dout, both, 0, 3)
     from_core, _ = lax.optimization_barrier((from_core, before))
     across_terms = own, along_x[0](after), along_x[1](before), from_opposite
-    share = slot_count // 8
-    pair = [
-        added(mine[n * share : (n + 1) * share], from_core[n * share : (n + 1) * share]) for n in range(4)
-    ]
-    deep_terms = collect(pair, *along_y)
+    share = slot_count // 32
+    deep_way = functools.partial(lax.ppermute, axis_name="dp", perm=[(i, i ^ 8) for i in range(16)])
+
+    def pair(at, count):
+        return added(mine[at * share : (at + count) * share], from_core[at * share : (at + count) * share])
+
+    late_own, late_other = pair(8, 4), pair(12, 4)
+    late_deep = deep_way(late_other)
+    deep_terms = collect([pair(2 * n, 2) for n in range(4)], *along_y)
     rows = own.shape[0] // 4
     across = [added(*(term[n * rows : (n + 1) * rows] for term in across_terms)) for n in range(4)]
-    deep_terms, _ = lax.optimization_barrier((deep_terms, across[0]))
-    half = share // 2
-    to_deep = added(*(term[half:] for term in deep_terms))
-    from_deep = lax.ppermute(to_deep, "dp", [(i, i ^ 8) for i in range(16)])
+    deep_terms, late_deep, _ = lax.optimization_barrier((deep_terms, late_deep, across[0]))
+    to_deep = added(*(term[share:] for term in deep_terms))
+    from_deep = deep_way(to_deep)
+    late_terms = collect(
+        [
+            added(late_own[n * share : (n + 1) * share], late_deep[n * share : (n + 1) * share])
+            for n in range(4)
+        ],
+        *along_y,
+    )
     own_part = own_turned(across[0])
     near_terms = collect(across, *along_z)[1:]
-    summed = sum(term[:half].astype(jnp.float32) for term in deep_terms) + from_deep.astype(jnp.float32)
+    early = sum(term[:share].astype(jnp.float32) for term in deep_terms) + from_deep.astype(jnp.float32)
+    late = sum(term.astype(jnp.float32) for term in late_terms)
+    summed = jnp.concatenate([early, late])
     out_grad = summed[:, :, :BLK].reshape(-1, BLK * BLK)
     in_grad = summed[:, :, BLK:].swapaxes(1, 2).reshape(-1, BLK * BLK)
     near_terms, out_grad, in_grad = lax.optimization_barrier((near_terms, out_grad, in_grad))

time: 129 us -> 126 us (0.977); the launches traced: 129 us -> 124 us
  waiting for transfers between devices: 43.3 us -> 29.9 us
  starting transfers between devices: 33.6 us -> 42.5 us
    ppermute x6 -> x9, waiting for transfers between devices: 18.3 us -> 4.76 us  [collect(): return (own, up(after), down(before), over(opposite))]
    ppermute x6 -> x9, starting transfers between devices: 10.7 us -> 17.4 us  [collect(): return (own, up(after), down(before), over(opposite))]
    ppermute x7 -> x11, starting transfers between devices: 16.4 us -> 20.8 us  [the longest x9 20.3 us: sent(): return [way(block) for way in ways]]
    ppermute x7 -> x11, waiting for transfers between devices: 17 us -> 13.6 us  [the longest x1 7.78 us: on_device(): from_deep = deep_way(to_deep)]
    ppermute x1, starting transfers between devices: 3.15 us -> 0.87 us  [on_device(): from_opposite = along_x[2](opposite)]
    ppermute x2, waiting for transfers between devices: 8.01 us -> 10.2 us  [on_device(): across_terms = (own, along_x[0](after), along_x[1](before), from_opposite)]
    ppermute x1, waiting for transfers between devices: 0.01 us -> 1.42 us  [on_device(): from_opposite = along_x[2](opposite)]
    unnamed x6 -> x15, local copies, waits for them, and re-layouts: 3.23 us -> 3.36 us
  transfers between devices with their start and end apart: 17 -> 24, of which waited for: 9 -> 7; matrix products, arithmetic and copies ran while one was open for 5% -> 5% of each run, Pallas kernels for 20% -> 21%
where the time goes in v3:
time: 126 us; the launch traced here: 124 us
  starting transfers between devices  42.5 us (34%)
  Pallas kernels  41.6 us (33%)
  waiting for transfers between devices  29.9 us (24%)
  local copies, waits for them, and re-layouts  6.62 us (5%)
  other arithmetic  2.66 us (2%)
    ppermute x9, starting transfers between devices, sent(): return [way(block) for way in ways]  20.3 us
    pallas_call x2, Pallas kernels, dense_weights(): pl.pallas_call(functools.partial(dense_kernel, turned), out_shape=jax.Sha...  18.8 us
    ppermute x9, starting transfers between devices, collect(): return (own, up(after), down(before), over(opposite))  17.4 us
    ppermute x2, waiting for transfers between devices, on_device(): across_terms = (own, along_x[0](after), along_x[1](before), from_opposite)  10.2 us
    pallas_call x2, Pallas kernels, part_stage(): pl.pallas_call(part_kernel, grid=(2 * count,), out_shape=(jax.ShapeDtypeS...  9.67 us
    ppermute x1, waiting for transfers between devices, on_device(): from_deep = deep_way(to_deep)  7.78 us
    pallas_call x1, Pallas kernels, grad_stage(): pl.pallas_call(functools.partial(grad_kernel, scale), grid=(16,), out_sha...  7.65 us
    ppermute x9, waiting for transfers between devices, sent(): return [way(block) for way in ways]  5.77 us
  transfers between devices with their start and end apart: 24, of which 7 were waited for; matrix products, arithmetic and copies ran while one was open for 5% of the time, Pallas kernels for 21%

profile of v3, /device:TPU:8, one launch (start us, length us, event | category | flops | bytes accessed | tf_op | source)
XLA Modules:
  0.0 124.3 jit_solution(11174324780434713568)
XLA Ops:
  0.6 0.8 constant_dynamic-update-slice_fusion.1
  1.5 0.8 constant_dynamic-update-slice_fusion
  2.3 3.0 %collective-permute-start.7 = (bf16[256,256]{1,0:T(8,128)(2,1)S(1)}, bf16[256,256]{1,0:T(8,128)(2,1)S(1)}, u32[]{:S(2)}, u32[]{:S(2)}) collective-permute-start(bf16[256,256]{1,0:T(8,128)(2,1)S(1)} %constant_dynamic-update-slice_fusion), channel_id=1, source_target_pairs={{0,8},{1,9},{2,10},{3,11},{4,12},{5,13},{6,14},{7,15},{8,0},{9,1},... | collective-permute-start | bytes 393224 | tf_op jit(solution)/shard_map/ppermute | solution.py:272
  5.3 1.1 collective-permute-start.5
  6.5 7.2 %collective-permute-start.2 = (bf16[256,256]{1,0:T(8,128)(2,1)S(1)}, bf16[256,256]{1,0:T(8,128)(2,1)S(1)}, u32[]{:S(2)}, u32[]{:S(2)}) collective-permute-start(bf16[256,256]{1,0:T(8,128)(2,1)S(1)} %constant_dynamic-update-slice_fusion), channel_id=1, source_target_pairs={{0,2},{1,3},{2,0},{3,1},{4,6},{5,7},{6,4},{7,5},{8,10},{9,11},{10,... | collective-permute-start | bytes 393224 | tf_op jit(solution)/shard_map/ppermute | solution.py:272
  13.7 2.9 %collective-permute-start = (bf16[256,256]{1,0:T(8,128)(2,1)S(1)}, bf16[256,256]{1,0:T(8,128)(2,1)S(1)}, u32[]{:S(2)}, u32[]{:S(2)}) collective-permute-start(bf16[256,256]{1,0:T(8,128)(2,1)S(1)} %constant_dynamic-update-slice_fusion), channel_id=1, source_target_pairs={{0,1},{1,2},{2,3},{3,0},{4,5},{5,6},{6,7},{7,4},{8,9},{9,10},{10,1... | collective-permute-start | bytes 393224 | tf_op jit(solution)/shard_map/ppermute | solution.py:272
  19.1 0.9 collective-permute-start.3
  20.0 5.6 %collective-permute-done.1 = bf16[256,256]{1,0:T(8,128)(2,1)S(1)} collective-permute-done((bf16[256,256]{1,0:T(8,128)(2,1)S(1)}, bf16[256,256]{1,0:T(8,128)(2,1)S(1)}, u32[]{:S(2)}, u32[]{:S(2)}) %collective-permute-start.1) | collective-permute-done | bytes 131104 | tf_op jit(solution)/shard_map/ppermute | solution.py:272
  25.6 1.6 %collective-permute-start.8 = (bf16[3,256,256]{2,1,0:T(8,128)(2,1)S(1)}, bf16[3,256,256]{2,1,0:T(8,128)(2,1)S(1)}, u32[]{:S(2)}, u32[]{:S(2)}) collective-permute-start(bf16[3,256,256]{2,1,0:T(8,128)(2,1)S(1)} %pad_maximum_fusion.1), channel_id=1, source_target_pairs={{0,8},{1,9},{2,10},{3,11},{4,12},{5,13},{6,14},{7,15},{8,0},{9,1},... | collective-permute-start | bytes 1179656 | tf_op jit(solution)/shard_map/ppermute | solution.py:272
  27.3 3.5 %collective-permute-start.6 = (bf16[3,256,256]{2,1,0:T(8,128)(2,1)S(1)}, bf16[3,256,256]{2,1,0:T(8,128)(2,1)S(1)}, u32[]{:S(2)}, u32[]{:S(2)}) collective-permute-start(bf16[3,256,256]{2,1,0:T(8,128)(2,1)S(1)} %pad_maximum_fusion.1), channel_id=1, source_target_pairs={{0,12},{1,13},{2,14},{3,15},{4,0},{5,1},{6,2},{7,3},{8,4},{9,5},{1... | collective-permute-start | bytes 1179656 | tf_op jit(solution)/shard_map/ppermute | solution.py:272
  30.8 1.6 %copy-done = bf16[256,4096]{1,0:T(8,128)(2,1)S(1)} copy-done((bf16[256,4096]{1,0:T(8,128)(2,1)S(1)}, bf16[256,4096]{1,0:T(8,128)(2,1)}, u32[]{:S(2)}) %copy-start) | copy-done | bytes 2097176
  32.4 8.9 %dense_out.1.dout_ref = bf16[8,4160,128]{2,1,0:T(8,128)(2,1)S(1)} custom-call(s32[256]{0:T(256)S(1)} %get-tuple-element.29.dest, bf16[256,4096]{1,0:T(8,128)(2,1)S(1)} %copy-done), custom_call_target="tpu_custom_call" | custom-call | bytes 20971520 | tf_op jit(solution)/shard_map/dense_out/pallas_call | solution.py:93
  41.3 9.9 %dense_in.1.din_ref = bf16[8,4160,128]{2,1,0:T(8,128)(2,1)S(1)} custom-call(s32[256]{0:T(256)S(1)} %get-tuple-element.29.dest, bf16[256,4096]{1,0:T(8,128)(2,1)S(1)} %copy-done.1), custom_call_target="tpu_custom_call" | custom-call | bytes 20971520 | tf_op jit(solution)/shard_map/dense_in/pallas_call | solution.py:93
  51.4 4.6 %hidden_stage.1.both_ref = bf16[1024,256]{1,0:T(8,128)(2,1)S(1)} custom-call(bf16[16,256,256]{2,1,0:T(8,128)(2,1)S(1)} %constant_dynamic-update-slice_fusion.2.xc_ref, bf16[8,4160,128]{2,1,0:T(8,128)(2,1)S(1)} %dense_in.1.din_ref, bf16[8,4160,128]{2,1,0:T(8,128)(2,1)S(1)} %dense_out.1.dout_ref), custom_call_target="tpu_custom_call" | custom-call | flops 2147483648 | bytes 18874368 | tf_op jit(solution)/shard_map/hidden_stage/pallas_call | solution.py:123
  56.0 2.4 %shard_map.84 = bf16[1024,256]{1,0:T(8,128)(2,1)S(1)} custom-call(bf16[8,4160,128]{2,1,0:T(8,128)(2,1)S(1)} %dense_in.1.din_ref, bf16[8,4160,128]{2,1,0:T(8,128)(2,1)S(1)} %dense_out.1.dout_ref, bf16[1024,256]{1,0:T(8,128)(2,1)S(1)} %hidden_stage.1.both_ref), custom_call_target="tpu_custom_call" | custom-call | flops 536870912 | bytes 4718592 | tf_op jit(solution)/shard_map/pallas_call | solution.py:216
  58.5 7.7 %grad_stage.1 = (bf16[128,64,128]{2,1,0:T(8,128)(2,1)S(1)}, bf16[128,64,128]{2,1,0:T(8,128)(2,1)S(1)}) custom-call(s32[256]{0:T(256)S(1)} %get-tuple-element.29.dest, s32[256]{0:T(256)S(1)} %fusion.18.send, s32[64]{0:T(128)S(1)} %get-tuple-element.55.first, s32[64]{0:T(128)S(1)} %get-tuple-element.54.last, ...), custom_call_target="tpu_custom_call" | custom-call | flops 536870912 | bytes 7340032 | tf_op jit(solution)/shard_map/grad_stage/pallas_call | solution.py:179
  66.2 0.9 collective-permute-start.11
  67.1 7.2 %shard_map.85 = (bf16[1024,256]{1,0:T(8,128)(2,1)S(1)}, bf16[1024,256]{1,0:T(8,128)(2,1)S(1)}, bf16[1024,256]{1,0:T(8,128)(2,1)S(1)}) custom-call(bf16[8,4160,128]{2,1,0:T(8,128)(2,1)S(1)} %dense_in.1.din_ref, bf16[8,4160,128]{2,1,0:T(8,128)(2,1)S(1)} %dense_out.1.dout_ref, bf16[1024,256]{1,0:T(8,128)(2,1)S(1)} %hidden_stage.1.both_ref), custom_call_target="tpu_custom_call" | custom-call | flops 1610612736 | bytes 14155776 | tf_op jit(solution)/shard_map/pallas_call | solution.py:216
  74.3 1.0 collective-permute-start.9
  75.3 2.3 %collective-permute-start.10 = (bf16[1024,256]{1,0:T(8,128)(2,1)S(1)}, bf16[1024,256]{1,0:T(8,128)(2,1)S(1)}, u32[]{:S(2)}, u32[]{:S(2)}) collective-permute-start(bf16[1024,256]{1,0:T(8,128)(2,1)S(1)} %get-tuple-element.35), channel_id=1, source_target_pairs={{0,12},{1,13},{2,14},{3,15},{4,0},{5,1},{6,2},{7,3},{8,4},{9,5},{1... | collective-permute-start | bytes 1572872 | tf_op jit(solution)/shard_map/ppermute | solution.py:309
  78.8 2.4 %collective-permute-start.18 = (bf16[16,64,128]{2,1,0:T(8,128)(2,1)S(1)}, bf16[16,64,128]{2,1,0:T(8,128)(2,1)S(1)}, u32[]{:S(2)}, u32[]{:S(2)}) collective-permute-start(bf16[16,64,128]{2,1,0:T(8,128)(2,1)S(1)} %get-tuple-element.60), channel_id=1, source_target_pairs={{0,64},{16,80},{32,96},{48,112},{64,0},{80,16},{96,32},{112,48},{1... | collective-permute-start | bytes 786440 | tf_op jit(solution)/shard_map/ppermute | solution.py:277
  81.2 1.4 %collective-permute-done.11 = bf16[1024,256]{1,0:T(8,128)(2,1)S(1)} collective-permute-done((bf16[1024,256]{1,0:T(8,128)(2,1)S(1)}, bf16[1024,256]{1,0:T(8,128)(2,1)S(1)}, u32[]{:S(2)}, u32[]{:S(2)}) %collective-permute-start.11) | collective-permute-done | bytes 524320 | tf_op jit(solution)/shard_map/ppermute | solution.py:303
  83.1 10.2 %collective-permute-done.9 = bf16[1024,256]{1,0:T(8,128)(2,1)S(1)} collective-permute-done((bf16[1024,256]{1,0:T(8,128)(2,1)S(1)}, bf16[1024,256]{1,0:T(8,128)(2,1)S(1)}, u32[]{:S(2)}, u32[]{:S(2)}) %collective-permute-start.9) | collective-permute-done | bytes 524320 | tf_op jit(solution)/shard_map/ppermute | solution.py:309
  93.3 1.6 %collective-permute-start.16 = (bf16[16,64,128]{2,1,0:T(8,128)(2,1)S(1)}, bf16[16,64,128]{2,1,0:T(8,128)(2,1)S(1)}, u32[]{:S(2)}, u32[]{:S(2)}) collective-permute-start(bf16[16,64,128]{2,1,0:T(8,128)(2,1)S(1)} %get-tuple-element.62), channel_id=1, source_target_pairs={{0,32},{16,48},{32,64},{48,80},{64,96},{80,112},{96,0},{112,16},{1... | collective-permute-start | bytes 786440 | tf_op jit(solution)/shard_map/ppermute | solution.py:277
  95.1 9.2 %collective-permute-start.14 = (bf16[256,256]{1,0:T(8,128)(2,1)S(1)}, bf16[256,256]{1,0:T(8,128)(2,1)S(1)}, u32[]{:S(2)}, u32[]{:S(2)}) collective-permute-start(bf16[256,256]{1,0:T(8,128)(2,1)S(1)} %get-tuple-element.64), channel_id=1, source_target_pairs={{0,2},{1,3},{2,0},{3,1},{4,6},{5,7},{6,4},{7,5},{8,10},{9,11},{10,... | collective-permute-start | bytes 393224 | tf_op jit(solution)/shard_map/ppermute | solution.py:277
  104.9 1.4 %collective-permute-start.21 = (bf16[8,64,128]{2,1,0:T(8,128)(2,1)S(1)}, bf16[8,64,128]{2,1,0:T(8,128)(2,1)S(1)}, u32[]{:S(2)}, u32[]{:S(2)}) collective-permute-start(bf16[8,64,128]{2,1,0:T(8,128)(2,1)S(1)} %get-tuple-element.68), channel_id=1, source_target_pairs={{0,32},{16,48},{32,64},{48,80},{64,96},{80,112},{96,0},{112,16},{1... | collective-permute-start | bytes 393224 | tf_op jit(solution)/shard_map/ppermute | solution.py:277
  106.3 1.2 collective-permute-start.23
  107.5 7.8 %collective-permute-done.20 = bf16[8,64,128]{2,1,0:T(8,128)(2,1)S(1)} collective-permute-done((bf16[8,64,128]{2,1,0:T(8,128)(2,1)S(1)}, bf16[8,64,128]{2,1,0:T(8,128)(2,1)S(1)}, u32[]{:S(2)}, u32[]{:S(2)}) %collective-permute-start.20) | collective-permute-done | bytes 131104 | tf_op jit(solution)/shard_map/ppermute | solution.py:323
  116.5 3.7 %collective-permute-done.22 = bf16[8,64,128]{2,1,0:T(8,128)(2,1)S(1)} collective-permute-done((bf16[8,64,128]{2,1,0:T(8,128)(2,1)S(1)}, bf16[8,64,128]{2,1,0:T(8,128)(2,1)S(1)}, u32[]{:S(2)}, u32[]{:S(2)}) %collective-permute-start.22) | collective-permute-done | bytes 131104 | tf_op jit(solution)/shard_map/ppermute | solution.py:277
  120.8 0.9 reshape.470
  121.6 0.9 reshape.469
  122.5 1.0 collective-permute-done.12.before_ref
  (67 shorter events, 7.6 us)
Async XLA Ops:
  2.3 49.0 %collective-permute-start.7 = (bf16[256,256]{1,0:T(8,128)(2,1)S(1)}, bf16[256,256]{1,0:T(8,128)(2,1)S(1)}, u32[]{:S(2)}, u32[]{:S(2)}) collective-permute-start(bf16[256,256]{1,0:T(8,128)(2,1)S(1)} %constant_dynamic-update-slice_fusion), channel_id=1, source_target_pairs={{0,8},{1,9},{2,10},{3,11},{4,12},{5,13},{6,14},{7,15},{8,0},{9,1},... | collective-permute-start | bytes 393224 | tf_op jit(solution)/shard_map/ppermute | solution.py:272
  5.3 45.9 %collective-permute-start.5 = (bf16[256,256]{1,0:T(8,128)(2,1)S(1)}, bf16[256,256]{1,0:T(8,128)(2,1)S(1)}, u32[]{:S(2)}, u32[]{:S(2)}) collective-permute-start(bf16[256,256]{1,0:T(8,128)(2,1)S(1)} %constant_dynamic-update-slice_fusion), channel_id=1, source_target_pairs={{0,12},{1,13},{2,14},{3,15},{4,0},{5,1},{6,2},{7,3},{8,4},{9,5},{1... | collective-permute-start | bytes 393224 | tf_op jit(solution)/shard_map/ppermute | solution.py:272
  6.5 12.6 %collective-permute-start.2 = (bf16[256,256]{1,0:T(8,128)(2,1)S(1)}, bf16[256,256]{1,0:T(8,128)(2,1)S(1)}, u32[]{:S(2)}, u32[]{:S(2)}) collective-permute-start(bf16[256,256]{1,0:T(8,128)(2,1)S(1)} %constant_dynamic-update-slice_fusion), channel_id=1, source_target_pairs={{0,2},{1,3},{2,0},{3,1},{4,6},{5,7},{6,4},{7,5},{8,10},{9,11},{10,... | collective-permute-start | bytes 393224 | tf_op jit(solution)/shard_map/ppermute | solution.py:272
  13.7 11.9 %collective-permute-start.1 = (bf16[256,256]{1,0:T(8,128)(2,1)S(1)}, bf16[256,256]{1,0:T(8,128)(2,1)S(1)}, u32[]{:S(2)}, u32[]{:S(2)}) collective-permute-start(bf16[256,256]{1,0:T(8,128)(2,1)S(1)} %constant_dynamic-update-slice_fusion), channel_id=1, source_target_pairs={{0,3},{1,0},{2,1},{3,2},{4,7},{5,4},{6,5},{7,6},{8,11},{9,8},{10,9... | collective-permute-start | bytes 393224 | tf_op jit(solution)/shard_map/ppermute | solution.py:272
  13.7 11.9 %collective-permute-start = (bf16[256,256]{1,0:T(8,128)(2,1)S(1)}, bf16[256,256]{1,0:T(8,128)(2,1)S(1)}, u32[]{:S(2)}, u32[]{:S(2)}) collective-permute-start(bf16[256,256]{1,0:T(8,128)(2,1)S(1)} %constant_dynamic-update-slice_fusion), channel_id=1, source_target_pairs={{0,1},{1,2},{2,3},{3,0},{4,5},{5,6},{6,7},{7,4},{8,9},{9,10},{10,1... | collective-permute-start | bytes 393224 | tf_op jit(solution)/shard_map/ppermute | solution.py:272
  19.1 8.2 %collective-permute-start.3 = (bf16[256,256]{1,0:T(8,128)(2,1)S(1)}, bf16[256,256]{1,0:T(8,128)(2,1)S(1)}, u32[]{:S(2)}, u32[]{:S(2)}) collective-permute-start(bf16[256,256]{1,0:T(8,128)(2,1)S(1)} %constant_dynamic-update-slice_fusion), channel_id=1, source_target_pairs={{0,4},{1,5},{2,6},{3,7},{4,8},{5,9},{6,10},{7,11},{8,12},{9,13},{1... | collective-permute-start | bytes 393224 | tf_op jit(solution)/shard_map/ppermute | solution.py:272
  25.6 25.7 %collective-permute-start.8 = (bf16[3,256,256]{2,1,0:T(8,128)(2,1)S(1)}, bf16[3,256,256]{2,1,0:T(8,128)(2,1)S(1)}, u32[]{:S(2)}, u32[]{:S(2)}) collective-permute-start(bf16[3,256,256]{2,1,0:T(8,128)(2,1)S(1)} %pad_maximum_fusion.1), channel_id=1, source_target_pairs={{0,8},{1,9},{2,10},{3,11},{4,12},{5,13},{6,14},{7,15},{8,0},{9,1},... | collective-permute-start | bytes 1179656 | tf_op jit(solution)/shard_map/ppermute | solution.py:272
  27.3 24.0 %collective-permute-start.4 = (bf16[3,256,256]{2,1,0:T(8,128)(2,1)S(1)}, bf16[3,256,256]{2,1,0:T(8,128)(2,1)S(1)}, u32[]{:S(2)}, u32[]{:S(2)}) collective-permute-start(bf16[3,256,256]{2,1,0:T(8,128)(2,1)S(1)} %pad_maximum_fusion.1), channel_id=1, source_target_pairs={{0,4},{1,5},{2,6},{3,7},{4,8},{5,9},{6,10},{7,11},{8,12},{9,13},{1... | collective-permute-start | bytes 1179656 | tf_op jit(solution)/shard_map/ppermute | solution.py:272
  27.3 24.0 %collective-permute-start.6 = (bf16[3,256,256]{2,1,0:T(8,128)(2,1)S(1)}, bf16[3,256,256]{2,1,0:T(8,128)(2,1)S(1)}, u32[]{:S(2)}, u32[]{:S(2)}) collective-permute-start(bf16[3,256,256]{2,1,0:T(8,128)(2,1)S(1)} %pad_maximum_fusion.1), channel_id=1, source_target_pairs={{0,12},{1,13},{2,14},{3,15},{4,0},{5,1},{6,2},{7,3},{8,4},{9,5},{1... | collective-permute-start | bytes 1179656 | tf_op jit(solution)/shard_map/ppermute | solution.py:272
  30.8 1.6 %copy-start = (bf16[256,4096]{1,0:T(8,128)(2,1)S(1)}, bf16[256,4096]{1,0:T(8,128)(2,1)}, u32[]{:S(2)}) copy-start(bf16[256,4096]{1,0:T(8,128)(2,1)} %w_ref.3) | copy-start | bytes 6291460
  32.4 8.9 %copy-start.1 = (bf16[256,4096]{1,0:T(8,128)(2,1)S(1)}, bf16[256,4096]{1,0:T(8,128)(2,1)}, u32[]{:S(2)}) copy-start(bf16[256,4096]{1,0:T(8,128)(2,1)} %w_ref.2) | copy-start | bytes 6291460
  66.1 11.5 %collective-permute-start.15 = (bf16[128,64,128]{2,1,0:T(8,128)(2,1)S(1)}, bf16[128,64,128]{2,1,0:T(8,128)(2,1)S(1)}, u32[]{:S(2)}, u32[]{:S(2)}) collective-permute-start(bf16[128,64,128]{2,1,0:T(8,128)(2,1)S(1)} %get-tuple-element.40), channel_id=1, source_target_pairs={{0,16},{16,0},{32,48},{48,32},{64,80},{80,64},{96,112},{112,96},{1... | collective-permute-start | bytes 6291464 | tf_op jit(solution)/shard_map/ppermute | solution.py:306
  66.2 16.4 %collective-permute-start.11 = (bf16[1024,256]{1,0:T(8,128)(2,1)S(1)}, bf16[1024,256]{1,0:T(8,128)(2,1)S(1)}, u32[]{:S(2)}, u32[]{:S(2)}) collective-permute-start(bf16[1024,256]{1,0:T(8,128)(2,1)S(1)} %shard_map.84), channel_id=1, source_target_pairs={{0,8},{1,9},{2,10},{3,11},{4,12},{5,13},{6,14},{7,15},{8,0},{9,1},... | collective-permute-start | bytes 1572872 | tf_op jit(solution)/shard_map/ppermute | solution.py:303
  74.3 18.9 %collective-permute-start.9 = (bf16[1024,256]{1,0:T(8,128)(2,1)S(1)}, bf16[1024,256]{1,0:T(8,128)(2,1)S(1)}, u32[]{:S(2)}, u32[]{:S(2)}) collective-permute-start(bf16[1024,256]{1,0:T(8,128)(2,1)S(1)} %get-tuple-element.34), channel_id=1, source_target_pairs={{0,4},{1,5},{2,6},{3,7},{4,8},{5,9},{6,10},{7,11},{8,12},{9,13},{1... | collective-permute-start | bytes 1572872 | tf_op jit(solution)/shard_map/ppermute | solution.py:309
  75.3 19.6 %collective-permute-start.10 = (bf16[1024,256]{1,0:T(8,128)(2,1)S(1)}, bf16[1024,256]{1,0:T(8,128)(2,1)S(1)}, u32[]{:S(2)}, u32[]{:S(2)}) collective-permute-start(bf16[1024,256]{1,0:T(8,128)(2,1)S(1)} %get-tuple-element.35), channel_id=1, source_target_pairs={{0,12},{1,13},{2,14},{3,15},{4,0},{5,1},{6,2},{7,3},{8,4},{9,5},{1... | collective-permute-start | bytes 1572872 | tf_op jit(solution)/shard_map/ppermute | solution.py:309
  78.0 26.6 %collective-permute-start.19 = (bf16[32,64,128]{2,1,0:T(8,128)(2,1)S(1)}, bf16[32,64,128]{2,1,0:T(8,128)(2,1)S(1)}, u32[]{:S(2)}, u32[]{:S(2)}) collective-permute-start(bf16[32,64,128]{2,1,0:T(8,128)(2,1)S(1)} %get-tuple-element.58), channel_id=1, source_target_pairs={{0,128},{16,144},{32,160},{48,176},{64,192},{80,208},{96,224},{112... | collective-permute-start | bytes 1572872 | tf_op jit(solution)/shard_map/ppermute | solution.py:317
  78.8 25.6 %collective-permute-start.18 = (bf16[16,64,128]{2,1,0:T(8,128)(2,1)S(1)}, bf16[16,64,128]{2,1,0:T(8,128)(2,1)S(1)}, u32[]{:S(2)}, u32[]{:S(2)}) collective-permute-start(bf16[16,64,128]{2,1,0:T(8,128)(2,1)S(1)} %get-tuple-element.60), channel_id=1, source_target_pairs={{0,64},{16,80},{32,96},{48,112},{64,0},{80,16},{96,32},{112,48},{1... | collective-permute-start | bytes 786440 | tf_op jit(solution)/shard_map/ppermute | solution.py:277
  82.7 21.9 %collective-permute-start.17 = (bf16[16,64,128]{2,1,0:T(8,128)(2,1)S(1)}, bf16[16,64,128]{2,1,0:T(8,128)(2,1)S(1)}, u32[]{:S(2)}, u32[]{:S(2)}) collective-permute-start(bf16[16,64,128]{2,1,0:T(8,128)(2,1)S(1)} %get-tuple-element.61), channel_id=1, source_target_pairs={{0,96},{16,112},{32,0},{48,16},{64,32},{80,48},{96,64},{112,80},{1... | collective-permute-start | bytes 786440 | tf_op jit(solution)/shard_map/ppermute | solution.py:277
  93.3 11.3 %collective-permute-start.16 = (bf16[16,64,128]{2,1,0:T(8,128)(2,1)S(1)}, bf16[16,64,128]{2,1,0:T(8,128)(2,1)S(1)}, u32[]{:S(2)}, u32[]{:S(2)}) collective-permute-start(bf16[16,64,128]{2,1,0:T(8,128)(2,1)S(1)} %get-tuple-element.62), channel_id=1, source_target_pairs={{0,32},{16,48},{32,64},{48,80},{64,96},{80,112},{96,0},{112,16},{1... | collective-permute-start | bytes 786440 | tf_op jit(solution)/shard_map/ppermute | solution.py:277
  95.1 27.4 %collective-permute-start.14 = (bf16[256,256]{1,0:T(8,128)(2,1)S(1)}, bf16[256,256]{1,0:T(8,128)(2,1)S(1)}, u32[]{:S(2)}, u32[]{:S(2)}) collective-permute-start(bf16[256,256]{1,0:T(8,128)(2,1)S(1)} %get-tuple-element.64), channel_id=1, source_target_pairs={{0,2},{1,3},{2,0},{3,1},{4,6},{5,7},{6,4},{7,5},{8,10},{9,11},{10,... | collective-permute-start | bytes 393224 | tf_op jit(solution)/shard_map/ppermute | solution.py:277
  104.5 18.1 %collective-permute-start.13 = (bf16[256,256]{1,0:T(8,128)(2,1)S(1)}, bf16[256,256]{1,0:T(8,128)(2,1)S(1)}, u32[]{:S(2)}, u32[]{:S(2)}) collective-permute-start(bf16[256,256]{1,0:T(8,128)(2,1)S(1)} %get-tuple-element.65), channel_id=1, source_target_pairs={{0,3},{1,0},{2,1},{3,2},{4,7},{5,4},{6,5},{7,6},{8,11},{9,8},{10,9... | collective-permute-start | bytes 393224 | tf_op jit(solution)/shard_map/ppermute | solution.py:277
  104.7 10.6 %collective-permute-start.20 = (bf16[8,64,128]{2,1,0:T(8,128)(2,1)S(1)}, bf16[8,64,128]{2,1,0:T(8,128)(2,1)S(1)}, u32[]{:S(2)}, u32[]{:S(2)}) collective-permute-start(bf16[8,64,128]{2,1,0:T(8,128)(2,1)S(1)} %add_convert_fusion.10), channel_id=1, source_target_pairs={{0,128},{16,144},{32,160},{48,176},{64,192},{80,208},{96,224},{112... | collective-permute-start | bytes 393224 | tf_op jit(solution)/shard_map/ppermute | solution.py:323
  104.9 10.9 %collective-permute-start.21 = (bf16[8,64,128]{2,1,0:T(8,128)(2,1)S(1)}, bf16[8,64,128]{2,1,0:T(8,128)(2,1)S(1)}, u32[]{:S(2)}, u32[]{:S(2)}) collective-permute-start(bf16[8,64,128]{2,1,0:T(8,128)(2,1)S(1)} %get-tuple-element.68), channel_id=1, source_target_pairs={{0,32},{16,48},{32,64},{48,80},{64,96},{80,112},{96,0},{112,16},{1... | collective-permute-start | bytes 393224 | tf_op jit(solution)/shard_map/ppermute | solution.py:277
  106.3 10.3 %collective-permute-start.23 = (bf16[8,64,128]{2,1,0:T(8,128)(2,1)S(1)}, bf16[8,64,128]{2,1,0:T(8,128)(2,1)S(1)}, u32[]{:S(2)}, u32[]{:S(2)}) collective-permute-start(bf16[8,64,128]{2,1,0:T(8,128)(2,1)S(1)} %get-tuple-element.69), channel_id=1, source_target_pairs={{0,64},{16,80},{32,96},{48,112},{64,0},{80,16},{96,32},{112,48},{1... | collective-permute-start | bytes 393224 | tf_op jit(solution)/shard_map/ppermute | solution.py:277
  115.3 5.0 %collective-permute-start.22 = (bf16[8,64,128]{2,1,0:T(8,128)(2,1)S(1)}, bf16[8,64,128]{2,1,0:T(8,128)(2,1)S(1)}, u32[]{:S(2)}, u32[]{:S(2)}) collective-permute-start(bf16[8,64,128]{2,1,0:T(8,128)(2,1)S(1)} %get-tuple-element.70), channel_id=1, source_target_pairs={{0,96},{16,112},{32,0},{48,16},{64,32},{80,48},{96,64},{112,80},{1... | collective-permute-start | bytes 393224 | tf_op jit(solution)/shard_map/ppermute | solution.py:277
  115.8 7.7 %collective-permute-start.12 = (bf16[256,256]{1,0:T(8,128)(2,1)S(1)}, bf16[256,256]{1,0:T(8,128)(2,1)S(1)}, u32[]{:S(2)}, u32[]{:S(2)}) collective-permute-start(bf16[256,256]{1,0:T(8,128)(2,1)S(1)} %get-tuple-element.66), channel_id=1, source_target_pairs={{0,1},{1,2},{2,3},{3,0},{4,5},{5,6},{6,7},{7,4},{8,9},{9,10},{10,1... | collective-permute-start | bytes 393224 | tf_op jit(solution)/shard_map/ppermute | solution.py:277

commit v4 on v3

--- a/solution.py
+++ b/solution.py
@@ -2,6 +2,7 @@
 
 import jax
 import jax.numpy as jnp
+import numpy as np
 from jax import lax
 from jax.experimental import pallas as pl
 from jax.experimental.pallas import tpu as pltpu
@@ -51,81 +52,98 @@
     return dest, send, first, last
 
 
-def dense_kernel(turned, dest, w_ref, d_ref, lines):
+def dense_kernel(turned, dest, w_ref, order_ref, d_ref):
     d_ref[...] = jnp.zeros_like(d_ref)
     at_once = 16
-    count = at_once // 2 if turned else at_once
+    count = 8
     low = lax.broadcasted_iota(jnp.int32, (count, 2 * BLK), 1) < BLK
     upper = lax.broadcasted_iota(jnp.int32, (BLK, 2 * BLK), 1) >= BLK
 
     def place(e, block):
-        c = e % HBL
-        here = d_ref.at[c // 2, pl.ds(pl.multiple_of(e // HBL * BLK, BLK), BLK), :]
-        here[...] = jnp.where(upper == (c % 2 == 1), block.astype(jnp.bfloat16), here[...])
+        here = d_ref.at[(e & (HBL - 1)) >> 1, pl.ds(pl.multiple_of((e >> 4) * BLK, BLK), BLK), :]
+        here[...] = jnp.where(upper == ((e & 1) == 1), block.astype(jnp.bfloat16), here[...])
+
+    def lines(even, odd):
+        rows = jnp.concatenate(even + odd, axis=0).astype(jnp.bfloat16)
+        return jnp.dot(order_ref[...], rows, preferred_element_type=jnp.float32)
 
     def some(k, carry):
         start = pl.multiple_of(k * at_once, at_once)
-        for t in range(BLK // 2):
-            two = w_ref[pl.ds(start, at_once), 2 * BLK * t : 2 * BLK * (t + 1)].astype(jnp.float32)
-            swapped = pltpu.roll(two, BLK, 1)
-            if turned:
-                even = jnp.where(low, two[:count], swapped[count:])
-                odd = jnp.where(low, swapped[:count], two[count:])
-            else:
-                even, odd = jnp.where(low, two, swapped), jnp.where(low, swapped, two)
-            lines[pl.ds(2 * t, count, stride=BLK), :] = even
-            lines[pl.ds(2 * t + 1, count, stride=BLK), :] = odd
-        for u in range(count):
-            block = lines[u * BLK : (u + 1) * BLK, :]
-            if turned:
+        two = [
+            w_ref[pl.ds(start, at_once), 2 * BLK * t : 2 * BLK * (t + 1)].astype(jnp.float32)
+            for t in range(BLK // 2)
+        ]
+        swapped = [pltpu.roll(x, BLK, 1) for x in two]
+        if turned:
+            even = [jnp.where(low, x[:count], y[count:]) for x, y in zip(two, swapped)]
+            odd = [jnp.where(low, y[:count], x[count:]) for x, y in zip(two, swapped)]
+            blocks = lines(even, odd)
+            for u in range(count):
+                block = blocks[u * BLK : (u + 1) * BLK]
                 both = jnp.concatenate([block, block], axis=0).T
                 place(dest[start + u], both[:BLK])
                 place(dest[start + u + count], both[BLK:])
-            else:
-                place(dest[start + u], block)
+        else:
+            for half in range(2):
+                part = slice(half * count, (half + 1) * count)
+                even = [jnp.where(low, x[part], y[part]) for x, y in zip(two, swapped)]
+                odd = [jnp.where(low, y[part], x[part]) for x, y in zip(two, swapped)]
+                blocks = lines(even, odd)
+                for u in range(count):
+                    place(dest[start + half * count + u], blocks[u * BLK : (u + 1) * BLK])
         return carry
 
     lax.fori_loop(0, dest.shape[0] // at_once, some, 0)
 
 
-def dense_weights(dest, weights, turned):
+def line_order():
+    to, at = np.indices((8 * BLK, 8 * BLK))
+    row = at // 8 % (BLK // 2) * 2 + at // (4 * BLK)
+    return jnp.asarray((to == at % 8 * BLK + row).astype(jnp.bfloat16))
+
+
+def dense_weights(dest, weights, order, turned):
     whole = pl.BlockSpec(memory_space=pltpu.VMEM)
     return pl.pallas_call(
         functools.partial(dense_kernel, turned),
         out_shape=jax.ShapeDtypeStruct((8, D + BLK, 2 * BLK), jnp.bfloat16),
-        in_specs=[pl.BlockSpec(memory_space=pltpu.SMEM), whole],
+        in_specs=[pl.BlockSpec(memory_space=pltpu.SMEM), whole, whole],
         out_specs=whole,
-        scratch_shapes=[pltpu.VMEM((16 * BLK, 2 * BLK), jnp.float32)],
-        compiler_params=pltpu.CompilerParams(vmem_limit_bytes=14 * MIB),
+        compiler_params=pltpu.CompilerParams(vmem_limit_bytes=15 * MIB),
         cost_estimate=pl.CostEstimate(flops=0, transcendentals=0, bytes_accessed=20 << 20),
         name="dense_out" if turned else "dense_in",
-    )(dest, weights)
+    )(dest, weights, order)
 
 
 def hidden_kernel(xc_ref, din_ref, dout_ref, both_ref):
     tok = xc_ref.shape[1] // 2
     x = jnp.concatenate([xc_ref[j, :tok, :] for j in range(16)], axis=1)
     c = jnp.concatenate([xc_ref[j, tok:, :] for j in range(16)], axis=1)
-    win = jnp.concatenate([din_ref[0], din_ref[1]], axis=1)
-    wout = jnp.concatenate([dout_ref[0], dout_ref[1]], axis=1)
-    v = jnp.dot(x, win, preferred_element_type=jnp.float32)
-    g = jnp.dot(c, wout, preferred_element_type=jnp.float32)
-    k0 = 0.7978845608028654
-    t = jnp.tanh(k0 * (v + 0.044715 * (v * v * v)))
-    both_ref[:, tok:] = (0.5 * v * (1.0 + t)).T.astype(jnp.bfloat16)
-    slope = 0.5 * (1.0 + t) + 0.5 * v * (1.0 - t * t) * (k0 * (1.0 + 3 * 0.044715 * (v * v)))
-    both_ref[:, :tok] = (g * slope).T.astype(jnp.bfloat16)
+
+    def some(q, carry):
+        win = jnp.concatenate([din_ref[2 * q + p, :D] for p in range(2)], axis=1)
+        wout = jnp.concatenate([dout_ref[2 * q + p, :D] for p in range(2)], axis=1)
+        v = jnp.dot(x, win, preferred_element_type=jnp.float32)
+        g = jnp.dot(c, wout, preferred_element_type=jnp.float32)
+        k0 = 0.7978845608028654
+        t = jnp.tanh(k0 * (v + 0.044715 * (v * v * v)))
+        rows = pl.ds(pl.multiple_of(q * 4 * BLK, 4 * BLK), 4 * BLK)
+        both_ref[rows, tok:] = (0.5 * v * (1.0 + t)).T.astype(jnp.bfloat16)
+        slope = 0.5 * (1.0 + t) + 0.5 * v * (1.0 - t * t) * (k0 * (1.0 + 3 * 0.044715 * (v * v)))
+        both_ref[rows, :tok] = (g * slope).T.astype(jnp.bfloat16)
+        return carry
+
+    lax.fori_loop(0, 4, some, 0)
 
 
 def hidden_stage(xc, din, dout, tok):
     cost = pl.CostEstimate(flops=4 * tok * D * 1024, transcendentals=tok * 1024, bytes_accessed=18 << 20)
-    wide = pl.BlockSpec((2, D, 2 * BLK), lambda q: (q, 0, 0))
+    whole = pl.BlockSpec(memory_space=pltpu.VMEM)
     return pl.pallas_call(
         hidden_kernel,
-        grid=(4,),
         out_shape=jax.ShapeDtypeStruct((1024, 2 * tok), jnp.bfloat16),
-        in_specs=[pl.BlockSpec(xc.shape, lambda q: (0, 0, 0)), wide, wide],
-        out_specs=pl.BlockSpec((4 * BLK, 2 * tok), lambda q: (q, 0)),
+        in_specs=[whole] * 3,
+        out_specs=whole,
         compiler_params=pltpu.CompilerParams(vmem_limit_bytes=26 * MIB),
         cost_estimate=cost,
         name="hidden_stage",
@@ -155,7 +173,7 @@
         blocks, targets = [], []
         for u in range(most):
             s = jnp.minimum(begin + u, unused - 1)
-            at = pl.multiple_of(dest[s] % HBL * BLK, BLK)
+            at = pl.multiple_of((dest[s] & (HBL - 1)) * BLK, BLK)
             blocks.append(both_ref[pl.ds(at, BLK), :])
             targets.append(jnp.where(begin + u < end, send[s], unused))
         terms = jnp.dot(jnp.concatenate(blocks, axis=0), sides, preferred_element_type=jnp.float32)
@@ -190,36 +208,35 @@
     )(*tables, xc, both)
 
 
-def part_kernel(din_ref, dout_ref, both_ref, *part_refs):
-    j = pl.program_id(0)
+def part_kernel(quarter, din_ref, dout_ref, both_ref, *part_refs):
     tok = both_ref.shape[1] // 2
-    win = jnp.concatenate([din_ref[p] for p in range(8)], axis=1)
-    wout = jnp.concatenate([dout_ref[p] for p in range(8)], axis=1)
-    out = jnp.dot(wout, both_ref[:, tok:], preferred_element_type=jnp.float32).astype(jnp.bfloat16)
-    back = jnp.dot(win, both_ref[:, :tok], preferred_element_type=jnp.float32).astype(jnp.bfloat16)
-    both = jnp.concatenate([out, back], axis=1)
+    size = 512
     for n, ref in enumerate(part_refs):
 
-        @pl.when(j // 2 == n)
-        def _():
-            ref[...] = both
+        def some(j, carry):
+            rows = pl.ds(pl.multiple_of((quarter + n) * 1024 + j * size, size), size)
+            win = jnp.concatenate([din_ref[p, rows, :] for p in range(8)], axis=1)
+            wout = jnp.concatenate([dout_ref[p, rows, :] for p in range(8)], axis=1)
+            out = jnp.dot(wout, both_ref[:, tok:], preferred_element_type=jnp.float32)
+            back = jnp.dot(win, both_ref[:, :tok], preferred_element_type=jnp.float32)
+            to = pl.ds(pl.multiple_of(j * size, size), size)
+            ref[to, :] = jnp.concatenate([out, back], axis=1).astype(jnp.bfloat16)
+            return carry
+
+        lax.fori_loop(0, 1024 // size, some, 0)
 
 
 def part_stage(din, dout, both, quarter, count):
     cost = pl.CostEstimate(
         flops=count * D * 1024 * both.shape[1] // 2, transcendentals=0, bytes_accessed=count * (9 << 19)
     )
-    wide = pl.BlockSpec((8, 512, 2 * BLK), lambda j: (0, 2 * quarter + j, 0))
-    pieces = tuple(
-        pl.BlockSpec((512, both.shape[1]), lambda j, n=n: (jnp.clip(j - 2 * n, 0, 1), 0)) for n in range(count)
-    )
-    return pl.pallas_call(
-        part_kernel,
-        grid=(2 * count,),
+    whole = pl.BlockSpec(memory_space=pltpu.VMEM)
+    return pl.pallas_call(
+        functools.partial(part_kernel, quarter),
         out_shape=(jax.ShapeDtypeStruct((1024, both.shape[1]), jnp.bfloat16),) * count,
-        in_specs=[wide, wide, pl.BlockSpec(both.shape, lambda j: (0, 0))],
-        out_specs=pieces,
-        compiler_params=pltpu.CompilerParams(vmem_limit_bytes=16 * MIB),
+        in_specs=[whole] * 3,
+        out_specs=(whole,) * count,
+        compiler_params=pltpu.CompilerParams(vmem_limit_bytes=24 * MIB),
         cost_estimate=cost,
     )(din, dout, both)
 
@@ -294,9 +311,10 @@
     wide = sent(near, along_x)
     pieces = [(own[None], others) for own, others in zip([block] + wide_own, [near] + wide)]
     xc = jnp.concatenate([piece for both in pieces for piece in both])
+    order = line_order()
     dest, _ = lax.optimization_barrier((tables[0], near))
-    din = dense_weights(dest, in_weights, False)
-    dout = dense_weights(dest, out_weights, True)
+    din = dense_weights(dest, in_weights, order, False)
+    dout = dense_weights(dest, out_weights, order, True)
     both = hidden_stage(xc, din, dout, tok)
     (opposite,) = part_stage(din, dout, both, 3, 1)
     opposite, both = lax.optimization_barrier((opposite, both))

time: 126 us -> 125 us (level)
  Pallas kernels: 41.6 us -> 37.8 us
  waiting for transfers between devices: 29.9 us -> 32.9 us
    pallas_call x3, Pallas kernels: 14.2 us -> 9.2 us  [the longest x2 5.65 us: part_stage(): pl.pallas_call(functools.partial(part_kernel, quarter), out_shape=(jax.Sh...]
    ppermute x1, waiting for transfers between devices: 1.42 us -> 4.4 us  [on_device(): from_opposite = along_x[2](opposite)]
    pallas_call x2, Pallas kernels: 18.8 us -> 20.1 us  [dense_weights(): pl.pallas_call(functools.partial(dense_kernel, turned), out_shape=jax.Sha...]
    unnamed x15 -> x17, local copies, waits for them, and re-layouts: 3.36 us -> 3.43 us
  transfers between devices with their start and end apart: 24 -> 24, of which waited for: 7 -> 7; matrix products, arithmetic and copies ran while one was open for 5% -> 5% of each run, Pallas kernels for 21% -> 20%
where the time goes in v4:
time: 125 us; the launch traced here: 124 us
  starting transfers between devices  42.5 us (34%)
  Pallas kernels  37.8 us (30%)
  waiting for transfers between devices  32.9 us (26%)
  local copies, waits for them, and re-layouts  6.68 us (5%)
  other arithmetic  2.7 us (2%)
    ppermute x9, starting transfers between devices, sent(): return [way(block) for way in ways]  20.3 us
    pallas_call x2, Pallas kernels, dense_weights(): pl.pallas_call(functools.partial(dense_kernel, turned), out_shape=jax.Sha...  20.1 us
    ppermute x9, starting transfers between devices, collect(): return (own, up(after), down(before), over(opposite))  17.4 us
    ppermute x2, waiting for transfers between devices, on_device(): across_terms = (own, along_x[0](after), along_x[1](before), from_opposite)  10.2 us
    ppermute x1, waiting for transfers between devices, on_device(): from_deep = deep_way(to_deep)  7.78 us
    pallas_call x1, Pallas kernels, grad_stage(): pl.pallas_call(functools.partial(grad_kernel, scale), grid=(16,), out_sha...  7.63 us
    ppermute x9, waiting for transfers between devices, sent(): return [way(block) for way in ways]  5.77 us
    pallas_call x2, Pallas kernels, part_stage(): pl.pallas_call(functools.partial(part_kernel, quarter), out_shape=(jax.Sh...  5.65 us
  transfers between devices with their start and end apart: 24, of which 7 were waited for; matrix products, arithmetic and copies ran while one was open for 5% of the time, Pallas kernels for 20%

profile of v4, /device:TPU:8, one launch (start us, length us, event | category | flops | bytes accessed | tf_op | source)
XLA Modules:
  0.0 123.6 jit_solution(3488044540403653307)
XLA Ops:
  0.6 0.9 constant_dynamic-update-slice_fusion.1
  1.5 0.8 constant_dynamic-update-slice_fusion
  2.4 3.0 %collective-permute-start.7 = (bf16[256,256]{1,0:T(8,128)(2,1)S(1)}, bf16[256,256]{1,0:T(8,128)(2,1)S(1)}, u32[]{:S(2)}, u32[]{:S(2)}) collective-permute-start(bf16[256,256]{1,0:T(8,128)(2,1)S(1)} %constant_dynamic-update-slice_fusion), channel_id=1, source_target_pairs={{0,8},{1,9},{2,10},{3,11},{4,12},{5,13},{6,14},{7,15},{8,0},{9,1},... | collective-permute-start | bytes 393224 | tf_op jit(solution)/shard_map/ppermute | solution.py:289
  5.4 1.1 collective-permute-start.5
  6.6 7.2 %collective-permute-start.2 = (bf16[256,256]{1,0:T(8,128)(2,1)S(1)}, bf16[256,256]{1,0:T(8,128)(2,1)S(1)}, u32[]{:S(2)}, u32[]{:S(2)}) collective-permute-start(bf16[256,256]{1,0:T(8,128)(2,1)S(1)} %constant_dynamic-update-slice_fusion), channel_id=1, source_target_pairs={{0,2},{1,3},{2,0},{3,1},{4,6},{5,7},{6,4},{7,5},{8,10},{9,11},{10,... | collective-permute-start | bytes 393224 | tf_op jit(solution)/shard_map/ppermute | solution.py:289
  13.7 2.9 %collective-permute-start = (bf16[256,256]{1,0:T(8,128)(2,1)S(1)}, bf16[256,256]{1,0:T(8,128)(2,1)S(1)}, u32[]{:S(2)}, u32[]{:S(2)}) collective-permute-start(bf16[256,256]{1,0:T(8,128)(2,1)S(1)} %constant_dynamic-update-slice_fusion), channel_id=1, source_target_pairs={{0,1},{1,2},{2,3},{3,0},{4,5},{5,6},{6,7},{7,4},{8,9},{9,10},{10,1... | collective-permute-start | bytes 393224 | tf_op jit(solution)/shard_map/ppermute | solution.py:289
  19.2 0.9 collective-permute-start.3
  20.0 5.6 %collective-permute-done.1 = bf16[256,256]{1,0:T(8,128)(2,1)S(1)} collective-permute-done((bf16[256,256]{1,0:T(8,128)(2,1)S(1)}, bf16[256,256]{1,0:T(8,128)(2,1)S(1)}, u32[]{:S(2)}, u32[]{:S(2)}) %collective-permute-start.1) | collective-permute-done | bytes 131104 | tf_op jit(solution)/shard_map/ppermute | solution.py:289
  25.7 1.6 %collective-permute-start.8 = (bf16[3,256,256]{2,1,0:T(8,128)(2,1)S(1)}, bf16[3,256,256]{2,1,0:T(8,128)(2,1)S(1)}, u32[]{:S(2)}, u32[]{:S(2)}) collective-permute-start(bf16[3,256,256]{2,1,0:T(8,128)(2,1)S(1)} %pad_maximum_fusion.1), channel_id=1, source_target_pairs={{0,8},{1,9},{2,10},{3,11},{4,12},{5,13},{6,14},{7,15},{8,0},{9,1},... | collective-permute-start | bytes 1179656 | tf_op jit(solution)/shard_map/ppermute | solution.py:289
  27.4 3.5 %collective-permute-start.6 = (bf16[3,256,256]{2,1,0:T(8,128)(2,1)S(1)}, bf16[3,256,256]{2,1,0:T(8,128)(2,1)S(1)}, u32[]{:S(2)}, u32[]{:S(2)}) collective-permute-start(bf16[3,256,256]{2,1,0:T(8,128)(2,1)S(1)} %pad_maximum_fusion.1), channel_id=1, source_target_pairs={{0,12},{1,13},{2,14},{3,15},{4,0},{5,1},{6,2},{7,3},{8,4},{9,5},{1... | collective-permute-start | bytes 1179656 | tf_op jit(solution)/shard_map/ppermute | solution.py:289
  30.9 1.6 %copy-done.1 = bf16[256,4096]{1,0:T(8,128)(2,1)S(1)} copy-done((bf16[256,4096]{1,0:T(8,128)(2,1)S(1)}, bf16[256,4096]{1,0:T(8,128)(2,1)}, u32[]{:S(2)}) %copy-start.1) | copy-done | bytes 2097176
  32.5 9.4 %dense_out.1.dout_ref = bf16[8,4160,128]{2,1,0:T(8,128)(2,1)S(1)} custom-call(s32[256]{0:T(256)S(1)} %get-tuple-element.29.dest, bf16[256,4096]{1,0:T(8,128)(2,1)S(1)} %copy-done.1, bf16[512,512]{1,0:T(8,128)(2,1)S(1)} %copy-done), custom_call_target="tpu_custom_call" | custom-call | bytes 20971520 | tf_op jit(solution)/shard_map/dense_out/pallas_call | solution.py:107
  41.9 10.7 %dense_in.1.din_ref = bf16[8,4160,128]{2,1,0:T(8,128)(2,1)S(1)} custom-call(s32[256]{0:T(256)S(1)} %get-tuple-element.29.dest, bf16[256,4096]{1,0:T(8,128)(2,1)S(1)} %copy-done.2, bf16[512,512]{1,0:T(8,128)(2,1)S(1)} %copy-done), custom_call_target="tpu_custom_call" | custom-call | bytes 20971520 | tf_op jit(solution)/shard_map/dense_in/pallas_call | solution.py:107
  52.8 3.6 %hidden_stage.1.both_ref = bf16[1024,256]{1,0:T(8,128)(2,1)S(1)} custom-call(bf16[16,256,256]{2,1,0:T(8,128)(2,1)S(1)} %constant_dynamic-update-slice_fusion.2.xc_ref, bf16[8,4160,128]{2,1,0:T(8,128)(2,1)S(1)} %dense_in.1.din_ref, bf16[8,4160,128]{2,1,0:T(8,128)(2,1)S(1)} %dense_out.1.dout_ref), custom_call_target="tpu_custom_call" | custom-call | flops 2147483648 | bytes 18874368 | tf_op jit(solution)/shard_map/hidden_stage/pallas_call | solution.py:142
  56.3 1.4 %shard_map.93 = bf16[1024,256]{1,0:T(8,128)(2,1)S(1)} custom-call(bf16[8,4160,128]{2,1,0:T(8,128)(2,1)S(1)} %dense_in.1.din_ref, bf16[8,4160,128]{2,1,0:T(8,128)(2,1)S(1)} %dense_out.1.dout_ref, bf16[1024,256]{1,0:T(8,128)(2,1)S(1)} %hidden_stage.1.both_ref), custom_call_target="tpu_custom_call" | custom-call | flops 536870912 | bytes 4718592 | tf_op jit(solution)/shard_map/pallas_call | solution.py:234
  57.8 7.6 %grad_stage.1 = (bf16[128,64,128]{2,1,0:T(8,128)(2,1)S(1)}, bf16[128,64,128]{2,1,0:T(8,128)(2,1)S(1)}) custom-call(s32[256]{0:T(256)S(1)} %get-tuple-element.29.dest, s32[256]{0:T(256)S(1)} %fusion.18.send, s32[64]{0:T(128)S(1)} %get-tuple-element.55.first, s32[64]{0:T(128)S(1)} %get-tuple-element.54.last, ...), custom_call_target="tpu_custom_call" | custom-call | flops 536870912 | bytes 7340032 | tf_op jit(solution)/shard_map/grad_stage/pallas_call | solution.py:197
  65.5 0.8 collective-permute-start.11
  66.3 4.2 %shard_map.94 = (bf16[1024,256]{1,0:T(8,128)(2,1)S(1)}, bf16[1024,256]{1,0:T(8,128)(2,1)S(1)}, bf16[1024,256]{1,0:T(8,128)(2,1)S(1)}) custom-call(bf16[8,4160,128]{2,1,0:T(8,128)(2,1)S(1)} %dense_in.1.din_ref, bf16[8,4160,128]{2,1,0:T(8,128)(2,1)S(1)} %dense_out.1.dout_ref, bf16[1024,256]{1,0:T(8,128)(2,1)S(1)} %hidden_stage.1.both_ref), custom_call_target="tpu_custom_call" | custom-call | flops 1610612736 | bytes 14155776 | tf_op jit(solution)/shard_map/pallas_call | solution.py:234
  70.6 0.9 collective-permute-start.9
  71.5 2.4 %collective-permute-start.10 = (bf16[1024,256]{1,0:T(8,128)(2,1)S(1)}, bf16[1024,256]{1,0:T(8,128)(2,1)S(1)}, u32[]{:S(2)}, u32[]{:S(2)}) collective-permute-start(bf16[1024,256]{1,0:T(8,128)(2,1)S(1)} %get-tuple-element.35), channel_id=1, source_target_pairs={{0,12},{1,13},{2,14},{3,15},{4,0},{5,1},{6,2},{7,3},{8,4},{9,5},{1... | collective-permute-start | bytes 1572872 | tf_op jit(solution)/shard_map/ppermute | solution.py:327
  75.1 2.4 %collective-permute-start.18 = (bf16[16,64,128]{2,1,0:T(8,128)(2,1)S(1)}, bf16[16,64,128]{2,1,0:T(8,128)(2,1)S(1)}, u32[]{:S(2)}, u32[]{:S(2)}) collective-permute-start(bf16[16,64,128]{2,1,0:T(8,128)(2,1)S(1)} %get-tuple-element.60), channel_id=1, source_target_pairs={{0,64},{16,80},{32,96},{48,112},{64,0},{80,16},{96,32},{112,48},{1... | collective-permute-start | bytes 786440 | tf_op jit(solution)/shard_map/ppermute | solution.py:294
  77.5 4.4 %collective-permute-done.11 = bf16[1024,256]{1,0:T(8,128)(2,1)S(1)} collective-permute-done((bf16[1024,256]{1,0:T(8,128)(2,1)S(1)}, bf16[1024,256]{1,0:T(8,128)(2,1)S(1)}, u32[]{:S(2)}, u32[]{:S(2)}) %collective-permute-start.11) | collective-permute-done | bytes 524320 | tf_op jit(solution)/shard_map/ppermute | solution.py:321
  82.4 10.2 %collective-permute-done.9 = bf16[1024,256]{1,0:T(8,128)(2,1)S(1)} collective-permute-done((bf16[1024,256]{1,0:T(8,128)(2,1)S(1)}, bf16[1024,256]{1,0:T(8,128)(2,1)S(1)}, u32[]{:S(2)}, u32[]{:S(2)}) %collective-permute-start.9) | collective-permute-done | bytes 524320 | tf_op jit(solution)/shard_map/ppermute | solution.py:327
  92.6 1.5 %collective-permute-start.16 = (bf16[16,64,128]{2,1,0:T(8,128)(2,1)S(1)}, bf16[16,64,128]{2,1,0:T(8,128)(2,1)S(1)}, u32[]{:S(2)}, u32[]{:S(2)}) collective-permute-start(bf16[16,64,128]{2,1,0:T(8,128)(2,1)S(1)} %get-tuple-element.62), channel_id=1, source_target_pairs={{0,32},{16,48},{32,64},{48,80},{64,96},{80,112},{96,0},{112,16},{1... | collective-permute-start | bytes 786440 | tf_op jit(solution)/shard_map/ppermute | solution.py:294
  94.4 9.2 %collective-permute-start.14 = (bf16[256,256]{1,0:T(8,128)(2,1)S(1)}, bf16[256,256]{1,0:T(8,128)(2,1)S(1)}, u32[]{:S(2)}, u32[]{:S(2)}) collective-permute-start(bf16[256,256]{1,0:T(8,128)(2,1)S(1)} %get-tuple-element.64), channel_id=1, source_target_pairs={{0,2},{1,3},{2,0},{3,1},{4,6},{5,7},{6,4},{7,5},{8,10},{9,11},{10,... | collective-permute-start | bytes 393224 | tf_op jit(solution)/shard_map/ppermute | solution.py:294
  104.2 1.4 %collective-permute-start.21 = (bf16[8,64,128]{2,1,0:T(8,128)(2,1)S(1)}, bf16[8,64,128]{2,1,0:T(8,128)(2,1)S(1)}, u32[]{:S(2)}, u32[]{:S(2)}) collective-permute-start(bf16[8,64,128]{2,1,0:T(8,128)(2,1)S(1)} %get-tuple-element.68), channel_id=1, source_target_pairs={{0,32},{16,48},{32,64},{48,80},{64,96},{80,112},{96,0},{112,16},{1... | collective-permute-start | bytes 393224 | tf_op jit(solution)/shard_map/ppermute | solution.py:294
  105.5 1.2 collective-permute-start.23
  106.7 7.8 %collective-permute-done.20 = bf16[8,64,128]{2,1,0:T(8,128)(2,1)S(1)} collective-permute-done((bf16[8,64,128]{2,1,0:T(8,128)(2,1)S(1)}, bf16[8,64,128]{2,1,0:T(8,128)(2,1)S(1)}, u32[]{:S(2)}, u32[]{:S(2)}) %collective-permute-start.20) | collective-permute-done | bytes 131104 | tf_op jit(solution)/shard_map/ppermute | solution.py:341
  115.8 3.7 %collective-permute-done.22 = bf16[8,64,128]{2,1,0:T(8,128)(2,1)S(1)} collective-permute-done((bf16[8,64,128]{2,1,0:T(8,128)(2,1)S(1)}, bf16[8,64,128]{2,1,0:T(8,128)(2,1)S(1)}, u32[]{:S(2)}, u32[]{:S(2)}) %collective-permute-start.22) | collective-permute-done | bytes 131104 | tf_op jit(solution)/shard_map/ppermute | solution.py:294
  120.0 0.9 reshape.470
  120.9 0.9 reshape.469
  121.8 1.0 collective-permute-done.12.before_ref
  (69 shorter events, 7.7 us)
Async XLA Ops:
  0.6 30.3 %copy-start = (bf16[512,512]{1,0:T(8,128)(2,1)S(1)}, bf16[512,512]{1,0:T(8,128)(2,1)}, u32[]{:S(2)}) copy-start(bf16[512,512]{1,0:T(8,128)(2,1)} %constant.277.clone.order_ref) | copy-start | bytes 1572868
  2.4 50.3 %collective-permute-start.7 = (bf16[256,256]{1,0:T(8,128)(2,1)S(1)}, bf16[256,256]{1,0:T(8,128)(2,1)S(1)}, u32[]{:S(2)}, u32[]{:S(2)}) collective-permute-start(bf16[256,256]{1,0:T(8,128)(2,1)S(1)} %constant_dynamic-update-slice_fusion), channel_id=1, source_target_pairs={{0,8},{1,9},{2,10},{3,11},{4,12},{5,13},{6,14},{7,15},{8,0},{9,1},... | collective-permute-start | bytes 393224 | tf_op jit(solution)/shard_map/ppermute | solution.py:289
  5.4 47.2 %collective-permute-start.5 = (bf16[256,256]{1,0:T(8,128)(2,1)S(1)}, bf16[256,256]{1,0:T(8,128)(2,1)S(1)}, u32[]{:S(2)}, u32[]{:S(2)}) collective-permute-start(bf16[256,256]{1,0:T(8,128)(2,1)S(1)} %constant_dynamic-update-slice_fusion), channel_id=1, source_target_pairs={{0,12},{1,13},{2,14},{3,15},{4,0},{5,1},{6,2},{7,3},{8,4},{9,5},{1... | collective-permute-start | bytes 393224 | tf_op jit(solution)/shard_map/ppermute | solution.py:289
  6.6 12.6 %collective-permute-start.2 = (bf16[256,256]{1,0:T(8,128)(2,1)S(1)}, bf16[256,256]{1,0:T(8,128)(2,1)S(1)}, u32[]{:S(2)}, u32[]{:S(2)}) collective-permute-start(bf16[256,256]{1,0:T(8,128)(2,1)S(1)} %constant_dynamic-update-slice_fusion), channel_id=1, source_target_pairs={{0,2},{1,3},{2,0},{3,1},{4,6},{5,7},{6,4},{7,5},{8,10},{9,11},{10,... | collective-permute-start | bytes 393224 | tf_op jit(solution)/shard_map/ppermute | solution.py:289
  13.7 11.9 %collective-permute-start.1 = (bf16[256,256]{1,0:T(8,128)(2,1)S(1)}, bf16[256,256]{1,0:T(8,128)(2,1)S(1)}, u32[]{:S(2)}, u32[]{:S(2)}) collective-permute-start(bf16[256,256]{1,0:T(8,128)(2,1)S(1)} %constant_dynamic-update-slice_fusion), channel_id=1, source_target_pairs={{0,3},{1,0},{2,1},{3,2},{4,7},{5,4},{6,5},{7,6},{8,11},{9,8},{10,9... | collective-permute-start | bytes 393224 | tf_op jit(solution)/shard_map/ppermute | solution.py:289
  13.7 11.9 %collective-permute-start = (bf16[256,256]{1,0:T(8,128)(2,1)S(1)}, bf16[256,256]{1,0:T(8,128)(2,1)S(1)}, u32[]{:S(2)}, u32[]{:S(2)}) collective-permute-start(bf16[256,256]{1,0:T(8,128)(2,1)S(1)} %constant_dynamic-update-slice_fusion), channel_id=1, source_target_pairs={{0,1},{1,2},{2,3},{3,0},{4,5},{5,6},{6,7},{7,4},{8,9},{9,10},{10,1... | collective-permute-start | bytes 393224 | tf_op jit(solution)/shard_map/ppermute | solution.py:289
  19.2 8.2 %collective-permute-start.3 = (bf16[256,256]{1,0:T(8,128)(2,1)S(1)}, bf16[256,256]{1,0:T(8,128)(2,1)S(1)}, u32[]{:S(2)}, u32[]{:S(2)}) collective-permute-start(bf16[256,256]{1,0:T(8,128)(2,1)S(1)} %constant_dynamic-update-slice_fusion), channel_id=1, source_target_pairs={{0,4},{1,5},{2,6},{3,7},{4,8},{5,9},{6,10},{7,11},{8,12},{9,13},{1... | collective-permute-start | bytes 393224 | tf_op jit(solution)/shard_map/ppermute | solution.py:289
  25.7 27.0 %collective-permute-start.8 = (bf16[3,256,256]{2,1,0:T(8,128)(2,1)S(1)}, bf16[3,256,256]{2,1,0:T(8,128)(2,1)S(1)}, u32[]{:S(2)}, u32[]{:S(2)}) collective-permute-start(bf16[3,256,256]{2,1,0:T(8,128)(2,1)S(1)} %pad_maximum_fusion.1), channel_id=1, source_target_pairs={{0,8},{1,9},{2,10},{3,11},{4,12},{5,13},{6,14},{7,15},{8,0},{9,1},... | collective-permute-start | bytes 1179656 | tf_op jit(solution)/shard_map/ppermute | solution.py:289
  27.3 25.3 %collective-permute-start.4 = (bf16[3,256,256]{2,1,0:T(8,128)(2,1)S(1)}, bf16[3,256,256]{2,1,0:T(8,128)(2,1)S(1)}, u32[]{:S(2)}, u32[]{:S(2)}) collective-permute-start(bf16[3,256,256]{2,1,0:T(8,128)(2,1)S(1)} %pad_maximum_fusion.1), channel_id=1, source_target_pairs={{0,4},{1,5},{2,6},{3,7},{4,8},{5,9},{6,10},{7,11},{8,12},{9,13},{1... | collective-permute-start | bytes 1179656 | tf_op jit(solution)/shard_map/ppermute | solution.py:289
  27.4 25.3 %collective-permute-start.6 = (bf16[3,256,256]{2,1,0:T(8,128)(2,1)S(1)}, bf16[3,256,256]{2,1,0:T(8,128)(2,1)S(1)}, u32[]{:S(2)}, u32[]{:S(2)}) collective-permute-start(bf16[3,256,256]{2,1,0:T(8,128)(2,1)S(1)} %pad_maximum_fusion.1), channel_id=1, source_target_pairs={{0,12},{1,13},{2,14},{3,15},{4,0},{5,1},{6,2},{7,3},{8,4},{9,5},{1... | collective-permute-start | bytes 1179656 | tf_op jit(solution)/shard_map/ppermute | solution.py:289
  30.9 1.6 %copy-start.1 = (bf16[256,4096]{1,0:T(8,128)(2,1)S(1)}, bf16[256,4096]{1,0:T(8,128)(2,1)}, u32[]{:S(2)}) copy-start(bf16[256,4096]{1,0:T(8,128)(2,1)} %w_ref.3) | copy-start | bytes 6291460
  32.5 9.4 %copy-start.2 = (bf16[256,4096]{1,0:T(8,128)(2,1)S(1)}, bf16[256,4096]{1,0:T(8,128)(2,1)}, u32[]{:S(2)}) copy-start(bf16[256,4096]{1,0:T(8,128)(2,1)} %w_ref.2) | copy-start | bytes 6291460
  65.4 8.5 %collective-permute-start.15 = (bf16[128,64,128]{2,1,0:T(8,128)(2,1)S(1)}, bf16[128,64,128]{2,1,0:T(8,128)(2,1)S(1)}, u32[]{:S(2)}, u32[]{:S(2)}) collective-permute-start(bf16[128,64,128]{2,1,0:T(8,128)(2,1)S(1)} %get-tuple-element.40), channel_id=1, source_target_pairs={{0,16},{16,0},{32,48},{48,32},{64,80},{80,64},{96,112},{112,96},{1... | collective-permute-start | bytes 6291464 | tf_op jit(solution)/shard_map/ppermute | solution.py:324
  65.5 16.4 %collective-permute-start.11 = (bf16[1024,256]{1,0:T(8,128)(2,1)S(1)}, bf16[1024,256]{1,0:T(8,128)(2,1)S(1)}, u32[]{:S(2)}, u32[]{:S(2)}) collective-permute-start(bf16[1024,256]{1,0:T(8,128)(2,1)S(1)} %shard_map.93), channel_id=1, source_target_pairs={{0,8},{1,9},{2,10},{3,11},{4,12},{5,13},{6,14},{7,15},{8,0},{9,1},... | collective-permute-start | bytes 1572872 | tf_op jit(solution)/shard_map/ppermute | solution.py:321
  70.6 22.0 %collective-permute-start.9 = (bf16[1024,256]{1,0:T(8,128)(2,1)S(1)}, bf16[1024,256]{1,0:T(8,128)(2,1)S(1)}, u32[]{:S(2)}, u32[]{:S(2)}) collective-permute-start(bf16[1024,256]{1,0:T(8,128)(2,1)S(1)} %get-tuple-element.34), channel_id=1, source_target_pairs={{0,4},{1,5},{2,6},{3,7},{4,8},{5,9},{6,10},{7,11},{8,12},{9,13},{1... | collective-permute-start | bytes 1572872 | tf_op jit(solution)/shard_map/ppermute | solution.py:327
  71.5 22.6 %collective-permute-start.10 = (bf16[1024,256]{1,0:T(8,128)(2,1)S(1)}, bf16[1024,256]{1,0:T(8,128)(2,1)S(1)}, u32[]{:S(2)}, u32[]{:S(2)}) collective-permute-start(bf16[1024,256]{1,0:T(8,128)(2,1)S(1)} %get-tuple-element.35), channel_id=1, source_target_pairs={{0,12},{1,13},{2,14},{3,15},{4,0},{5,1},{6,2},{7,3},{8,4},{9,5},{1... | collective-permute-start | bytes 1572872 | tf_op jit(solution)/shard_map/ppermute | solution.py:327
  74.3 29.6 %collective-permute-start.19 = (bf16[32,64,128]{2,1,0:T(8,128)(2,1)S(1)}, bf16[32,64,128]{2,1,0:T(8,128)(2,1)S(1)}, u32[]{:S(2)}, u32[]{:S(2)}) collective-permute-start(bf16[32,64,128]{2,1,0:T(8,128)(2,1)S(1)} %get-tuple-element.58), channel_id=1, source_target_pairs={{0,128},{16,144},{32,160},{48,176},{64,192},{80,208},{96,224},{112... | collective-permute-start | bytes 1572872 | tf_op jit(solution)/shard_map/ppermute | solution.py:335
  75.1 28.6 %collective-permute-start.18 = (bf16[16,64,128]{2,1,0:T(8,128)(2,1)S(1)}, bf16[16,64,128]{2,1,0:T(8,128)(2,1)S(1)}, u32[]{:S(2)}, u32[]{:S(2)}) collective-permute-start(bf16[16,64,128]{2,1,0:T(8,128)(2,1)S(1)} %get-tuple-element.60), channel_id=1, source_target_pairs={{0,64},{16,80},{32,96},{48,112},{64,0},{80,16},{96,32},{112,48},{1... | collective-permute-start | bytes 786440 | tf_op jit(solution)/shard_map/ppermute | solution.py:294
  81.9 21.9 %collective-permute-start.17 = (bf16[16,64,128]{2,1,0:T(8,128)(2,1)S(1)}, bf16[16,64,128]{2,1,0:T(8,128)(2,1)S(1)}, u32[]{:S(2)}, u32[]{:S(2)}) collective-permute-start(bf16[16,64,128]{2,1,0:T(8,128)(2,1)S(1)} %get-tuple-element.61), channel_id=1, source_target_pairs={{0,96},{16,112},{32,0},{48,16},{64,32},{80,48},{96,64},{112,80},{1... | collective-permute-start | bytes 786440 | tf_op jit(solution)/shard_map/ppermute | solution.py:294
  92.6 11.3 %collective-permute-start.16 = (bf16[16,64,128]{2,1,0:T(8,128)(2,1)S(1)}, bf16[16,64,128]{2,1,0:T(8,128)(2,1)S(1)}, u32[]{:S(2)}, u32[]{:S(2)}) collective-permute-start(bf16[16,64,128]{2,1,0:T(8,128)(2,1)S(1)} %get-tuple-element.62), channel_id=1, source_target_pairs={{0,32},{16,48},{32,64},{48,80},{64,96},{80,112},{96,0},{112,16},{1... | collective-permute-start | bytes 786440 | tf_op jit(solution)/shard_map/ppermute | solution.py:294
  94.4 27.4 %collective-permute-start.14 = (bf16[256,256]{1,0:T(8,128)(2,1)S(1)}, bf16[256,256]{1,0:T(8,128)(2,1)S(1)}, u32[]{:S(2)}, u32[]{:S(2)}) collective-permute-start(bf16[256,256]{1,0:T(8,128)(2,1)S(1)} %get-tuple-element.64), channel_id=1, source_target_pairs={{0,2},{1,3},{2,0},{3,1},{4,6},{5,7},{6,4},{7,5},{8,10},{9,11},{10,... | collective-permute-start | bytes 393224 | tf_op jit(solution)/shard_map/ppermute | solution.py:294
  103.7 18.1 %collective-permute-start.13 = (bf16[256,256]{1,0:T(8,128)(2,1)S(1)}, bf16[256,256]{1,0:T(8,128)(2,1)S(1)}, u32[]{:S(2)}, u32[]{:S(2)}) collective-permute-start(bf16[256,256]{1,0:T(8,128)(2,1)S(1)} %get-tuple-element.65), channel_id=1, source_target_pairs={{0,3},{1,0},{2,1},{3,2},{4,7},{5,4},{6,5},{7,6},{8,11},{9,8},{10,9... | collective-permute-start | bytes 393224 | tf_op jit(solution)/shard_map/ppermute | solution.py:294
  103.9 10.6 %collective-permute-start.20 = (bf16[8,64,128]{2,1,0:T(8,128)(2,1)S(1)}, bf16[8,64,128]{2,1,0:T(8,128)(2,1)S(1)}, u32[]{:S(2)}, u32[]{:S(2)}) collective-permute-start(bf16[8,64,128]{2,1,0:T(8,128)(2,1)S(1)} %add_convert_fusion.10), channel_id=1, source_target_pairs={{0,128},{16,144},{32,160},{48,176},{64,192},{80,208},{96,224},{112... | collective-permute-start | bytes 393224 | tf_op jit(solution)/shard_map/ppermute | solution.py:341
  104.2 10.9 %collective-permute-start.21 = (bf16[8,64,128]{2,1,0:T(8,128)(2,1)S(1)}, bf16[8,64,128]{2,1,0:T(8,128)(2,1)S(1)}, u32[]{:S(2)}, u32[]{:S(2)}) collective-permute-start(bf16[8,64,128]{2,1,0:T(8,128)(2,1)S(1)} %get-tuple-element.68), channel_id=1, source_target_pairs={{0,32},{16,48},{32,64},{48,80},{64,96},{80,112},{96,0},{112,16},{1... | collective-permute-start | bytes 393224 | tf_op jit(solution)/shard_map/ppermute | solution.py:294
  105.5 10.3 %collective-permute-start.23 = (bf16[8,64,128]{2,1,0:T(8,128)(2,1)S(1)}, bf16[8,64,128]{2,1,0:T(8,128)(2,1)S(1)}, u32[]{:S(2)}, u32[]{:S(2)}) collective-permute-start(bf16[8,64,128]{2,1,0:T(8,128)(2,1)S(1)} %get-tuple-element.69), channel_id=1, source_target_pairs={{0,64},{16,80},{32,96},{48,112},{64,0},{80,16},{96,32},{112,48},{1... | collective-permute-start | bytes 393224 | tf_op jit(solution)/shard_map/ppermute | solution.py:294
  114.5 5.0 %collective-permute-start.22 = (bf16[8,64,128]{2,1,0:T(8,128)(2,1)S(1)}, bf16[8,64,128]{2,1,0:T(8,128)(2,1)S(1)}, u32[]{:S(2)}, u32[]{:S(2)}) collective-permute-start(bf16[8,64,128]{2,1,0:T(8,128)(2,1)S(1)} %get-tuple-element.70), channel_id=1, source_target_pairs={{0,96},{16,112},{32,0},{48,16},{64,32},{80,48},{96,64},{112,80},{1... | collective-permute-start | bytes 393224 | tf_op jit(solution)/shard_map/ppermute | solution.py:294
  115.1 7.7 %collective-permute-start.12 = (bf16[256,256]{1,0:T(8,128)(2,1)S(1)}, bf16[256,256]{1,0:T(8,128)(2,1)S(1)}, u32[]{:S(2)}, u32[]{:S(2)}) collective-permute-start(bf16[256,256]{1,0:T(8,128)(2,1)S(1)} %get-tuple-element.66), channel_id=1, source_target_pairs={{0,1},{1,2},{2,3},{3,0},{4,5},{5,6},{6,7},{7,4},{8,9},{9,10},{10,1... | collective-permute-start | bytes 393224 | tf_op jit(solution)/shard_map/ppermute | solution.py:294

commit v5 on v4

--- a/solution.py
+++ b/solution.py
@@ -2,7 +2,6 @@
 
 import jax
 import jax.numpy as jnp
-import numpy as np
 from jax import lax
 from jax.experimental import pallas as pl
 from jax.experimental.pallas import tpu as pltpu
@@ -52,10 +51,10 @@
     return dest, send, first, last
 
 
-def dense_kernel(turned, dest, w_ref, order_ref, d_ref):
+def dense_kernel(turned, dest, w_ref, d_ref, lines):
     d_ref[...] = jnp.zeros_like(d_ref)
     at_once = 16
-    count = 8
+    count = at_once // 2 if turned else at_once
     low = lax.broadcasted_iota(jnp.int32, (count, 2 * BLK), 1) < BLK
     upper = lax.broadcasted_iota(jnp.int32, (BLK, 2 * BLK), 1) >= BLK
 
@@ -63,56 +62,43 @@
         here = d_ref.at[(e & (HBL - 1)) >> 1, pl.ds(pl.multiple_of((e >> 4) * BLK, BLK), BLK), :]
         here[...] = jnp.where(upper == ((e & 1) == 1), block.astype(jnp.bfloat16), here[...])
 
-    def lines(even, odd):
-        rows = jnp.concatenate(even + odd, axis=0).astype(jnp.bfloat16)
-        return jnp.dot(order_ref[...], rows, preferred_element_type=jnp.float32)
-
     def some(k, carry):
         start = pl.multiple_of(k * at_once, at_once)
-        two = [
-            w_ref[pl.ds(start, at_once), 2 * BLK * t : 2 * BLK * (t + 1)].astype(jnp.float32)
-            for t in range(BLK // 2)
-        ]
-        swapped = [pltpu.roll(x, BLK, 1) for x in two]
-        if turned:
-            even = [jnp.where(low, x[:count], y[count:]) for x, y in zip(two, swapped)]
-            odd = [jnp.where(low, y[:count], x[count:]) for x, y in zip(two, swapped)]
-            blocks = lines(even, odd)
-            for u in range(count):
-                block = blocks[u * BLK : (u + 1) * BLK]
+        for t in range(BLK // 2):
+            two = w_ref[pl.ds(start, at_once), 2 * BLK * t : 2 * BLK * (t + 1)].astype(jnp.float32)
+            swapped = pltpu.roll(two, BLK, 1)
+            if turned:
+                even = jnp.where(low, two[:count], swapped[count:])
+                odd = jnp.where(low, swapped[:count], two[count:])
+            else:
+                even, odd = jnp.where(low, two, swapped), jnp.where(low, swapped, two)
+            lines[pl.ds(2 * t, count, stride=BLK), :] = even
+            lines[pl.ds(2 * t + 1, count, stride=BLK), :] = odd
+        for u in range(count):
+            block = lines[u * BLK : (u + 1) * BLK, :]
+            if turned:
                 both = jnp.concatenate([block, block], axis=0).T
                 place(dest[start + u], both[:BLK])
                 place(dest[start + u + count], both[BLK:])
-        else:
-            for half in range(2):
-                part = slice(half * count, (half + 1) * count)
-                even = [jnp.where(low, x[part], y[part]) for x, y in zip(two, swapped)]
-                odd = [jnp.where(low, y[part], x[part]) for x, y in zip(two, swapped)]
-                blocks = lines(even, odd)
-                for u in range(count):
-                    place(dest[start + half * count + u], blocks[u * BLK : (u + 1) * BLK])
+            else:
+                place(dest[start + u], block)
         return carry
 
     lax.fori_loop(0, dest.shape[0] // at_once, some, 0)
 
 
-def line_order():
-    to, at = np.indices((8 * BLK, 8 * BLK))
-    row = at // 8 % (BLK // 2) * 2 + at // (4 * BLK)
-    return jnp.asarray((to == at % 8 * BLK + row).astype(jnp.bfloat16))
-
-
-def dense_weights(dest, weights, order, turned):
+def dense_weights(dest, weights, turned):
     whole = pl.BlockSpec(memory_space=pltpu.VMEM)
     return pl.pallas_call(
         functools.partial(dense_kernel, turned),
         out_shape=jax.ShapeDtypeStruct((8, D + BLK, 2 * BLK), jnp.bfloat16),
-        in_specs=[pl.BlockSpec(memory_space=pltpu.SMEM), whole, whole],
+        in_specs=[pl.BlockSpec(memory_space=pltpu.SMEM), whole],
         out_specs=whole,
-        compiler_params=pltpu.CompilerParams(vmem_limit_bytes=15 * MIB),
+        scratch_shapes=[pltpu.VMEM((16 * BLK, 2 * BLK), jnp.float32)],
+        compiler_params=pltpu.CompilerParams(vmem_limit_bytes=14 * MIB),
         cost_estimate=pl.CostEstimate(flops=0, transcendentals=0, bytes_accessed=20 << 20),
         name="dense_out" if turned else "dense_in",
-    )(dest, weights, order)
+    )(dest, weights)
 
 
 def hidden_kernel(xc_ref, din_ref, dout_ref, both_ref):
@@ -144,7 +130,7 @@
         out_shape=jax.ShapeDtypeStruct((1024, 2 * tok), jnp.bfloat16),
         in_specs=[whole] * 3,
         out_specs=whole,
-        compiler_params=pltpu.CompilerParams(vmem_limit_bytes=26 * MIB),
+        compiler_params=pltpu.CompilerParams(vmem_limit_bytes=16 * MIB),
         cost_estimate=cost,
         name="hidden_stage",
     )(xc, din, dout)
@@ -236,7 +222,7 @@
         out_shape=(jax.ShapeDtypeStruct((1024, both.shape[1]), jnp.bfloat16),) * count,
         in_specs=[whole] * 3,
         out_specs=(whole,) * count,
-        compiler_params=pltpu.CompilerParams(vmem_limit_bytes=24 * MIB),
+        compiler_params=pltpu.CompilerParams(vmem_limit_bytes=12 * MIB),
         cost_estimate=cost,
     )(din, dout, both)
 
@@ -311,10 +297,9 @@
     wide = sent(near, along_x)
     pieces = [(own[None], others) for own, others in zip([block] + wide_own, [near] + wide)]
     xc = jnp.concatenate([piece for both in pieces for piece in both])
-    order = line_order()
     dest, _ = lax.optimization_barrier((tables[0], near))
-    din = dense_weights(dest, in_weights, order, False)
-    dout = dense_weights(dest, out_weights, order, True)
+    din = dense_weights(dest, in_weights, False)
+    dout = dense_weights(dest, out_weights, True)
     both = hidden_stage(xc, din, dout, tok)
     (opposite,) = part_stage(din, dout, both, 3, 1)
     opposite, both = lax.optimization_barrier((opposite, both))

time: 125 us -> 123 us (0.984)
  Pallas kernels: 37.8 us -> 35.8 us
    pallas_call x2, Pallas kernels: 20.1 us -> 18.1 us  [dense_weights(): pl.pallas_call(functools.partial(dense_kernel, turned), out_shape=jax.Sha...]
    unnamed x17 -> x15, local copies, waits for them, and re-layouts: 3.43 us -> 3.36 us
  transfers between devices with their start and end apart: 24 -> 24, of which waited for: 7 -> 7; matrix products, arithmetic and copies ran while one was open for 5% -> 5% of each run, Pallas kernels for 20% -> 18%
where the time goes in v5:
time: 123 us; the launch traced here: 121 us
  starting transfers between devices  42.5 us (35%)
  Pallas kernels  35.8 us (29%)
  waiting for transfers between devices  32.8 us (27%)
  local copies, waits for them, and re-layouts  6.62 us (5%)
  other arithmetic  2.76 us (2%)
    ppermute x9, starting transfers between devices, sent(): return [way(block) for way in ways]  20.3 us
    pallas_call x2, Pallas kernels, dense_weights(): pl.pallas_call(functools.partial(dense_kernel, turned), out_shape=jax.Sha...  18.1 us
    ppermute x9, starting transfers between devices, collect(): return (own, up(after), down(before), over(opposite))  17.4 us
    ppermute x2, waiting for transfers between devices, on_device(): across_terms = (own, along_x[0](after), along_x[1](before), from_opposite)  10.2 us
    ppermute x1, waiting for transfers between devices, on_device(): from_deep = deep_way(to_deep)  7.78 us
    pallas_call x1, Pallas kernels, grad_stage(): pl.pallas_call(functools.partial(grad_kernel, scale), grid=(16,), out_sha...  7.63 us
    ppermute x9, waiting for transfers between devices, sent(): return [way(block) for way in ways]  5.77 us
    pallas_call x2, Pallas kernels, part_stage(): pl.pallas_call(functools.partial(part_kernel, quarter), out_shape=(jax.Sh...  5.65 us
  transfers between devices with their start and end apart: 24, of which 7 were waited for; matrix products, arithmetic and copies ran while one was open for 5% of the time, Pallas kernels for 18%

profile of v5, /device:TPU:8, one launch (start us, length us, event | category | flops | bytes accessed | tf_op | source)
XLA Modules:
  0.0 121.5 jit_solution(4517622173734459293)
XLA Ops:
  0.6 0.8 constant_dynamic-update-slice_fusion.1
  1.5 0.8 constant_dynamic-update-slice_fusion
  2.3 3.0 %collective-permute-start.7 = (bf16[256,256]{1,0:T(8,128)(2,1)S(1)}, bf16[256,256]{1,0:T(8,128)(2,1)S(1)}, u32[]{:S(2)}, u32[]{:S(2)}) collective-permute-start(bf16[256,256]{1,0:T(8,128)(2,1)S(1)} %constant_dynamic-update-slice_fusion), channel_id=1, source_target_pairs={{0,8},{1,9},{2,10},{3,11},{4,12},{5,13},{6,14},{7,15},{8,0},{9,1},... | collective-permute-start | bytes 393224 | tf_op jit(solution)/shard_map/ppermute | solution.py:275
  5.3 1.1 collective-permute-start.5
  6.5 7.2 %collective-permute-start.2 = (bf16[256,256]{1,0:T(8,128)(2,1)S(1)}, bf16[256,256]{1,0:T(8,128)(2,1)S(1)}, u32[]{:S(2)}, u32[]{:S(2)}) collective-permute-start(bf16[256,256]{1,0:T(8,128)(2,1)S(1)} %constant_dynamic-update-slice_fusion), channel_id=1, source_target_pairs={{0,2},{1,3},{2,0},{3,1},{4,6},{5,7},{6,4},{7,5},{8,10},{9,11},{10,... | collective-permute-start | bytes 393224 | tf_op jit(solution)/shard_map/ppermute | solution.py:275
  13.7 2.9 %collective-permute-start = (bf16[256,256]{1,0:T(8,128)(2,1)S(1)}, bf16[256,256]{1,0:T(8,128)(2,1)S(1)}, u32[]{:S(2)}, u32[]{:S(2)}) collective-permute-start(bf16[256,256]{1,0:T(8,128)(2,1)S(1)} %constant_dynamic-update-slice_fusion), channel_id=1, source_target_pairs={{0,1},{1,2},{2,3},{3,0},{4,5},{5,6},{6,7},{7,4},{8,9},{9,10},{10,1... | collective-permute-start | bytes 393224 | tf_op jit(solution)/shard_map/ppermute | solution.py:275
  19.1 0.9 collective-permute-start.3
  20.0 5.6 %collective-permute-done.1 = bf16[256,256]{1,0:T(8,128)(2,1)S(1)} collective-permute-done((bf16[256,256]{1,0:T(8,128)(2,1)S(1)}, bf16[256,256]{1,0:T(8,128)(2,1)S(1)}, u32[]{:S(2)}, u32[]{:S(2)}) %collective-permute-start.1) | collective-permute-done | bytes 131104 | tf_op jit(solution)/shard_map/ppermute | solution.py:275
  25.6 1.6 %collective-permute-start.8 = (bf16[3,256,256]{2,1,0:T(8,128)(2,1)S(1)}, bf16[3,256,256]{2,1,0:T(8,128)(2,1)S(1)}, u32[]{:S(2)}, u32[]{:S(2)}) collective-permute-start(bf16[3,256,256]{2,1,0:T(8,128)(2,1)S(1)} %pad_maximum_fusion.1), channel_id=1, source_target_pairs={{0,8},{1,9},{2,10},{3,11},{4,12},{5,13},{6,14},{7,15},{8,0},{9,1},... | collective-permute-start | bytes 1179656 | tf_op jit(solution)/shard_map/ppermute | solution.py:275
  27.3 3.5 %collective-permute-start.6 = (bf16[3,256,256]{2,1,0:T(8,128)(2,1)S(1)}, bf16[3,256,256]{2,1,0:T(8,128)(2,1)S(1)}, u32[]{:S(2)}, u32[]{:S(2)}) collective-permute-start(bf16[3,256,256]{2,1,0:T(8,128)(2,1)S(1)} %pad_maximum_fusion.1), channel_id=1, source_target_pairs={{0,12},{1,13},{2,14},{3,15},{4,0},{5,1},{6,2},{7,3},{8,4},{9,5},{1... | collective-permute-start | bytes 1179656 | tf_op jit(solution)/shard_map/ppermute | solution.py:275
  30.8 1.6 %copy-done = bf16[256,4096]{1,0:T(8,128)(2,1)S(1)} copy-done((bf16[256,4096]{1,0:T(8,128)(2,1)S(1)}, bf16[256,4096]{1,0:T(8,128)(2,1)}, u32[]{:S(2)}) %copy-start) | copy-done | bytes 2097176
  32.4 8.4 %dense_out.1.dout_ref = bf16[8,4160,128]{2,1,0:T(8,128)(2,1)S(1)} custom-call(s32[256]{0:T(256)S(1)} %get-tuple-element.29.dest, bf16[256,4096]{1,0:T(8,128)(2,1)S(1)} %copy-done), custom_call_target="tpu_custom_call" | custom-call | bytes 20971520 | tf_op jit(solution)/shard_map/dense_out/pallas_call | solution.py:92
  40.9 9.6 %dense_in.1.din_ref = bf16[8,4160,128]{2,1,0:T(8,128)(2,1)S(1)} custom-call(s32[256]{0:T(256)S(1)} %get-tuple-element.29.dest, bf16[256,4096]{1,0:T(8,128)(2,1)S(1)} %copy-done.1), custom_call_target="tpu_custom_call" | custom-call | bytes 20971520 | tf_op jit(solution)/shard_map/dense_in/pallas_call | solution.py:92
  50.7 3.6 %hidden_stage.1.both_ref = bf16[1024,256]{1,0:T(8,128)(2,1)S(1)} custom-call(bf16[16,256,256]{2,1,0:T(8,128)(2,1)S(1)} %constant_dynamic-update-slice_fusion.2.xc_ref, bf16[8,4160,128]{2,1,0:T(8,128)(2,1)S(1)} %dense_in.1.din_ref, bf16[8,4160,128]{2,1,0:T(8,128)(2,1)S(1)} %dense_out.1.dout_ref), custom_call_target="tpu_custom_call" | custom-call | flops 2147483648 | bytes 18874368 | tf_op jit(solution)/shard_map/hidden_stage/pallas_call | solution.py:128
  54.2 1.4 %shard_map.84 = bf16[1024,256]{1,0:T(8,128)(2,1)S(1)} custom-call(bf16[8,4160,128]{2,1,0:T(8,128)(2,1)S(1)} %dense_in.1.din_ref, bf16[8,4160,128]{2,1,0:T(8,128)(2,1)S(1)} %dense_out.1.dout_ref, bf16[1024,256]{1,0:T(8,128)(2,1)S(1)} %hidden_stage.1.both_ref), custom_call_target="tpu_custom_call" | custom-call | flops 536870912 | bytes 4718592 | tf_op jit(solution)/shard_map/pallas_call | solution.py:220
  55.7 7.6 %grad_stage.1 = (bf16[128,64,128]{2,1,0:T(8,128)(2,1)S(1)}, bf16[128,64,128]{2,1,0:T(8,128)(2,1)S(1)}) custom-call(s32[256]{0:T(256)S(1)} %get-tuple-element.29.dest, s32[256]{0:T(256)S(1)} %fusion.18.send, s32[64]{0:T(128)S(1)} %get-tuple-element.55.first, s32[64]{0:T(128)S(1)} %get-tuple-element.54.last, ...), custom_call_target="tpu_custom_call" | custom-call | flops 536870912 | bytes 7340032 | tf_op jit(solution)/shard_map/grad_stage/pallas_call | solution.py:183
  63.4 0.8 collective-permute-start.11
  64.2 4.2 %shard_map.85 = (bf16[1024,256]{1,0:T(8,128)(2,1)S(1)}, bf16[1024,256]{1,0:T(8,128)(2,1)S(1)}, bf16[1024,256]{1,0:T(8,128)(2,1)S(1)}) custom-call(bf16[8,4160,128]{2,1,0:T(8,128)(2,1)S(1)} %dense_in.1.din_ref, bf16[8,4160,128]{2,1,0:T(8,128)(2,1)S(1)} %dense_out.1.dout_ref, bf16[1024,256]{1,0:T(8,128)(2,1)S(1)} %hidden_stage.1.both_ref), custom_call_target="tpu_custom_call" | custom-call | flops 1610612736 | bytes 14155776 | tf_op jit(solution)/shard_map/pallas_call | solution.py:220
  68.5 1.0 collective-permute-start.9
  69.4 2.4 %collective-permute-start.10 = (bf16[1024,256]{1,0:T(8,128)(2,1)S(1)}, bf16[1024,256]{1,0:T(8,128)(2,1)S(1)}, u32[]{:S(2)}, u32[]{:S(2)}) collective-permute-start(bf16[1024,256]{1,0:T(8,128)(2,1)S(1)} %get-tuple-element.35), channel_id=1, source_target_pairs={{0,12},{1,13},{2,14},{3,15},{4,0},{5,1},{6,2},{7,3},{8,4},{9,5},{1... | collective-permute-start | bytes 1572872 | tf_op jit(solution)/shard_map/ppermute | solution.py:312
  73.1 2.4 %collective-permute-start.18 = (bf16[16,64,128]{2,1,0:T(8,128)(2,1)S(1)}, bf16[16,64,128]{2,1,0:T(8,128)(2,1)S(1)}, u32[]{:S(2)}, u32[]{:S(2)}) collective-permute-start(bf16[16,64,128]{2,1,0:T(8,128)(2,1)S(1)} %get-tuple-element.60), channel_id=1, source_target_pairs={{0,64},{16,80},{32,96},{48,112},{64,0},{80,16},{96,32},{112,48},{1... | collective-permute-start | bytes 786440 | tf_op jit(solution)/shard_map/ppermute | solution.py:280
  75.5 4.4 %collective-permute-done.11 = bf16[1024,256]{1,0:T(8,128)(2,1)S(1)} collective-permute-done((bf16[1024,256]{1,0:T(8,128)(2,1)S(1)}, bf16[1024,256]{1,0:T(8,128)(2,1)S(1)}, u32[]{:S(2)}, u32[]{:S(2)}) %collective-permute-start.11) | collective-permute-done | bytes 524320 | tf_op jit(solution)/shard_map/ppermute | solution.py:306
  80.3 10.2 %collective-permute-done.9 = bf16[1024,256]{1,0:T(8,128)(2,1)S(1)} collective-permute-done((bf16[1024,256]{1,0:T(8,128)(2,1)S(1)}, bf16[1024,256]{1,0:T(8,128)(2,1)S(1)}, u32[]{:S(2)}, u32[]{:S(2)}) %collective-permute-start.9) | collective-permute-done | bytes 524320 | tf_op jit(solution)/shard_map/ppermute | solution.py:312
  90.5 1.6 %collective-permute-start.16 = (bf16[16,64,128]{2,1,0:T(8,128)(2,1)S(1)}, bf16[16,64,128]{2,1,0:T(8,128)(2,1)S(1)}, u32[]{:S(2)}, u32[]{:S(2)}) collective-permute-start(bf16[16,64,128]{2,1,0:T(8,128)(2,1)S(1)} %get-tuple-element.62), channel_id=1, source_target_pairs={{0,32},{16,48},{32,64},{48,80},{64,96},{80,112},{96,0},{112,16},{1... | collective-permute-start | bytes 786440 | tf_op jit(solution)/shard_map/ppermute | solution.py:280
  92.3 9.2 %collective-permute-start.14 = (bf16[256,256]{1,0:T(8,128)(2,1)S(1)}, bf16[256,256]{1,0:T(8,128)(2,1)S(1)}, u32[]{:S(2)}, u32[]{:S(2)}) collective-permute-start(bf16[256,256]{1,0:T(8,128)(2,1)S(1)} %get-tuple-element.64), channel_id=1, source_target_pairs={{0,2},{1,3},{2,0},{3,1},{4,6},{5,7},{6,4},{7,5},{8,10},{9,11},{10,... | collective-permute-start | bytes 393224 | tf_op jit(solution)/shard_map/ppermute | solution.py:280
  102.0 1.4 %collective-permute-start.21 = (bf16[8,64,128]{2,1,0:T(8,128)(2,1)S(1)}, bf16[8,64,128]{2,1,0:T(8,128)(2,1)S(1)}, u32[]{:S(2)}, u32[]{:S(2)}) collective-permute-start(bf16[8,64,128]{2,1,0:T(8,128)(2,1)S(1)} %get-tuple-element.68), channel_id=1, source_target_pairs={{0,32},{16,48},{32,64},{48,80},{64,96},{80,112},{96,0},{112,16},{1... | collective-permute-start | bytes 393224 | tf_op jit(solution)/shard_map/ppermute | solution.py:280
  103.4 1.2 %collective-permute-start.23 = (bf16[8,64,128]{2,1,0:T(8,128)(2,1)S(1)}, bf16[8,64,128]{2,1,0:T(8,128)(2,1)S(1)}, u32[]{:S(2)}, u32[]{:S(2)}) collective-permute-start(bf16[8,64,128]{2,1,0:T(8,128)(2,1)S(1)} %get-tuple-element.69), channel_id=1, source_target_pairs={{0,64},{16,80},{32,96},{48,112},{64,0},{80,16},{96,32},{112,48},{1... | collective-permute-start | bytes 393224 | tf_op jit(solution)/shard_map/ppermute | solution.py:280
  104.6 7.8 %collective-permute-done.20 = bf16[8,64,128]{2,1,0:T(8,128)(2,1)S(1)} collective-permute-done((bf16[8,64,128]{2,1,0:T(8,128)(2,1)S(1)}, bf16[8,64,128]{2,1,0:T(8,128)(2,1)S(1)}, u32[]{:S(2)}, u32[]{:S(2)}) %collective-permute-start.20) | collective-permute-done | bytes 131104 | tf_op jit(solution)/shard_map/ppermute | solution.py:326
  113.7 3.7 %collective-permute-done.22 = bf16[8,64,128]{2,1,0:T(8,128)(2,1)S(1)} collective-permute-done((bf16[8,64,128]{2,1,0:T(8,128)(2,1)S(1)}, bf16[8,64,128]{2,1,0:T(8,128)(2,1)S(1)}, u32[]{:S(2)}, u32[]{:S(2)}) %collective-permute-start.22) | collective-permute-done | bytes 131104 | tf_op jit(solution)/shard_map/ppermute | solution.py:280
  117.9 0.9 reshape.470
  118.8 0.9 reshape.469
  119.7 1.0 collective-permute-done.12.before_ref
  (67 shorter events, 7.8 us)
Async XLA Ops:
  2.3 48.3 %collective-permute-start.7 = (bf16[256,256]{1,0:T(8,128)(2,1)S(1)}, bf16[256,256]{1,0:T(8,128)(2,1)S(1)}, u32[]{:S(2)}, u32[]{:S(2)}) collective-permute-start(bf16[256,256]{1,0:T(8,128)(2,1)S(1)} %constant_dynamic-update-slice_fusion), channel_id=1, source_target_pairs={{0,8},{1,9},{2,10},{3,11},{4,12},{5,13},{6,14},{7,15},{8,0},{9,1},... | collective-permute-start | bytes 393224 | tf_op jit(solution)/shard_map/ppermute | solution.py:275
  5.3 45.2 %collective-permute-start.5 = (bf16[256,256]{1,0:T(8,128)(2,1)S(1)}, bf16[256,256]{1,0:T(8,128)(2,1)S(1)}, u32[]{:S(2)}, u32[]{:S(2)}) collective-permute-start(bf16[256,256]{1,0:T(8,128)(2,1)S(1)} %constant_dynamic-update-slice_fusion), channel_id=1, source_target_pairs={{0,12},{1,13},{2,14},{3,15},{4,0},{5,1},{6,2},{7,3},{8,4},{9,5},{1... | collective-permute-start | bytes 393224 | tf_op jit(solution)/shard_map/ppermute | solution.py:275
  6.5 12.6 %collective-permute-start.2 = (bf16[256,256]{1,0:T(8,128)(2,1)S(1)}, bf16[256,256]{1,0:T(8,128)(2,1)S(1)}, u32[]{:S(2)}, u32[]{:S(2)}) collective-permute-start(bf16[256,256]{1,0:T(8,128)(2,1)S(1)} %constant_dynamic-update-slice_fusion), channel_id=1, source_target_pairs={{0,2},{1,3},{2,0},{3,1},{4,6},{5,7},{6,4},{7,5},{8,10},{9,11},{10,... | collective-permute-start | bytes 393224 | tf_op jit(solution)/shard_map/ppermute | solution.py:275
  13.7 11.9 %collective-permute-start.1 = (bf16[256,256]{1,0:T(8,128)(2,1)S(1)}, bf16[256,256]{1,0:T(8,128)(2,1)S(1)}, u32[]{:S(2)}, u32[]{:S(2)}) collective-permute-start(bf16[256,256]{1,0:T(8,128)(2,1)S(1)} %constant_dynamic-update-slice_fusion), channel_id=1, source_target_pairs={{0,3},{1,0},{2,1},{3,2},{4,7},{5,4},{6,5},{7,6},{8,11},{9,8},{10,9... | collective-permute-start | bytes 393224 | tf_op jit(solution)/shard_map/ppermute | solution.py:275
  13.7 11.9 %collective-permute-start = (bf16[256,256]{1,0:T(8,128)(2,1)S(1)}, bf16[256,256]{1,0:T(8,128)(2,1)S(1)}, u32[]{:S(2)}, u32[]{:S(2)}) collective-permute-start(bf16[256,256]{1,0:T(8,128)(2,1)S(1)} %constant_dynamic-update-slice_fusion), channel_id=1, source_target_pairs={{0,1},{1,2},{2,3},{3,0},{4,5},{5,6},{6,7},{7,4},{8,9},{9,10},{10,1... | collective-permute-start | bytes 393224 | tf_op jit(solution)/shard_map/ppermute | solution.py:275
  19.1 8.2 %collective-permute-start.3 = (bf16[256,256]{1,0:T(8,128)(2,1)S(1)}, bf16[256,256]{1,0:T(8,128)(2,1)S(1)}, u32[]{:S(2)}, u32[]{:S(2)}) collective-permute-start(bf16[256,256]{1,0:T(8,128)(2,1)S(1)} %constant_dynamic-update-slice_fusion), channel_id=1, source_target_pairs={{0,4},{1,5},{2,6},{3,7},{4,8},{5,9},{6,10},{7,11},{8,12},{9,13},{1... | collective-permute-start | bytes 393224 | tf_op jit(solution)/shard_map/ppermute | solution.py:275
  25.6 25.0 %collective-permute-start.8 = (bf16[3,256,256]{2,1,0:T(8,128)(2,1)S(1)}, bf16[3,256,256]{2,1,0:T(8,128)(2,1)S(1)}, u32[]{:S(2)}, u32[]{:S(2)}) collective-permute-start(bf16[3,256,256]{2,1,0:T(8,128)(2,1)S(1)} %pad_maximum_fusion.1), channel_id=1, source_target_pairs={{0,8},{1,9},{2,10},{3,11},{4,12},{5,13},{6,14},{7,15},{8,0},{9,1},... | collective-permute-start | bytes 1179656 | tf_op jit(solution)/shard_map/ppermute | solution.py:275
  27.3 23.2 %collective-permute-start.4 = (bf16[3,256,256]{2,1,0:T(8,128)(2,1)S(1)}, bf16[3,256,256]{2,1,0:T(8,128)(2,1)S(1)}, u32[]{:S(2)}, u32[]{:S(2)}) collective-permute-start(bf16[3,256,256]{2,1,0:T(8,128)(2,1)S(1)} %pad_maximum_fusion.1), channel_id=1, source_target_pairs={{0,4},{1,5},{2,6},{3,7},{4,8},{5,9},{6,10},{7,11},{8,12},{9,13},{1... | collective-permute-start | bytes 1179656 | tf_op jit(solution)/shard_map/ppermute | solution.py:275
  27.3 23.2 %collective-permute-start.6 = (bf16[3,256,256]{2,1,0:T(8,128)(2,1)S(1)}, bf16[3,256,256]{2,1,0:T(8,128)(2,1)S(1)}, u32[]{:S(2)}, u32[]{:S(2)}) collective-permute-start(bf16[3,256,256]{2,1,0:T(8,128)(2,1)S(1)} %pad_maximum_fusion.1), channel_id=1, source_target_pairs={{0,12},{1,13},{2,14},{3,15},{4,0},{5,1},{6,2},{7,3},{8,4},{9,5},{1... | collective-permute-start | bytes 1179656 | tf_op jit(solution)/shard_map/ppermute | solution.py:275
  30.8 1.6 %copy-start = (bf16[256,4096]{1,0:T(8,128)(2,1)S(1)}, bf16[256,4096]{1,0:T(8,128)(2,1)}, u32[]{:S(2)}) copy-start(bf16[256,4096]{1,0:T(8,128)(2,1)} %w_ref.3) | copy-start | bytes 6291460
  32.4 8.4 %copy-start.1 = (bf16[256,4096]{1,0:T(8,128)(2,1)S(1)}, bf16[256,4096]{1,0:T(8,128)(2,1)}, u32[]{:S(2)}) copy-start(bf16[256,4096]{1,0:T(8,128)(2,1)} %w_ref.2) | copy-start | bytes 6291460
  63.3 8.5 %collective-permute-start.15 = (bf16[128,64,128]{2,1,0:T(8,128)(2,1)S(1)}, bf16[128,64,128]{2,1,0:T(8,128)(2,1)S(1)}, u32[]{:S(2)}, u32[]{:S(2)}) collective-permute-start(bf16[128,64,128]{2,1,0:T(8,128)(2,1)S(1)} %get-tuple-element.40), channel_id=1, source_target_pairs={{0,16},{16,0},{32,48},{48,32},{64,80},{80,64},{96,112},{112,96},{1... | collective-permute-start | bytes 6291464 | tf_op jit(solution)/shard_map/ppermute | solution.py:309
  63.4 16.4 %collective-permute-start.11 = (bf16[1024,256]{1,0:T(8,128)(2,1)S(1)}, bf16[1024,256]{1,0:T(8,128)(2,1)S(1)}, u32[]{:S(2)}, u32[]{:S(2)}) collective-permute-start(bf16[1024,256]{1,0:T(8,128)(2,1)S(1)} %shard_map.84), channel_id=1, source_target_pairs={{0,8},{1,9},{2,10},{3,11},{4,12},{5,13},{6,14},{7,15},{8,0},{9,1},... | collective-permute-start | bytes 1572872 | tf_op jit(solution)/shard_map/ppermute | solution.py:306
  68.5 22.0 %collective-permute-start.9 = (bf16[1024,256]{1,0:T(8,128)(2,1)S(1)}, bf16[1024,256]{1,0:T(8,128)(2,1)S(1)}, u32[]{:S(2)}, u32[]{:S(2)}) collective-permute-start(bf16[1024,256]{1,0:T(8,128)(2,1)S(1)} %get-tuple-element.34), channel_id=1, source_target_pairs={{0,4},{1,5},{2,6},{3,7},{4,8},{5,9},{6,10},{7,11},{8,12},{9,13},{1... | collective-permute-start | bytes 1572872 | tf_op jit(solution)/shard_map/ppermute | solution.py:312
  69.4 22.6 %collective-permute-start.10 = (bf16[1024,256]{1,0:T(8,128)(2,1)S(1)}, bf16[1024,256]{1,0:T(8,128)(2,1)S(1)}, u32[]{:S(2)}, u32[]{:S(2)}) collective-permute-start(bf16[1024,256]{1,0:T(8,128)(2,1)S(1)} %get-tuple-element.35), channel_id=1, source_target_pairs={{0,12},{1,13},{2,14},{3,15},{4,0},{5,1},{6,2},{7,3},{8,4},{9,5},{1... | collective-permute-start | bytes 1572872 | tf_op jit(solution)/shard_map/ppermute | solution.py:312
  72.2 29.5 %collective-permute-start.19 = (bf16[32,64,128]{2,1,0:T(8,128)(2,1)S(1)}, bf16[32,64,128]{2,1,0:T(8,128)(2,1)S(1)}, u32[]{:S(2)}, u32[]{:S(2)}) collective-permute-start(bf16[32,64,128]{2,1,0:T(8,128)(2,1)S(1)} %get-tuple-element.58), channel_id=1, source_target_pairs={{0,128},{16,144},{32,160},{48,176},{64,192},{80,208},{96,224},{112... | collective-permute-start | bytes 1572872 | tf_op jit(solution)/shard_map/ppermute | solution.py:320
  73.1 28.5 %collective-permute-start.18 = (bf16[16,64,128]{2,1,0:T(8,128)(2,1)S(1)}, bf16[16,64,128]{2,1,0:T(8,128)(2,1)S(1)}, u32[]{:S(2)}, u32[]{:S(2)}) collective-permute-start(bf16[16,64,128]{2,1,0:T(8,128)(2,1)S(1)} %get-tuple-element.60), channel_id=1, source_target_pairs={{0,64},{16,80},{32,96},{48,112},{64,0},{80,16},{96,32},{112,48},{1... | collective-permute-start | bytes 786440 | tf_op jit(solution)/shard_map/ppermute | solution.py:280
  79.8 21.9 %collective-permute-start.17 = (bf16[16,64,128]{2,1,0:T(8,128)(2,1)S(1)}, bf16[16,64,128]{2,1,0:T(8,128)(2,1)S(1)}, u32[]{:S(2)}, u32[]{:S(2)}) collective-permute-start(bf16[16,64,128]{2,1,0:T(8,128)(2,1)S(1)} %get-tuple-element.61), channel_id=1, source_target_pairs={{0,96},{16,112},{32,0},{48,16},{64,32},{80,48},{96,64},{112,80},{1... | collective-permute-start | bytes 786440 | tf_op jit(solution)/shard_map/ppermute | solution.py:280
  90.5 11.2 %collective-permute-start.16 = (bf16[16,64,128]{2,1,0:T(8,128)(2,1)S(1)}, bf16[16,64,128]{2,1,0:T(8,128)(2,1)S(1)}, u32[]{:S(2)}, u32[]{:S(2)}) collective-permute-start(bf16[16,64,128]{2,1,0:T(8,128)(2,1)S(1)} %get-tuple-element.62), channel_id=1, source_target_pairs={{0,32},{16,48},{32,64},{48,80},{64,96},{80,112},{96,0},{112,16},{1... | collective-permute-start | bytes 786440 | tf_op jit(solution)/shard_map/ppermute | solution.py:280
  92.3 27.3 %collective-permute-start.14 = (bf16[256,256]{1,0:T(8,128)(2,1)S(1)}, bf16[256,256]{1,0:T(8,128)(2,1)S(1)}, u32[]{:S(2)}, u32[]{:S(2)}) collective-permute-start(bf16[256,256]{1,0:T(8,128)(2,1)S(1)} %get-tuple-element.64), channel_id=1, source_target_pairs={{0,2},{1,3},{2,0},{3,1},{4,6},{5,7},{6,4},{7,5},{8,10},{9,11},{10,... | collective-permute-start | bytes 393224 | tf_op jit(solution)/shard_map/ppermute | solution.py:280
  101.6 18.1 %collective-permute-start.13 = (bf16[256,256]{1,0:T(8,128)(2,1)S(1)}, bf16[256,256]{1,0:T(8,128)(2,1)S(1)}, u32[]{:S(2)}, u32[]{:S(2)}) collective-permute-start(bf16[256,256]{1,0:T(8,128)(2,1)S(1)} %get-tuple-element.65), channel_id=1, source_target_pairs={{0,3},{1,0},{2,1},{3,2},{4,7},{5,4},{6,5},{7,6},{8,11},{9,8},{10,9... | collective-permute-start | bytes 393224 | tf_op jit(solution)/shard_map/ppermute | solution.py:280
  101.8 10.6 %collective-permute-start.20 = (bf16[8,64,128]{2,1,0:T(8,128)(2,1)S(1)}, bf16[8,64,128]{2,1,0:T(8,128)(2,1)S(1)}, u32[]{:S(2)}, u32[]{:S(2)}) collective-permute-start(bf16[8,64,128]{2,1,0:T(8,128)(2,1)S(1)} %add_convert_fusion.10), channel_id=1, source_target_pairs={{0,128},{16,144},{32,160},{48,176},{64,192},{80,208},{96,224},{112... | collective-permute-start | bytes 393224 | tf_op jit(solution)/shard_map/ppermute | solution.py:326
  102.0 10.9 %collective-permute-start.21 = (bf16[8,64,128]{2,1,0:T(8,128)(2,1)S(1)}, bf16[8,64,128]{2,1,0:T(8,128)(2,1)S(1)}, u32[]{:S(2)}, u32[]{:S(2)}) collective-permute-start(bf16[8,64,128]{2,1,0:T(8,128)(2,1)S(1)} %get-tuple-element.68), channel_id=1, source_target_pairs={{0,32},{16,48},{32,64},{48,80},{64,96},{80,112},{96,0},{112,16},{1... | collective-permute-start | bytes 393224 | tf_op jit(solution)/shard_map/ppermute | solution.py:280
  103.4 10.3 %collective-permute-start.23 = (bf16[8,64,128]{2,1,0:T(8,128)(2,1)S(1)}, bf16[8,64,128]{2,1,0:T(8,128)(2,1)S(1)}, u32[]{:S(2)}, u32[]{:S(2)}) collective-permute-start(bf16[8,64,128]{2,1,0:T(8,128)(2,1)S(1)} %get-tuple-element.69), channel_id=1, source_target_pairs={{0,64},{16,80},{32,96},{48,112},{64,0},{80,16},{96,32},{112,48},{1... | collective-permute-start | bytes 393224 | tf_op jit(solution)/shard_map/ppermute | solution.py:280
  112.4 5.0 %collective-permute-start.22 = (bf16[8,64,128]{2,1,0:T(8,128)(2,1)S(1)}, bf16[8,64,128]{2,1,0:T(8,128)(2,1)S(1)}, u32[]{:S(2)}, u32[]{:S(2)}) collective-permute-start(bf16[8,64,128]{2,1,0:T(8,128)(2,1)S(1)} %get-tuple-element.70), channel_id=1, source_target_pairs={{0,96},{16,112},{32,0},{48,16},{64,32},{80,48},{96,64},{112,80},{1... | collective-permute-start | bytes 393224 | tf_op jit(solution)/shard_map/ppermute | solution.py:280
  113.0 7.7 %collective-permute-start.12 = (bf16[256,256]{1,0:T(8,128)(2,1)S(1)}, bf16[256,256]{1,0:T(8,128)(2,1)S(1)}, u32[]{:S(2)}, u32[]{:S(2)}) collective-permute-start(bf16[256,256]{1,0:T(8,128)(2,1)S(1)} %get-tuple-element.66), channel_id=1, source_target_pairs={{0,1},{1,2},{2,3},{3,0},{4,5},{5,6},{6,7},{7,4},{8,9},{9,10},{10,1... | collective-permute-start | bytes 393224 | tf_op jit(solution)/shard_map/ppermute | solution.py:280

commit v6 on v5

--- a/solution.py
+++ b/solution.py
@@ -58,9 +58,13 @@
     low = lax.broadcasted_iota(jnp.int32, (count, 2 * BLK), 1) < BLK
     upper = lax.broadcasted_iota(jnp.int32, (BLK, 2 * BLK), 1) >= BLK
 
-    def place(e, block):
-        here = d_ref.at[(e & (HBL - 1)) >> 1, pl.ds(pl.multiple_of((e >> 4) * BLK, BLK), BLK), :]
-        here[...] = jnp.where(upper == ((e & 1) == 1), block.astype(jnp.bfloat16), here[...])
+    def place(blocks):
+        placed = []
+        for e, block in blocks:
+            here = d_ref.at[(e & (HBL - 1)) >> 1, pl.ds(pl.multiple_of((e >> 4) * BLK, BLK), BLK), :]
+            placed.append((here, jnp.where(upper == ((e & 1) == 1), block.astype(jnp.bfloat16), here[...])))
+        for here, block in placed:
+            here[...] = block
 
     def some(k, carry):
         start = pl.multiple_of(k * at_once, at_once)
@@ -74,14 +78,17 @@
                 even, odd = jnp.where(low, two, swapped), jnp.where(low, swapped, two)
             lines[pl.ds(2 * t, count, stride=BLK), :] = even
             lines[pl.ds(2 * t + 1, count, stride=BLK), :] = odd
-        for u in range(count):
-            block = lines[u * BLK : (u + 1) * BLK, :]
-            if turned:
-                both = jnp.concatenate([block, block], axis=0).T
-                place(dest[start + u], both[:BLK])
-                place(dest[start + u + count], both[BLK:])
-            else:
-                place(dest[start + u], block)
+        for group in range(4):
+            blocks = []
+            for u in range(group // 2 * count // 2 + group % 2, (group // 2 + 1) * count // 2, 2):
+                block = lines[u * BLK : (u + 1) * BLK, :]
+                if turned:
+                    both = jnp.concatenate([block, block], axis=0).T
+                    blocks.append((dest[start + u], both[:BLK]))
+                    blocks.append((dest[start + u + count], both[BLK:]))
+                else:
+                    blocks.append((dest[start + u], block))
+            place(blocks)
         return carry
 
     lax.fori_loop(0, dest.shape[0] // at_once, some, 0)
@@ -137,58 +144,53 @@
 
 
 def grad_kernel(scale, dest, send, first, last, xc_ref, both_ref, own_ref, other_ref, g_scr):
-    j = pl.program_id(0)
     tok = both_ref.shape[1] // 2
     unused = g_scr.shape[0] - 1
     most = 4
-
-    @pl.when(j == 0)
-    def _():
-        g_scr[...] = jnp.zeros_like(g_scr)
-
+    g_scr[...] = jnp.zeros_like(g_scr)
     upper = lax.broadcasted_iota(jnp.int32, (tok, 2 * BLK), 1) >= BLK
-    for q in range(4):
-        begin, end = first[j * 4 + q], last[j * 4 + q]
-        tile = xc_ref[0, :, q // 2 * 2 * BLK : (q // 2 + 1) * 2 * BLK].astype(jnp.float32)
-        x, c = tile[:tok], tile[tok:]
-        if q % 2:
-            c = pltpu.roll(c, BLK, 1)
-        else:
-            x = pltpu.roll(x, BLK, 1)
-        sides = jnp.concatenate([jnp.where(upper, x, 0.0), jnp.where(upper, 0.0, c)], axis=0).astype(jnp.bfloat16)
-        blocks, targets = [], []
-        for u in range(most):
-            s = jnp.minimum(begin + u, unused - 1)
-            at = pl.multiple_of((dest[s] & (HBL - 1)) * BLK, BLK)
-            blocks.append(both_ref[pl.ds(at, BLK), :])
-            targets.append(jnp.where(begin + u < end, send[s], unused))
-        terms = jnp.dot(jnp.concatenate(blocks, axis=0), sides, preferred_element_type=jnp.float32)
-        terms = (terms * scale).astype(jnp.bfloat16)
-        for u in range(most):
-            g_scr[targets[u]] = terms[u * BLK : (u + 1) * BLK]
-
-    @pl.when(j == pl.num_programs(0) - 1)
-    def _():
-        half = own_ref.shape[0]
-        own_ref[...] = g_scr[:half]
-        other_ref[...] = g_scr[half : 2 * half]
+
+    def some(j, carry):
+        for q in range(4):
+            begin, end = first[j * 4 + q], last[j * 4 + q]
+            tile = xc_ref[j, :, q // 2 * 2 * BLK : (q // 2 + 1) * 2 * BLK].astype(jnp.float32)
+            x, c = tile[:tok], tile[tok:]
+            if q % 2:
+                c = pltpu.roll(c, BLK, 1)
+            else:
+                x = pltpu.roll(x, BLK, 1)
+            sides = jnp.concatenate([jnp.where(upper, x, 0.0), jnp.where(upper, 0.0, c)], axis=0).astype(jnp.bfloat16)
+            blocks, targets = [], []
+            for u in range(most):
+                s = jnp.minimum(begin + u, unused - 1)
+                at = pl.multiple_of((dest[s] & (HBL - 1)) * BLK, BLK)
+                blocks.append(both_ref[pl.ds(at, BLK), :])
+                targets.append(jnp.where(begin + u < end, send[s], unused))
+            terms = jnp.dot(jnp.concatenate(blocks, axis=0), sides, preferred_element_type=jnp.float32)
+            terms = (terms * scale).astype(jnp.bfloat16)
+            for u in range(most):
+                g_scr[targets[u]] = terms[u * BLK : (u + 1) * BLK]
+        return carry
+
+    lax.fori_loop(0, xc_ref.shape[0], some, 0)
+    half = own_ref.shape[0]
+    own_ref[...] = g_scr[:half]
+    other_ref[...] = g_scr[half : 2 * half]
 
 
 def grad_stage(tables, xc, both, slot_count, scale):
     tok = both.shape[1] // 2
     cost = pl.CostEstimate(flops=tok * D * 1024, transcendentals=0, bytes_accessed=7 << 20)
     smem = pl.BlockSpec(memory_space=pltpu.SMEM)
+    whole = pl.BlockSpec(memory_space=pltpu.VMEM)
     half = (slot_count // 2, BLK, 2 * BLK)
-    half_spec = pl.BlockSpec(half, lambda j: (0, 0, 0), pipeline_mode=pl.Buffered(1))
     return pl.pallas_call(
         functools.partial(grad_kernel, scale),
-        grid=(16,),
         out_shape=(jax.ShapeDtypeStruct(half, jnp.bfloat16),) * 2,
-        in_specs=[smem] * 4
-        + [pl.BlockSpec((1,) + xc.shape[1:], lambda j: (j, 0, 0)), pl.BlockSpec(both.shape, lambda j: (0, 0))],
-        out_specs=(half_spec, half_spec),
+        in_specs=[smem] * 4 + [whole] * 2,
+        out_specs=(whole, whole),
         scratch_shapes=[pltpu.VMEM((slot_count + 1, BLK, 2 * BLK), jnp.bfloat16)],
-        compiler_params=pltpu.CompilerParams(vmem_limit_bytes=14 * MIB),
+        compiler_params=pltpu.CompilerParams(vmem_limit_bytes=10 * MIB),
         cost_estimate=cost,
         name="grad_stage",
     )(*tables, xc, both)

time: 123 us -> 121 us (0.984)
  Pallas kernels: 35.8 us -> 34 us
    pallas_call x2, Pallas kernels: 18.1 us -> 16.7 us  [dense_weights(): pl.pallas_call(functools.partial(dense_kernel, turned), out_shape=jax.Sha...]
where the time goes in v6:
time: 121 us; the launch traced here: 120 us
  starting transfers between devices  42.5 us (35%)
  Pallas kernels  34 us (28%)
  waiting for transfers between devices  32.8 us (27%)
  local copies, waits for them, and re-layouts  6.62 us (5%)
  other arithmetic  2.74 us (2%)
    ppermute x9, starting transfers between devices, sent(): return [way(block) for way in ways]  20.3 us
    ppermute x9, starting transfers between devices, collect(): return (own, up(after), down(before), over(opposite))  17.4 us
    pallas_call x2, Pallas kernels, dense_weights(): pl.pallas_call(functools.partial(dense_kernel, turned), out_shape=jax.Sha...  16.7 us
    ppermute x2, waiting for transfers between devices, on_device(): across_terms = (own, along_x[0](after), along_x[1](before), from_opposite)  10.2 us
    ppermute x1, waiting for transfers between devices, on_device(): from_deep = deep_way(to_deep)  7.78 us
    pallas_call x1, Pallas kernels, grad_stage(): pl.pallas_call(functools.partial(grad_kernel, scale), out_shape=(jax.Shap...  7.18 us
    ppermute x9, waiting for transfers between devices, sent(): return [way(block) for way in ways]  5.77 us
    pallas_call x2, Pallas kernels, part_stage(): pl.pallas_call(functools.partial(part_kernel, quarter), out_shape=(jax.Sh...  5.65 us
  transfers between devices with their start and end apart: 24, of which 7 were waited for; matrix products, arithmetic and copies ran while one was open for 5% of the time, Pallas kernels for 18%

profile of v6, /device:TPU:8, one launch (start us, length us, event | category | flops | bytes accessed | tf_op | source)
XLA Modules:
  0.0 119.7 jit_solution(513810421695022335)
XLA Ops:
  0.6 0.8 constant_dynamic-update-slice_fusion.1
  1.5 0.8 constant_dynamic-update-slice_fusion
  2.3 3.0 %collective-permute-start.7 = (bf16[256,256]{1,0:T(8,128)(2,1)S(1)}, bf16[256,256]{1,0:T(8,128)(2,1)S(1)}, u32[]{:S(2)}, u32[]{:S(2)}) collective-permute-start(bf16[256,256]{1,0:T(8,128)(2,1)S(1)} %constant_dynamic-update-slice_fusion), channel_id=1, source_target_pairs={{0,8},{1,9},{2,10},{3,11},{4,12},{5,13},{6,14},{7,15},{8,0},{9,1},... | collective-permute-start | bytes 393224 | tf_op jit(solution)/shard_map/ppermute | solution.py:277
  5.3 1.1 collective-permute-start.5
  6.5 7.2 %collective-permute-start.2 = (bf16[256,256]{1,0:T(8,128)(2,1)S(1)}, bf16[256,256]{1,0:T(8,128)(2,1)S(1)}, u32[]{:S(2)}, u32[]{:S(2)}) collective-permute-start(bf16[256,256]{1,0:T(8,128)(2,1)S(1)} %constant_dynamic-update-slice_fusion), channel_id=1, source_target_pairs={{0,2},{1,3},{2,0},{3,1},{4,6},{5,7},{6,4},{7,5},{8,10},{9,11},{10,... | collective-permute-start | bytes 393224 | tf_op jit(solution)/shard_map/ppermute | solution.py:277
  13.7 2.9 %collective-permute-start = (bf16[256,256]{1,0:T(8,128)(2,1)S(1)}, bf16[256,256]{1,0:T(8,128)(2,1)S(1)}, u32[]{:S(2)}, u32[]{:S(2)}) collective-permute-start(bf16[256,256]{1,0:T(8,128)(2,1)S(1)} %constant_dynamic-update-slice_fusion), channel_id=1, source_target_pairs={{0,1},{1,2},{2,3},{3,0},{4,5},{5,6},{6,7},{7,4},{8,9},{9,10},{10,1... | collective-permute-start | bytes 393224 | tf_op jit(solution)/shard_map/ppermute | solution.py:277
  19.1 0.9 collective-permute-start.3
  20.0 5.6 %collective-permute-done.1 = bf16[256,256]{1,0:T(8,128)(2,1)S(1)} collective-permute-done((bf16[256,256]{1,0:T(8,128)(2,1)S(1)}, bf16[256,256]{1,0:T(8,128)(2,1)S(1)}, u32[]{:S(2)}, u32[]{:S(2)}) %collective-permute-start.1) | collective-permute-done | bytes 131104 | tf_op jit(solution)/shard_map/ppermute | solution.py:277
  25.6 1.6 %collective-permute-start.8 = (bf16[3,256,256]{2,1,0:T(8,128)(2,1)S(1)}, bf16[3,256,256]{2,1,0:T(8,128)(2,1)S(1)}, u32[]{:S(2)}, u32[]{:S(2)}) collective-permute-start(bf16[3,256,256]{2,1,0:T(8,128)(2,1)S(1)} %pad_maximum_fusion.1), channel_id=1, source_target_pairs={{0,8},{1,9},{2,10},{3,11},{4,12},{5,13},{6,14},{7,15},{8,0},{9,1},... | collective-permute-start | bytes 1179656 | tf_op jit(solution)/shard_map/ppermute | solution.py:277
  27.3 3.5 %collective-permute-start.6 = (bf16[3,256,256]{2,1,0:T(8,128)(2,1)S(1)}, bf16[3,256,256]{2,1,0:T(8,128)(2,1)S(1)}, u32[]{:S(2)}, u32[]{:S(2)}) collective-permute-start(bf16[3,256,256]{2,1,0:T(8,128)(2,1)S(1)} %pad_maximum_fusion.1), channel_id=1, source_target_pairs={{0,12},{1,13},{2,14},{3,15},{4,0},{5,1},{6,2},{7,3},{8,4},{9,5},{1... | collective-permute-start | bytes 1179656 | tf_op jit(solution)/shard_map/ppermute | solution.py:277
  30.8 1.6 %copy-done = bf16[256,4096]{1,0:T(8,128)(2,1)S(1)} copy-done((bf16[256,4096]{1,0:T(8,128)(2,1)S(1)}, bf16[256,4096]{1,0:T(8,128)(2,1)}, u32[]{:S(2)}) %copy-start) | copy-done | bytes 2097176
  32.4 7.9 %dense_out.1.dout_ref = bf16[8,4160,128]{2,1,0:T(8,128)(2,1)S(1)} custom-call(s32[256]{0:T(256)S(1)} %get-tuple-element.29.dest, bf16[256,4096]{1,0:T(8,128)(2,1)S(1)} %copy-done), custom_call_target="tpu_custom_call" | custom-call | bytes 20971520 | tf_op jit(solution)/shard_map/dense_out/pallas_call | solution.py:99
  40.4 8.8 %dense_in.1.din_ref = bf16[8,4160,128]{2,1,0:T(8,128)(2,1)S(1)} custom-call(s32[256]{0:T(256)S(1)} %get-tuple-element.29.dest, bf16[256,4096]{1,0:T(8,128)(2,1)S(1)} %copy-done.1), custom_call_target="tpu_custom_call" | custom-call | bytes 20971520 | tf_op jit(solution)/shard_map/dense_in/pallas_call | solution.py:99
  49.4 3.6 %hidden_stage.1.both_ref = bf16[1024,256]{1,0:T(8,128)(2,1)S(1)} custom-call(bf16[16,256,256]{2,1,0:T(8,128)(2,1)S(1)} %constant_dynamic-update-slice_fusion.2.xc_ref, bf16[8,4160,128]{2,1,0:T(8,128)(2,1)S(1)} %dense_in.1.din_ref, bf16[8,4160,128]{2,1,0:T(8,128)(2,1)S(1)} %dense_out.1.dout_ref), custom_call_target="tpu_custom_call" | custom-call | flops 2147483648 | bytes 18874368 | tf_op jit(solution)/shard_map/hidden_stage/pallas_call | solution.py:135
  52.9 1.4 %shard_map.84 = bf16[1024,256]{1,0:T(8,128)(2,1)S(1)} custom-call(bf16[8,4160,128]{2,1,0:T(8,128)(2,1)S(1)} %dense_in.1.din_ref, bf16[8,4160,128]{2,1,0:T(8,128)(2,1)S(1)} %dense_out.1.dout_ref, bf16[1024,256]{1,0:T(8,128)(2,1)S(1)} %hidden_stage.1.both_ref), custom_call_target="tpu_custom_call" | custom-call | flops 536870912 | bytes 4718592 | tf_op jit(solution)/shard_map/pallas_call | solution.py:222
  54.4 7.2 %grad_stage.1 = (bf16[128,64,128]{2,1,0:T(8,128)(2,1)S(1)}, bf16[128,64,128]{2,1,0:T(8,128)(2,1)S(1)}) custom-call(s32[256]{0:T(256)S(1)} %get-tuple-element.29.dest, s32[256]{0:T(256)S(1)} %fusion.18.send, s32[64]{0:T(128)S(1)} %get-tuple-element.55.first, s32[64]{0:T(128)S(1)} %get-tuple-element.54.last, ...), custom_call_target="tpu_custom_call" | custom-call | flops 536870912 | bytes 7340032 | tf_op jit(solution)/shard_map/grad_stage/pallas_call | solution.py:187
  61.6 0.9 collective-permute-start.11
  62.5 4.2 %shard_map.85 = (bf16[1024,256]{1,0:T(8,128)(2,1)S(1)}, bf16[1024,256]{1,0:T(8,128)(2,1)S(1)}, bf16[1024,256]{1,0:T(8,128)(2,1)S(1)}) custom-call(bf16[8,4160,128]{2,1,0:T(8,128)(2,1)S(1)} %dense_in.1.din_ref, bf16[8,4160,128]{2,1,0:T(8,128)(2,1)S(1)} %dense_out.1.dout_ref, bf16[1024,256]{1,0:T(8,128)(2,1)S(1)} %hidden_stage.1.both_ref), custom_call_target="tpu_custom_call" | custom-call | flops 1610612736 | bytes 14155776 | tf_op jit(solution)/shard_map/pallas_call | solution.py:222
  66.8 1.0 collective-permute-start.9
  67.7 2.4 %collective-permute-start.10 = (bf16[1024,256]{1,0:T(8,128)(2,1)S(1)}, bf16[1024,256]{1,0:T(8,128)(2,1)S(1)}, u32[]{:S(2)}, u32[]{:S(2)}) collective-permute-start(bf16[1024,256]{1,0:T(8,128)(2,1)S(1)} %get-tuple-element.35), channel_id=1, source_target_pairs={{0,12},{1,13},{2,14},{3,15},{4,0},{5,1},{6,2},{7,3},{8,4},{9,5},{1... | collective-permute-start | bytes 1572872 | tf_op jit(solution)/shard_map/ppermute | solution.py:314
  71.3 2.4 %collective-permute-start.18 = (bf16[16,64,128]{2,1,0:T(8,128)(2,1)S(1)}, bf16[16,64,128]{2,1,0:T(8,128)(2,1)S(1)}, u32[]{:S(2)}, u32[]{:S(2)}) collective-permute-start(bf16[16,64,128]{2,1,0:T(8,128)(2,1)S(1)} %get-tuple-element.60), channel_id=1, source_target_pairs={{0,64},{16,80},{32,96},{48,112},{64,0},{80,16},{96,32},{112,48},{1... | collective-permute-start | bytes 786440 | tf_op jit(solution)/shard_map/ppermute | solution.py:282
  73.7 4.4 %collective-permute-done.11 = bf16[1024,256]{1,0:T(8,128)(2,1)S(1)} collective-permute-done((bf16[1024,256]{1,0:T(8,128)(2,1)S(1)}, bf16[1024,256]{1,0:T(8,128)(2,1)S(1)}, u32[]{:S(2)}, u32[]{:S(2)}) %collective-permute-start.11) | collective-permute-done | bytes 524320 | tf_op jit(solution)/shard_map/ppermute | solution.py:308
  78.5 10.2 %collective-permute-done.9 = bf16[1024,256]{1,0:T(8,128)(2,1)S(1)} collective-permute-done((bf16[1024,256]{1,0:T(8,128)(2,1)S(1)}, bf16[1024,256]{1,0:T(8,128)(2,1)S(1)}, u32[]{:S(2)}, u32[]{:S(2)}) %collective-permute-start.9) | collective-permute-done | bytes 524320 | tf_op jit(solution)/shard_map/ppermute | solution.py:314
  88.7 1.6 %collective-permute-start.16 = (bf16[16,64,128]{2,1,0:T(8,128)(2,1)S(1)}, bf16[16,64,128]{2,1,0:T(8,128)(2,1)S(1)}, u32[]{:S(2)}, u32[]{:S(2)}) collective-permute-start(bf16[16,64,128]{2,1,0:T(8,128)(2,1)S(1)} %get-tuple-element.62), channel_id=1, source_target_pairs={{0,32},{16,48},{32,64},{48,80},{64,96},{80,112},{96,0},{112,16},{1... | collective-permute-start | bytes 786440 | tf_op jit(solution)/shard_map/ppermute | solution.py:282
  90.6 9.2 %collective-permute-start.14 = (bf16[256,256]{1,0:T(8,128)(2,1)S(1)}, bf16[256,256]{1,0:T(8,128)(2,1)S(1)}, u32[]{:S(2)}, u32[]{:S(2)}) collective-permute-start(bf16[256,256]{1,0:T(8,128)(2,1)S(1)} %get-tuple-element.64), channel_id=1, source_target_pairs={{0,2},{1,3},{2,0},{3,1},{4,6},{5,7},{6,4},{7,5},{8,10},{9,11},{10,... | collective-permute-start | bytes 393224 | tf_op jit(solution)/shard_map/ppermute | solution.py:282
  100.3 1.4 %collective-permute-start.21 = (bf16[8,64,128]{2,1,0:T(8,128)(2,1)S(1)}, bf16[8,64,128]{2,1,0:T(8,128)(2,1)S(1)}, u32[]{:S(2)}, u32[]{:S(2)}) collective-permute-start(bf16[8,64,128]{2,1,0:T(8,128)(2,1)S(1)} %get-tuple-element.68), channel_id=1, source_target_pairs={{0,32},{16,48},{32,64},{48,80},{64,96},{80,112},{96,0},{112,16},{1... | collective-permute-start | bytes 393224 | tf_op jit(solution)/shard_map/ppermute | solution.py:282
  101.7 1.2 %collective-permute-start.23 = (bf16[8,64,128]{2,1,0:T(8,128)(2,1)S(1)}, bf16[8,64,128]{2,1,0:T(8,128)(2,1)S(1)}, u32[]{:S(2)}, u32[]{:S(2)}) collective-permute-start(bf16[8,64,128]{2,1,0:T(8,128)(2,1)S(1)} %get-tuple-element.69), channel_id=1, source_target_pairs={{0,64},{16,80},{32,96},{48,112},{64,0},{80,16},{96,32},{112,48},{1... | collective-permute-start | bytes 393224 | tf_op jit(solution)/shard_map/ppermute | solution.py:282
  102.9 7.8 %collective-permute-done.20 = bf16[8,64,128]{2,1,0:T(8,128)(2,1)S(1)} collective-permute-done((bf16[8,64,128]{2,1,0:T(8,128)(2,1)S(1)}, bf16[8,64,128]{2,1,0:T(8,128)(2,1)S(1)}, u32[]{:S(2)}, u32[]{:S(2)}) %collective-permute-start.20) | collective-permute-done | bytes 131104 | tf_op jit(solution)/shard_map/ppermute | solution.py:328
  112.0 3.7 %collective-permute-done.22 = bf16[8,64,128]{2,1,0:T(8,128)(2,1)S(1)} collective-permute-done((bf16[8,64,128]{2,1,0:T(8,128)(2,1)S(1)}, bf16[8,64,128]{2,1,0:T(8,128)(2,1)S(1)}, u32[]{:S(2)}, u32[]{:S(2)}) %collective-permute-start.22) | collective-permute-done | bytes 131104 | tf_op jit(solution)/shard_map/ppermute | solution.py:282
  116.2 0.9 reshape.470
  117.1 0.9 reshape.469
  118.0 1.0 collective-permute-done.12.before_ref
  (67 shorter events, 7.7 us)
Async XLA Ops:
  2.3 47.0 %collective-permute-start.7 = (bf16[256,256]{1,0:T(8,128)(2,1)S(1)}, bf16[256,256]{1,0:T(8,128)(2,1)S(1)}, u32[]{:S(2)}, u32[]{:S(2)}) collective-permute-start(bf16[256,256]{1,0:T(8,128)(2,1)S(1)} %constant_dynamic-update-slice_fusion), channel_id=1, source_target_pairs={{0,8},{1,9},{2,10},{3,11},{4,12},{5,13},{6,14},{7,15},{8,0},{9,1},... | collective-permute-start | bytes 393224 | tf_op jit(solution)/shard_map/ppermute | solution.py:277
  5.3 43.9 %collective-permute-start.5 = (bf16[256,256]{1,0:T(8,128)(2,1)S(1)}, bf16[256,256]{1,0:T(8,128)(2,1)S(1)}, u32[]{:S(2)}, u32[]{:S(2)}) collective-permute-start(bf16[256,256]{1,0:T(8,128)(2,1)S(1)} %constant_dynamic-update-slice_fusion), channel_id=1, source_target_pairs={{0,12},{1,13},{2,14},{3,15},{4,0},{5,1},{6,2},{7,3},{8,4},{9,5},{1... | collective-permute-start | bytes 393224 | tf_op jit(solution)/shard_map/ppermute | solution.py:277
  6.5 12.6 %collective-permute-start.2 = (bf16[256,256]{1,0:T(8,128)(2,1)S(1)}, bf16[256,256]{1,0:T(8,128)(2,1)S(1)}, u32[]{:S(2)}, u32[]{:S(2)}) collective-permute-start(bf16[256,256]{1,0:T(8,128)(2,1)S(1)} %constant_dynamic-update-slice_fusion), channel_id=1, source_target_pairs={{0,2},{1,3},{2,0},{3,1},{4,6},{5,7},{6,4},{7,5},{8,10},{9,11},{10,... | collective-permute-start | bytes 393224 | tf_op jit(solution)/shard_map/ppermute | solution.py:277
  13.7 11.9 %collective-permute-start.1 = (bf16[256,256]{1,0:T(8,128)(2,1)S(1)}, bf16[256,256]{1,0:T(8,128)(2,1)S(1)}, u32[]{:S(2)}, u32[]{:S(2)}) collective-permute-start(bf16[256,256]{1,0:T(8,128)(2,1)S(1)} %constant_dynamic-update-slice_fusion), channel_id=1, source_target_pairs={{0,3},{1,0},{2,1},{3,2},{4,7},{5,4},{6,5},{7,6},{8,11},{9,8},{10,9... | collective-permute-start | bytes 393224 | tf_op jit(solution)/shard_map/ppermute | solution.py:277
  13.7 11.9 %collective-permute-start = (bf16[256,256]{1,0:T(8,128)(2,1)S(1)}, bf16[256,256]{1,0:T(8,128)(2,1)S(1)}, u32[]{:S(2)}, u32[]{:S(2)}) collective-permute-start(bf16[256,256]{1,0:T(8,128)(2,1)S(1)} %constant_dynamic-update-slice_fusion), channel_id=1, source_target_pairs={{0,1},{1,2},{2,3},{3,0},{4,5},{5,6},{6,7},{7,4},{8,9},{9,10},{10,1... | collective-permute-start | bytes 393224 | tf_op jit(solution)/shard_map/ppermute | solution.py:277
  19.1 8.2 %collective-permute-start.3 = (bf16[256,256]{1,0:T(8,128)(2,1)S(1)}, bf16[256,256]{1,0:T(8,128)(2,1)S(1)}, u32[]{:S(2)}, u32[]{:S(2)}) collective-permute-start(bf16[256,256]{1,0:T(8,128)(2,1)S(1)} %constant_dynamic-update-slice_fusion), channel_id=1, source_target_pairs={{0,4},{1,5},{2,6},{3,7},{4,8},{5,9},{6,10},{7,11},{8,12},{9,13},{1... | collective-permute-start | bytes 393224 | tf_op jit(solution)/shard_map/ppermute | solution.py:277
  25.6 23.7 %collective-permute-start.8 = (bf16[3,256,256]{2,1,0:T(8,128)(2,1)S(1)}, bf16[3,256,256]{2,1,0:T(8,128)(2,1)S(1)}, u32[]{:S(2)}, u32[]{:S(2)}) collective-permute-start(bf16[3,256,256]{2,1,0:T(8,128)(2,1)S(1)} %pad_maximum_fusion.1), channel_id=1, source_target_pairs={{0,8},{1,9},{2,10},{3,11},{4,12},{5,13},{6,14},{7,15},{8,0},{9,1},... | collective-permute-start | bytes 1179656 | tf_op jit(solution)/shard_map/ppermute | solution.py:277
  27.3 21.9 %collective-permute-start.4 = (bf16[3,256,256]{2,1,0:T(8,128)(2,1)S(1)}, bf16[3,256,256]{2,1,0:T(8,128)(2,1)S(1)}, u32[]{:S(2)}, u32[]{:S(2)}) collective-permute-start(bf16[3,256,256]{2,1,0:T(8,128)(2,1)S(1)} %pad_maximum_fusion.1), channel_id=1, source_target_pairs={{0,4},{1,5},{2,6},{3,7},{4,8},{5,9},{6,10},{7,11},{8,12},{9,13},{1... | collective-permute-start | bytes 1179656 | tf_op jit(solution)/shard_map/ppermute | solution.py:277
  27.3 21.9 %collective-permute-start.6 = (bf16[3,256,256]{2,1,0:T(8,128)(2,1)S(1)}, bf16[3,256,256]{2,1,0:T(8,128)(2,1)S(1)}, u32[]{:S(2)}, u32[]{:S(2)}) collective-permute-start(bf16[3,256,256]{2,1,0:T(8,128)(2,1)S(1)} %pad_maximum_fusion.1), channel_id=1, source_target_pairs={{0,12},{1,13},{2,14},{3,15},{4,0},{5,1},{6,2},{7,3},{8,4},{9,5},{1... | collective-permute-start | bytes 1179656 | tf_op jit(solution)/shard_map/ppermute | solution.py:277
  30.8 1.6 %copy-start = (bf16[256,4096]{1,0:T(8,128)(2,1)S(1)}, bf16[256,4096]{1,0:T(8,128)(2,1)}, u32[]{:S(2)}) copy-start(bf16[256,4096]{1,0:T(8,128)(2,1)} %w_ref.3) | copy-start | bytes 6291460
  32.4 8.0 %copy-start.1 = (bf16[256,4096]{1,0:T(8,128)(2,1)S(1)}, bf16[256,4096]{1,0:T(8,128)(2,1)}, u32[]{:S(2)}) copy-start(bf16[256,4096]{1,0:T(8,128)(2,1)} %w_ref.2) | copy-start | bytes 6291460
  61.5 8.5 %collective-permute-start.15 = (bf16[128,64,128]{2,1,0:T(8,128)(2,1)S(1)}, bf16[128,64,128]{2,1,0:T(8,128)(2,1)S(1)}, u32[]{:S(2)}, u32[]{:S(2)}) collective-permute-start(bf16[128,64,128]{2,1,0:T(8,128)(2,1)S(1)} %get-tuple-element.40), channel_id=1, source_target_pairs={{0,16},{16,0},{32,48},{48,32},{64,80},{80,64},{96,112},{112,96},{1... | collective-permute-start | bytes 6291464 | tf_op jit(solution)/shard_map/ppermute | solution.py:311
  61.6 16.4 %collective-permute-start.11 = (bf16[1024,256]{1,0:T(8,128)(2,1)S(1)}, bf16[1024,256]{1,0:T(8,128)(2,1)S(1)}, u32[]{:S(2)}, u32[]{:S(2)}) collective-permute-start(bf16[1024,256]{1,0:T(8,128)(2,1)S(1)} %shard_map.84), channel_id=1, source_target_pairs={{0,8},{1,9},{2,10},{3,11},{4,12},{5,13},{6,14},{7,15},{8,0},{9,1},... | collective-permute-start | bytes 1572872 | tf_op jit(solution)/shard_map/ppermute | solution.py:308
  66.8 22.0 %collective-permute-start.9 = (bf16[1024,256]{1,0:T(8,128)(2,1)S(1)}, bf16[1024,256]{1,0:T(8,128)(2,1)S(1)}, u32[]{:S(2)}, u32[]{:S(2)}) collective-permute-start(bf16[1024,256]{1,0:T(8,128)(2,1)S(1)} %get-tuple-element.34), channel_id=1, source_target_pairs={{0,4},{1,5},{2,6},{3,7},{4,8},{5,9},{6,10},{7,11},{8,12},{9,13},{1... | collective-permute-start | bytes 1572872 | tf_op jit(solution)/shard_map/ppermute | solution.py:314
  67.7 22.6 %collective-permute-start.10 = (bf16[1024,256]{1,0:T(8,128)(2,1)S(1)}, bf16[1024,256]{1,0:T(8,128)(2,1)S(1)}, u32[]{:S(2)}, u32[]{:S(2)}) collective-permute-start(bf16[1024,256]{1,0:T(8,128)(2,1)S(1)} %get-tuple-element.35), channel_id=1, source_target_pairs={{0,12},{1,13},{2,14},{3,15},{4,0},{5,1},{6,2},{7,3},{8,4},{9,5},{1... | collective-permute-start | bytes 1572872 | tf_op jit(solution)/shard_map/ppermute | solution.py:314
  70.5 29.5 %collective-permute-start.19 = (bf16[32,64,128]{2,1,0:T(8,128)(2,1)S(1)}, bf16[32,64,128]{2,1,0:T(8,128)(2,1)S(1)}, u32[]{:S(2)}, u32[]{:S(2)}) collective-permute-start(bf16[32,64,128]{2,1,0:T(8,128)(2,1)S(1)} %get-tuple-element.58), channel_id=1, source_target_pairs={{0,128},{16,144},{32,160},{48,176},{64,192},{80,208},{96,224},{112... | collective-permute-start | bytes 1572872 | tf_op jit(solution)/shard_map/ppermute | solution.py:322
  71.3 28.5 %collective-permute-start.18 = (bf16[16,64,128]{2,1,0:T(8,128)(2,1)S(1)}, bf16[16,64,128]{2,1,0:T(8,128)(2,1)S(1)}, u32[]{:S(2)}, u32[]{:S(2)}) collective-permute-start(bf16[16,64,128]{2,1,0:T(8,128)(2,1)S(1)} %get-tuple-element.60), channel_id=1, source_target_pairs={{0,64},{16,80},{32,96},{48,112},{64,0},{80,16},{96,32},{112,48},{1... | collective-permute-start | bytes 786440 | tf_op jit(solution)/shard_map/ppermute | solution.py:282
  78.1 21.9 %collective-permute-start.17 = (bf16[16,64,128]{2,1,0:T(8,128)(2,1)S(1)}, bf16[16,64,128]{2,1,0:T(8,128)(2,1)S(1)}, u32[]{:S(2)}, u32[]{:S(2)}) collective-permute-start(bf16[16,64,128]{2,1,0:T(8,128)(2,1)S(1)} %get-tuple-element.61), channel_id=1, source_target_pairs={{0,96},{16,112},{32,0},{48,16},{64,32},{80,48},{96,64},{112,80},{1... | collective-permute-start | bytes 786440 | tf_op jit(solution)/shard_map/ppermute | solution.py:282
  88.7 11.3 %collective-permute-start.16 = (bf16[16,64,128]{2,1,0:T(8,128)(2,1)S(1)}, bf16[16,64,128]{2,1,0:T(8,128)(2,1)S(1)}, u32[]{:S(2)}, u32[]{:S(2)}) collective-permute-start(bf16[16,64,128]{2,1,0:T(8,128)(2,1)S(1)} %get-tuple-element.62), channel_id=1, source_target_pairs={{0,32},{16,48},{32,64},{48,80},{64,96},{80,112},{96,0},{112,16},{1... | collective-permute-start | bytes 786440 | tf_op jit(solution)/shard_map/ppermute | solution.py:282
  90.6 27.4 %collective-permute-start.14 = (bf16[256,256]{1,0:T(8,128)(2,1)S(1)}, bf16[256,256]{1,0:T(8,128)(2,1)S(1)}, u32[]{:S(2)}, u32[]{:S(2)}) collective-permute-start(bf16[256,256]{1,0:T(8,128)(2,1)S(1)} %get-tuple-element.64), channel_id=1, source_target_pairs={{0,2},{1,3},{2,0},{3,1},{4,6},{5,7},{6,4},{7,5},{8,10},{9,11},{10,... | collective-permute-start | bytes 393224 | tf_op jit(solution)/shard_map/ppermute | solution.py:282
  99.9 18.1 %collective-permute-start.13 = (bf16[256,256]{1,0:T(8,128)(2,1)S(1)}, bf16[256,256]{1,0:T(8,128)(2,1)S(1)}, u32[]{:S(2)}, u32[]{:S(2)}) collective-permute-start(bf16[256,256]{1,0:T(8,128)(2,1)S(1)} %get-tuple-element.65), channel_id=1, source_target_pairs={{0,3},{1,0},{2,1},{3,2},{4,7},{5,4},{6,5},{7,6},{8,11},{9,8},{10,9... | collective-permute-start | bytes 393224 | tf_op jit(solution)/shard_map/ppermute | solution.py:282
  100.1 10.6 %collective-permute-start.20 = (bf16[8,64,128]{2,1,0:T(8,128)(2,1)S(1)}, bf16[8,64,128]{2,1,0:T(8,128)(2,1)S(1)}, u32[]{:S(2)}, u32[]{:S(2)}) collective-permute-start(bf16[8,64,128]{2,1,0:T(8,128)(2,1)S(1)} %add_convert_fusion.10), channel_id=1, source_target_pairs={{0,128},{16,144},{32,160},{48,176},{64,192},{80,208},{96,224},{112... | collective-permute-start | bytes 393224 | tf_op jit(solution)/shard_map/ppermute | solution.py:328
  100.3 10.9 %collective-permute-start.21 = (bf16[8,64,128]{2,1,0:T(8,128)(2,1)S(1)}, bf16[8,64,128]{2,1,0:T(8,128)(2,1)S(1)}, u32[]{:S(2)}, u32[]{:S(2)}) collective-permute-start(bf16[8,64,128]{2,1,0:T(8,128)(2,1)S(1)} %get-tuple-element.68), channel_id=1, source_target_pairs={{0,32},{16,48},{32,64},{48,80},{64,96},{80,112},{96,0},{112,16},{1... | collective-permute-start | bytes 393224 | tf_op jit(solution)/shard_map/ppermute | solution.py:282
  101.7 10.3 %collective-permute-start.23 = (bf16[8,64,128]{2,1,0:T(8,128)(2,1)S(1)}, bf16[8,64,128]{2,1,0:T(8,128)(2,1)S(1)}, u32[]{:S(2)}, u32[]{:S(2)}) collective-permute-start(bf16[8,64,128]{2,1,0:T(8,128)(2,1)S(1)} %get-tuple-element.69), channel_id=1, source_target_pairs={{0,64},{16,80},{32,96},{48,112},{64,0},{80,16},{96,32},{112,48},{1... | collective-permute-start | bytes 393224 | tf_op jit(solution)/shard_map/ppermute | solution.py:282
  110.7 5.0 %collective-permute-start.22 = (bf16[8,64,128]{2,1,0:T(8,128)(2,1)S(1)}, bf16[8,64,128]{2,1,0:T(8,128)(2,1)S(1)}, u32[]{:S(2)}, u32[]{:S(2)}) collective-permute-start(bf16[8,64,128]{2,1,0:T(8,128)(2,1)S(1)} %get-tuple-element.70), channel_id=1, source_target_pairs={{0,96},{16,112},{32,0},{48,16},{64,32},{80,48},{96,64},{112,80},{1... | collective-permute-start | bytes 393224 | tf_op jit(solution)/shard_map/ppermute | solution.py:282
  111.2 7.7 %collective-permute-start.12 = (bf16[256,256]{1,0:T(8,128)(2,1)S(1)}, bf16[256,256]{1,0:T(8,128)(2,1)S(1)}, u32[]{:S(2)}, u32[]{:S(2)}) collective-permute-start(bf16[256,256]{1,0:T(8,128)(2,1)S(1)} %get-tuple-element.66), channel_id=1, source_target_pairs={{0,1},{1,2},{2,3},{3,0},{4,5},{5,6},{6,7},{7,4},{8,9},{9,10},{10,1... | collective-permute-start | bytes 393224 | tf_op jit(solution)/shard_map/ppermute | solution.py:282

commit v7 on v6

--- a/solution.py
+++ b/solution.py
@@ -51,8 +51,10 @@
     return dest, send, first, last
 
 
-def dense_kernel(turned, dest, w_ref, d_ref, lines):
-    d_ref[...] = jnp.zeros_like(d_ref)
+def dense_kernel(turned, dest, w_ref, *refs):
+    d_ref, lines = refs[-2:]
+    if len(refs) == 2:
+        d_ref[...] = jnp.zeros_like(d_ref)
     at_once = 16
     count = at_once // 2 if turned else at_once
     low = lax.broadcasted_iota(jnp.int32, (count, 2 * BLK), 1) < BLK
@@ -94,18 +96,19 @@
     lax.fori_loop(0, dest.shape[0] // at_once, some, 0)
 
 
-def dense_weights(dest, weights, turned):
+def dense_weights(dest, weights, turned, *empty):
     whole = pl.BlockSpec(memory_space=pltpu.VMEM)
     return pl.pallas_call(
         functools.partial(dense_kernel, turned),
         out_shape=jax.ShapeDtypeStruct((8, D + BLK, 2 * BLK), jnp.bfloat16),
-        in_specs=[pl.BlockSpec(memory_space=pltpu.SMEM), whole],
+        in_specs=[pl.BlockSpec(memory_space=pltpu.SMEM), whole] + [whole] * len(empty),
         out_specs=whole,
+        input_output_aliases={2: 0} if empty else {},
         scratch_shapes=[pltpu.VMEM((16 * BLK, 2 * BLK), jnp.float32)],
         compiler_params=pltpu.CompilerParams(vmem_limit_bytes=14 * MIB),
         cost_estimate=pl.CostEstimate(flops=0, transcendentals=0, bytes_accessed=20 << 20),
         name="dense_out" if turned else "dense_in",
-    )(dest, weights)
+    )(dest, weights, *empty)
 
 
 def hidden_kernel(xc_ref, din_ref, dout_ref, both_ref):
@@ -300,8 +303,9 @@
     pieces = [(own[None], others) for own, others in zip([block] + wide_own, [near] + wide)]
     xc = jnp.concatenate([piece for both in pieces for piece in both])
     dest, _ = lax.optimization_barrier((tables[0], near))
+    empty = jnp.zeros((8, D + BLK, 2 * BLK), jnp.bfloat16)
     din = dense_weights(dest, in_weights, False)
-    dout = dense_weights(dest, out_weights, True)
+    dout = dense_weights(dest, out_weights, True, empty)
     both = hidden_stage(xc, din, dout, tok)
     (opposite,) = part_stage(din, dout, both, 3, 1)
     opposite, both = lax.optimization_barrier((opposite, both))

time: 121 us -> 123 us (1.017)
  waiting for transfers between devices: 32.8 us -> 22.5 us
  starting transfers between devices: 42.5 us -> 51.6 us
  local copies, waits for them, and re-layouts: 6.62 us -> 9.3 us
    ppermute x1, waiting for transfers between devices: 7.78 us -> 1.09 us  [on_device(): from_deep = deep_way(to_deep)]
    ppermute x2, waiting for transfers between devices: 10.2 us -> 16.2 us  [on_device(): across_terms = (own, along_x[0](after), along_x[1](before), from_opposite)]
    ppermute x9, waiting for transfers between devices: 5.77 us -> 0.02 us  [sent(): return [way(block) for way in ways]]
    ppermute x1, starting transfers between devices: 0.09 us -> 4.79 us  [on_device(): from_deep = deep_way(to_deep)]
    ppermute x1, waiting for transfers between devices: 4.35 us -> 0.01 us  [on_device(): from_opposite = along_x[2](opposite)]
    ppermute x1, starting transfers between devices: 0.46 us -> 4.38 us  [on_device(): late_deep = deep_way(late_other)]
    unnamed x15, local copies, waits for them, and re-layouts: 3.36 us -> 4.95 us
    ppermute x9, starting transfers between devices: 20.3 us -> 21.5 us  [sent(): return [way(block) for way in ways]]
  transfers between devices with their start and end apart: 24 -> 24, of which waited for: 7 -> 6; matrix products, arithmetic and copies ran while one was open for 5% -> 6% of each run, Pallas kernels for 18% -> 17%
where the time goes in v7:
time: 123 us; the launch traced here: 121 us
  starting transfers between devices  51.6 us (42%)
  Pallas kernels  33.5 us (27%)
  waiting for transfers between devices  22.5 us (18%)
  local copies, waits for them, and re-layouts  9.3 us (8%)
  other arithmetic  2.81 us (2%)
    ppermute x9, starting transfers between devices, sent(): return [way(block) for way in ways]  21.5 us
    ppermute x9, starting transfers between devices, collect(): return (own, up(after), down(before), over(opposite))  16.7 us
    ppermute x2, waiting for transfers between devices, on_device(): across_terms = (own, along_x[0](after), along_x[1](before), from_opposite)  16.2 us
    pallas_call x2, Pallas kernels, dense_weights(): pl.pallas_call(functools.partial(dense_kernel, turned), out_shape=jax.Sha...  15.7 us
    pallas_call x1, Pallas kernels, grad_stage(): pl.pallas_call(functools.partial(grad_kernel, scale), out_shape=(jax.Shap...  7.21 us
    pallas_call x2, Pallas kernels, part_stage(): pl.pallas_call(functools.partial(part_kernel, quarter), out_shape=(jax.Sh...  5.65 us
    ppermute x9, waiting for transfers between devices, collect(): return (own, up(after), down(before), over(opposite))  5.16 us
    unnamed x15, local copies, waits for them, and re-layouts  4.95 us
  transfers between devices with their start and end apart: 24, of which 6 were waited for; matrix products, arithmetic and copies ran while one was open for 6% of the time, Pallas kernels for 17%

profile of v7, /device:TPU:8, one launch (start us, length us, event | category | flops | bytes accessed | tf_op | source)
XLA Modules:
  0.0 120.7 jit_solution(5150824562551406545)
XLA Ops:
  2.3 3.3 %collective-permute-start = (bf16[256,256]{1,0:T(8,128)(2,1)S(1)}, bf16[256,256]{1,0:T(8,128)(2,1)S(1)}, u32[]{:S(2)}, u32[]{:S(2)}) collective-permute-start(bf16[256,256]{1,0:T(8,128)(2,1)S(1)} %constant_dynamic-update-slice_fusion), channel_id=1, source_target_pairs={{0,1},{1,2},{2,3},{3,0},{4,5},{5,6},{6,7},{7,4},{8,9},{9,10},{10,1... | collective-permute-start | bytes 393224 | tf_op jit(solution)/shard_map/ppermute | solution.py:280
  5.6 3.0 %collective-permute-start.1 = (bf16[256,256]{1,0:T(8,128)(2,1)S(1)}, bf16[256,256]{1,0:T(8,128)(2,1)S(1)}, u32[]{:S(2)}, u32[]{:S(2)}) collective-permute-start(bf16[256,256]{1,0:T(8,128)(2,1)S(1)} %constant_dynamic-update-slice_fusion), channel_id=1, source_target_pairs={{0,3},{1,0},{2,1},{3,2},{4,7},{5,4},{6,5},{7,6},{8,11},{9,8},{10,9... | collective-permute-start | bytes 393224 | tf_op jit(solution)/shard_map/ppermute | solution.py:280
  8.6 5.0 %collective-permute-start.2 = (bf16[256,256]{1,0:T(8,128)(2,1)S(1)}, bf16[256,256]{1,0:T(8,128)(2,1)S(1)}, u32[]{:S(2)}, u32[]{:S(2)}) collective-permute-start(bf16[256,256]{1,0:T(8,128)(2,1)S(1)} %constant_dynamic-update-slice_fusion), channel_id=1, source_target_pairs={{0,2},{1,3},{2,0},{3,1},{4,6},{5,7},{6,4},{7,5},{8,10},{9,11},{10,... | collective-permute-start | bytes 393224 | tf_op jit(solution)/shard_map/ppermute | solution.py:280
  13.6 1.5 %collective-permute-start.3 = (bf16[256,256]{1,0:T(8,128)(2,1)S(1)}, bf16[256,256]{1,0:T(8,128)(2,1)S(1)}, u32[]{:S(2)}, u32[]{:S(2)}) collective-permute-start(bf16[256,256]{1,0:T(8,128)(2,1)S(1)} %constant_dynamic-update-slice_fusion), channel_id=1, source_target_pairs={{0,4},{1,5},{2,6},{3,7},{4,8},{5,9},{6,10},{7,11},{8,12},{9,13},{1... | collective-permute-start | bytes 393224 | tf_op jit(solution)/shard_map/ppermute | solution.py:280
  15.1 1.7 %collective-permute-start.5 = (bf16[256,256]{1,0:T(8,128)(2,1)S(1)}, bf16[256,256]{1,0:T(8,128)(2,1)S(1)}, u32[]{:S(2)}, u32[]{:S(2)}) collective-permute-start(bf16[256,256]{1,0:T(8,128)(2,1)S(1)} %constant_dynamic-update-slice_fusion), channel_id=1, source_target_pairs={{0,12},{1,13},{2,14},{3,15},{4,0},{5,1},{6,2},{7,3},{8,4},{9,5},{1... | collective-permute-start | bytes 393224 | tf_op jit(solution)/shard_map/ppermute | solution.py:280
  19.3 1.9 %collective-permute-start.7 = (bf16[256,256]{1,0:T(8,128)(2,1)S(1)}, bf16[256,256]{1,0:T(8,128)(2,1)S(1)}, u32[]{:S(2)}, u32[]{:S(2)}) collective-permute-start(bf16[256,256]{1,0:T(8,128)(2,1)S(1)} %constant_dynamic-update-slice_fusion), channel_id=1, source_target_pairs={{0,8},{1,9},{2,10},{3,11},{4,12},{5,13},{6,14},{7,15},{8,0},{9,1},... | collective-permute-start | bytes 393224 | tf_op jit(solution)/shard_map/ppermute | solution.py:280
  21.2 1.2 %collective-permute-start.4 = (bf16[3,256,256]{2,1,0:T(8,128)(2,1)S(1)}, bf16[3,256,256]{2,1,0:T(8,128)(2,1)S(1)}, u32[]{:S(2)}, u32[]{:S(2)}) collective-permute-start(bf16[3,256,256]{2,1,0:T(8,128)(2,1)S(1)} %pad_maximum_fusion.1), channel_id=1, source_target_pairs={{0,4},{1,5},{2,6},{3,7},{4,8},{5,9},{6,10},{7,11},{8,12},{9,13},{1... | collective-permute-start | bytes 1179656 | tf_op jit(solution)/shard_map/ppermute | solution.py:280
  22.4 2.1 %collective-permute-start.6 = (bf16[3,256,256]{2,1,0:T(8,128)(2,1)S(1)}, bf16[3,256,256]{2,1,0:T(8,128)(2,1)S(1)}, u32[]{:S(2)}, u32[]{:S(2)}) collective-permute-start(bf16[3,256,256]{2,1,0:T(8,128)(2,1)S(1)} %pad_maximum_fusion.1), channel_id=1, source_target_pairs={{0,12},{1,13},{2,14},{3,15},{4,0},{5,1},{6,2},{7,3},{8,4},{9,5},{1... | collective-permute-start | bytes 1179656 | tf_op jit(solution)/shard_map/ppermute | solution.py:280
  24.6 1.7 %collective-permute-start.8 = (bf16[3,256,256]{2,1,0:T(8,128)(2,1)S(1)}, bf16[3,256,256]{2,1,0:T(8,128)(2,1)S(1)}, u32[]{:S(2)}, u32[]{:S(2)}) collective-permute-start(bf16[3,256,256]{2,1,0:T(8,128)(2,1)S(1)} %pad_maximum_fusion.1), channel_id=1, source_target_pairs={{0,8},{1,9},{2,10},{3,11},{4,12},{5,13},{6,14},{7,15},{8,0},{9,1},... | collective-permute-start | bytes 1179656 | tf_op jit(solution)/shard_map/ppermute | solution.py:280
  26.4 1.6 %copy-done.1 = bf16[256,4096]{1,0:T(8,128)(2,1)S(1)} copy-done((bf16[256,4096]{1,0:T(8,128)(2,1)S(1)}, bf16[256,4096]{1,0:T(8,128)(2,1)}, u32[]{:S(2)}) %copy-start.1) | copy-done | bytes 2097176
  27.9 8.9 %dense_in.1.din_ref = bf16[8,4160,128]{2,1,0:T(8,128)(2,1)S(1)} custom-call(s32[256]{0:T(256)S(1)} %get-tuple-element.29.dest, bf16[256,4096]{1,0:T(8,128)(2,1)S(1)} %copy-done.1), custom_call_target="tpu_custom_call" | custom-call | bytes 20971520 | tf_op jit(solution)/shard_map/dense_in/pallas_call | solution.py:101
  36.8 1.1 broadcast_in_dim.73.refs_0_
  37.9 1.6 %copy-done = bf16[256,4096]{1,0:T(8,128)(2,1)S(1)} copy-done((bf16[256,4096]{1,0:T(8,128)(2,1)S(1)}, bf16[256,4096]{1,0:T(8,128)(2,1)}, u32[]{:S(2)}) %copy-start) | copy-done | bytes 2097176
  39.5 6.9 %dense_out.1.dout_ref = bf16[8,4160,128]{2,1,0:T(8,128)(2,1)S(1)} custom-call(s32[256]{0:T(256)S(1)} %get-tuple-element.29.dest, bf16[256,4096]{1,0:T(8,128)(2,1)S(1)} %copy-done, bf16[8,4160,128]{2,1,0:T(8,128)(2,1)S(1)} %broadcast_in_dim.73.refs_0_), custom_call_target="tpu_custom_call", output_to_operand_aliasing={{}: (2, {})} | custom-call | bytes 20971520 | tf_op jit(solution)/shard_map/dense_out/pallas_call | solution.py:101
  46.6 4.0 %hidden_stage.1.both_ref = bf16[1024,256]{1,0:T(8,128)(2,1)S(1)} custom-call(bf16[16,256,256]{2,1,0:T(8,128)(2,1)S(1)} %constant_dynamic-update-slice_fusion.2.xc_ref, bf16[8,4160,128]{2,1,0:T(8,128)(2,1)S(1)} %dense_in.1.din_ref, bf16[8,4160,128]{2,1,0:T(8,128)(2,1)S(1)} %dense_out.1.dout_ref), custom_call_target="tpu_custom_call" | custom-call | flops 2147483648 | bytes 18874368 | tf_op jit(solution)/shard_map/hidden_stage/pallas_call | solution.py:138
  50.6 1.4 %shard_map.84 = bf16[1024,256]{1,0:T(8,128)(2,1)S(1)} custom-call(bf16[8,4160,128]{2,1,0:T(8,128)(2,1)S(1)} %dense_in.1.din_ref, bf16[8,4160,128]{2,1,0:T(8,128)(2,1)S(1)} %dense_out.1.dout_ref, bf16[1024,256]{1,0:T(8,128)(2,1)S(1)} %hidden_stage.1.both_ref), custom_call_target="tpu_custom_call" | custom-call | flops 536870912 | bytes 4718592 | tf_op jit(solution)/shard_map/pallas_call | solution.py:225
  52.0 7.2 %grad_stage.1 = (bf16[128,64,128]{2,1,0:T(8,128)(2,1)S(1)}, bf16[128,64,128]{2,1,0:T(8,128)(2,1)S(1)}) custom-call(s32[256]{0:T(256)S(1)} %get-tuple-element.29.dest, s32[256]{0:T(256)S(1)} %fusion.18.send, s32[64]{0:T(128)S(1)} %get-tuple-element.55.first, s32[64]{0:T(128)S(1)} %get-tuple-element.54.last, ...), custom_call_target="tpu_custom_call" | custom-call | flops 536870912 | bytes 7340032 | tf_op jit(solution)/shard_map/grad_stage/pallas_call | solution.py:190
  59.3 4.2 %shard_map.85 = (bf16[1024,256]{1,0:T(8,128)(2,1)S(1)}, bf16[1024,256]{1,0:T(8,128)(2,1)S(1)}, bf16[1024,256]{1,0:T(8,128)(2,1)S(1)}) custom-call(bf16[8,4160,128]{2,1,0:T(8,128)(2,1)S(1)} %dense_in.1.din_ref, bf16[8,4160,128]{2,1,0:T(8,128)(2,1)S(1)} %dense_out.1.dout_ref, bf16[1024,256]{1,0:T(8,128)(2,1)S(1)} %hidden_stage.1.both_ref), custom_call_target="tpu_custom_call" | custom-call | flops 1610612736 | bytes 14155776 | tf_op jit(solution)/shard_map/pallas_call | solution.py:225
  63.6 1.2 collective-permute-start.10
  65.7 2.0 %collective-permute-start.11 = (bf16[1024,256]{1,0:T(8,128)(2,1)S(1)}, bf16[1024,256]{1,0:T(8,128)(2,1)S(1)}, u32[]{:S(2)}, u32[]{:S(2)}) collective-permute-start(bf16[1024,256]{1,0:T(8,128)(2,1)S(1)} %shard_map.84), channel_id=1, source_target_pairs={{0,8},{1,9},{2,10},{3,11},{4,12},{5,13},{6,14},{7,15},{8,0},{9,1},... | collective-permute-start | bytes 1572872 | tf_op jit(solution)/shard_map/ppermute | solution.py:312
  68.2 4.4 %collective-permute-start.19 = (bf16[32,64,128]{2,1,0:T(8,128)(2,1)S(1)}, bf16[32,64,128]{2,1,0:T(8,128)(2,1)S(1)}, u32[]{:S(2)}, u32[]{:S(2)}) collective-permute-start(bf16[32,64,128]{2,1,0:T(8,128)(2,1)S(1)} %get-tuple-element.58), channel_id=1, source_target_pairs={{0,128},{16,144},{32,160},{48,176},{64,192},{80,208},{96,224},{112... | collective-permute-start | bytes 1572872 | tf_op jit(solution)/shard_map/ppermute | solution.py:326
  73.0 1.7 %collective-permute-start.16 = (bf16[16,64,128]{2,1,0:T(8,128)(2,1)S(1)}, bf16[16,64,128]{2,1,0:T(8,128)(2,1)S(1)}, u32[]{:S(2)}, u32[]{:S(2)}) collective-permute-start(bf16[16,64,128]{2,1,0:T(8,128)(2,1)S(1)} %get-tuple-element.62), channel_id=1, source_target_pairs={{0,32},{16,48},{32,64},{48,80},{64,96},{80,112},{96,0},{112,16},{1... | collective-permute-start | bytes 786440 | tf_op jit(solution)/shard_map/ppermute | solution.py:285
  74.6 3.8 %collective-permute-done.10 = bf16[1024,256]{1,0:T(8,128)(2,1)S(1)} collective-permute-done((bf16[1024,256]{1,0:T(8,128)(2,1)S(1)}, bf16[1024,256]{1,0:T(8,128)(2,1)S(1)}, u32[]{:S(2)}, u32[]{:S(2)}) %collective-permute-start.10) | collective-permute-done | bytes 524320 | tf_op jit(solution)/shard_map/ppermute | solution.py:318
  78.9 12.4 %collective-permute-done.9 = bf16[1024,256]{1,0:T(8,128)(2,1)S(1)} collective-permute-done((bf16[1024,256]{1,0:T(8,128)(2,1)S(1)}, bf16[1024,256]{1,0:T(8,128)(2,1)S(1)}, u32[]{:S(2)}, u32[]{:S(2)}) %collective-permute-start.9) | collective-permute-done | bytes 524320 | tf_op jit(solution)/shard_map/ppermute | solution.py:318
  91.3 2.3 %collective-permute-start.18 = (bf16[16,64,128]{2,1,0:T(8,128)(2,1)S(1)}, bf16[16,64,128]{2,1,0:T(8,128)(2,1)S(1)}, u32[]{:S(2)}, u32[]{:S(2)}) collective-permute-start(bf16[16,64,128]{2,1,0:T(8,128)(2,1)S(1)} %get-tuple-element.60), channel_id=1, source_target_pairs={{0,64},{16,80},{32,96},{48,112},{64,0},{80,16},{96,32},{112,48},{1... | collective-permute-start | bytes 786440 | tf_op jit(solution)/shard_map/ppermute | solution.py:285
  93.8 4.8 %collective-permute-start.12 = (bf16[256,256]{1,0:T(8,128)(2,1)S(1)}, bf16[256,256]{1,0:T(8,128)(2,1)S(1)}, u32[]{:S(2)}, u32[]{:S(2)}) collective-permute-start(bf16[256,256]{1,0:T(8,128)(2,1)S(1)} %get-tuple-element.66), channel_id=1, source_target_pairs={{0,1},{1,2},{2,3},{3,0},{4,5},{5,6},{6,7},{7,4},{8,9},{9,10},{10,1... | collective-permute-start | bytes 393224 | tf_op jit(solution)/shard_map/ppermute | solution.py:285
  99.2 4.8 %collective-permute-start.20 = (bf16[8,64,128]{2,1,0:T(8,128)(2,1)S(1)}, bf16[8,64,128]{2,1,0:T(8,128)(2,1)S(1)}, u32[]{:S(2)}, u32[]{:S(2)}) collective-permute-start(bf16[8,64,128]{2,1,0:T(8,128)(2,1)S(1)} %add_convert_fusion.10), channel_id=1, source_target_pairs={{0,128},{16,144},{32,160},{48,176},{64,192},{80,208},{96,224},{112... | collective-permute-start | bytes 393224 | tf_op jit(solution)/shard_map/ppermute | solution.py:332
  104.2 3.0 %collective-permute-start.21 = (bf16[8,64,128]{2,1,0:T(8,128)(2,1)S(1)}, bf16[8,64,128]{2,1,0:T(8,128)(2,1)S(1)}, u32[]{:S(2)}, u32[]{:S(2)}) collective-permute-start(bf16[8,64,128]{2,1,0:T(8,128)(2,1)S(1)} %get-tuple-element.68), channel_id=1, source_target_pairs={{0,32},{16,48},{32,64},{48,80},{64,96},{80,112},{96,0},{112,16},{1... | collective-permute-start | bytes 393224 | tf_op jit(solution)/shard_map/ppermute | solution.py:285
  108.3 2.2 %collective-permute-start.23 = (bf16[8,64,128]{2,1,0:T(8,128)(2,1)S(1)}, bf16[8,64,128]{2,1,0:T(8,128)(2,1)S(1)}, u32[]{:S(2)}, u32[]{:S(2)}) collective-permute-start(bf16[8,64,128]{2,1,0:T(8,128)(2,1)S(1)} %get-tuple-element.69), channel_id=1, source_target_pairs={{0,64},{16,80},{32,96},{48,112},{64,0},{80,16},{96,32},{112,48},{1... | collective-permute-start | bytes 393224 | tf_op jit(solution)/shard_map/ppermute | solution.py:285
  110.6 2.2 %collective-permute-start.14 = (bf16[256,256]{1,0:T(8,128)(2,1)S(1)}, bf16[256,256]{1,0:T(8,128)(2,1)S(1)}, u32[]{:S(2)}, u32[]{:S(2)}) collective-permute-start(bf16[256,256]{1,0:T(8,128)(2,1)S(1)} %get-tuple-element.64), channel_id=1, source_target_pairs={{0,2},{1,3},{2,0},{3,1},{4,6},{5,7},{6,4},{7,5},{8,10},{9,11},{10,... | collective-permute-start | bytes 393224 | tf_op jit(solution)/shard_map/ppermute | solution.py:285
  112.8 2.0 %collective-permute-done.23 = bf16[8,64,128]{2,1,0:T(8,128)(2,1)S(1)} collective-permute-done((bf16[8,64,128]{2,1,0:T(8,128)(2,1)S(1)}, bf16[8,64,128]{2,1,0:T(8,128)(2,1)S(1)}, u32[]{:S(2)}, u32[]{:S(2)}) %collective-permute-start.23) | collective-permute-done | bytes 131104 | tf_op jit(solution)/shard_map/ppermute | solution.py:285
  117.1 2.9 %collective-permute-done.14.opposite_ref = bf16[256,256]{1,0:T(8,128)(2,1)S(1)} collective-permute-done((bf16[256,256]{1,0:T(8,128)(2,1)S(1)}, bf16[256,256]{1,0:T(8,128)(2,1)S(1)}, u32[]{:S(2)}, u32[]{:S(2)}) %collective-permute-start.14) | collective-permute-done | bytes 131104 | tf_op jit(solution)/shard_map/ppermute | solution.py:285
  (68 shorter events, 11.7 us)
Async XLA Ops:
  2.3 16.9 %collective-permute-start = (bf16[256,256]{1,0:T(8,128)(2,1)S(1)}, bf16[256,256]{1,0:T(8,128)(2,1)S(1)}, u32[]{:S(2)}, u32[]{:S(2)}) collective-permute-start(bf16[256,256]{1,0:T(8,128)(2,1)S(1)} %constant_dynamic-update-slice_fusion), channel_id=1, source_target_pairs={{0,1},{1,2},{2,3},{3,0},{4,5},{5,6},{6,7},{7,4},{8,9},{9,10},{10,1... | collective-permute-start | bytes 393224 | tf_op jit(solution)/shard_map/ppermute | solution.py:280
  5.6 15.6 %collective-permute-start.1 = (bf16[256,256]{1,0:T(8,128)(2,1)S(1)}, bf16[256,256]{1,0:T(8,128)(2,1)S(1)}, u32[]{:S(2)}, u32[]{:S(2)}) collective-permute-start(bf16[256,256]{1,0:T(8,128)(2,1)S(1)} %constant_dynamic-update-slice_fusion), channel_id=1, source_target_pairs={{0,3},{1,0},{2,1},{3,2},{4,7},{5,4},{6,5},{7,6},{8,11},{9,8},{10,9... | collective-permute-start | bytes 393224 | tf_op jit(solution)/shard_map/ppermute | solution.py:280
  8.6 12.6 %collective-permute-start.2 = (bf16[256,256]{1,0:T(8,128)(2,1)S(1)}, bf16[256,256]{1,0:T(8,128)(2,1)S(1)}, u32[]{:S(2)}, u32[]{:S(2)}) collective-permute-start(bf16[256,256]{1,0:T(8,128)(2,1)S(1)} %constant_dynamic-update-slice_fusion), channel_id=1, source_target_pairs={{0,2},{1,3},{2,0},{3,1},{4,6},{5,7},{6,4},{7,5},{8,10},{9,11},{10,... | collective-permute-start | bytes 393224 | tf_op jit(solution)/shard_map/ppermute | solution.py:280
  13.6 11.0 %collective-permute-start.3 = (bf16[256,256]{1,0:T(8,128)(2,1)S(1)}, bf16[256,256]{1,0:T(8,128)(2,1)S(1)}, u32[]{:S(2)}, u32[]{:S(2)}) collective-permute-start(bf16[256,256]{1,0:T(8,128)(2,1)S(1)} %constant_dynamic-update-slice_fusion), channel_id=1, source_target_pairs={{0,4},{1,5},{2,6},{3,7},{4,8},{5,9},{6,10},{7,11},{8,12},{9,13},{1... | collective-permute-start | bytes 393224 | tf_op jit(solution)/shard_map/ppermute | solution.py:280
  15.1 31.3 %collective-permute-start.5 = (bf16[256,256]{1,0:T(8,128)(2,1)S(1)}, bf16[256,256]{1,0:T(8,128)(2,1)S(1)}, u32[]{:S(2)}, u32[]{:S(2)}) collective-permute-start(bf16[256,256]{1,0:T(8,128)(2,1)S(1)} %constant_dynamic-update-slice_fusion), channel_id=1, source_target_pairs={{0,12},{1,13},{2,14},{3,15},{4,0},{5,1},{6,2},{7,3},{8,4},{9,5},{1... | collective-permute-start | bytes 393224 | tf_op jit(solution)/shard_map/ppermute | solution.py:280
  19.3 27.2 %collective-permute-start.7 = (bf16[256,256]{1,0:T(8,128)(2,1)S(1)}, bf16[256,256]{1,0:T(8,128)(2,1)S(1)}, u32[]{:S(2)}, u32[]{:S(2)}) collective-permute-start(bf16[256,256]{1,0:T(8,128)(2,1)S(1)} %constant_dynamic-update-slice_fusion), channel_id=1, source_target_pairs={{0,8},{1,9},{2,10},{3,11},{4,12},{5,13},{6,14},{7,15},{8,0},{9,1},... | collective-permute-start | bytes 393224 | tf_op jit(solution)/shard_map/ppermute | solution.py:280
  21.2 25.2 %collective-permute-start.4 = (bf16[3,256,256]{2,1,0:T(8,128)(2,1)S(1)}, bf16[3,256,256]{2,1,0:T(8,128)(2,1)S(1)}, u32[]{:S(2)}, u32[]{:S(2)}) collective-permute-start(bf16[3,256,256]{2,1,0:T(8,128)(2,1)S(1)} %pad_maximum_fusion.1), channel_id=1, source_target_pairs={{0,4},{1,5},{2,6},{3,7},{4,8},{5,9},{6,10},{7,11},{8,12},{9,13},{1... | collective-permute-start | bytes 1179656 | tf_op jit(solution)/shard_map/ppermute | solution.py:280
  22.4 24.0 %collective-permute-start.6 = (bf16[3,256,256]{2,1,0:T(8,128)(2,1)S(1)}, bf16[3,256,256]{2,1,0:T(8,128)(2,1)S(1)}, u32[]{:S(2)}, u32[]{:S(2)}) collective-permute-start(bf16[3,256,256]{2,1,0:T(8,128)(2,1)S(1)} %pad_maximum_fusion.1), channel_id=1, source_target_pairs={{0,12},{1,13},{2,14},{3,15},{4,0},{5,1},{6,2},{7,3},{8,4},{9,5},{1... | collective-permute-start | bytes 1179656 | tf_op jit(solution)/shard_map/ppermute | solution.py:280
  24.6 21.9 %collective-permute-start.8 = (bf16[3,256,256]{2,1,0:T(8,128)(2,1)S(1)}, bf16[3,256,256]{2,1,0:T(8,128)(2,1)S(1)}, u32[]{:S(2)}, u32[]{:S(2)}) collective-permute-start(bf16[3,256,256]{2,1,0:T(8,128)(2,1)S(1)} %pad_maximum_fusion.1), channel_id=1, source_target_pairs={{0,8},{1,9},{2,10},{3,11},{4,12},{5,13},{6,14},{7,15},{8,0},{9,1},... | collective-permute-start | bytes 1179656 | tf_op jit(solution)/shard_map/ppermute | solution.py:280
  26.4 1.6 %copy-start.1 = (bf16[256,4096]{1,0:T(8,128)(2,1)S(1)}, bf16[256,4096]{1,0:T(8,128)(2,1)}, u32[]{:S(2)}) copy-start(bf16[256,4096]{1,0:T(8,128)(2,1)} %w_ref.2) | copy-start | bytes 6291460
  37.9 1.6 %copy-start = (bf16[256,4096]{1,0:T(8,128)(2,1)S(1)}, bf16[256,4096]{1,0:T(8,128)(2,1)}, u32[]{:S(2)}) copy-start(bf16[256,4096]{1,0:T(8,128)(2,1)} %w_ref.3) | copy-start | bytes 6291460
  59.2 8.5 %collective-permute-start.15 = (bf16[128,64,128]{2,1,0:T(8,128)(2,1)S(1)}, bf16[128,64,128]{2,1,0:T(8,128)(2,1)S(1)}, u32[]{:S(2)}, u32[]{:S(2)}) collective-permute-start(bf16[128,64,128]{2,1,0:T(8,128)(2,1)S(1)} %get-tuple-element.40), channel_id=1, source_target_pairs={{0,16},{16,0},{32,48},{48,32},{64,80},{80,64},{96,112},{112,96},{1... | collective-permute-start | bytes 6291464 | tf_op jit(solution)/shard_map/ppermute | solution.py:315
  63.6 14.9 %collective-permute-start.10 = (bf16[1024,256]{1,0:T(8,128)(2,1)S(1)}, bf16[1024,256]{1,0:T(8,128)(2,1)S(1)}, u32[]{:S(2)}, u32[]{:S(2)}) collective-permute-start(bf16[1024,256]{1,0:T(8,128)(2,1)S(1)} %get-tuple-element.35), channel_id=1, source_target_pairs={{0,12},{1,13},{2,14},{3,15},{4,0},{5,1},{6,2},{7,3},{8,4},{9,5},{1... | collective-permute-start | bytes 1572872 | tf_op jit(solution)/shard_map/ppermute | solution.py:318
  64.8 26.5 %collective-permute-start.9 = (bf16[1024,256]{1,0:T(8,128)(2,1)S(1)}, bf16[1024,256]{1,0:T(8,128)(2,1)S(1)}, u32[]{:S(2)}, u32[]{:S(2)}) collective-permute-start(bf16[1024,256]{1,0:T(8,128)(2,1)S(1)} %get-tuple-element.34), channel_id=1, source_target_pairs={{0,4},{1,5},{2,6},{3,7},{4,8},{5,9},{6,10},{7,11},{8,12},{9,13},{1... | collective-permute-start | bytes 1572872 | tf_op jit(solution)/shard_map/ppermute | solution.py:318
  65.7 27.9 %collective-permute-start.11 = (bf16[1024,256]{1,0:T(8,128)(2,1)S(1)}, bf16[1024,256]{1,0:T(8,128)(2,1)S(1)}, u32[]{:S(2)}, u32[]{:S(2)}) collective-permute-start(bf16[1024,256]{1,0:T(8,128)(2,1)S(1)} %shard_map.84), channel_id=1, source_target_pairs={{0,8},{1,9},{2,10},{3,11},{4,12},{5,13},{6,14},{7,15},{8,0},{9,1},... | collective-permute-start | bytes 1572872 | tf_op jit(solution)/shard_map/ppermute | solution.py:312
  68.2 31.0 %collective-permute-start.19 = (bf16[32,64,128]{2,1,0:T(8,128)(2,1)S(1)}, bf16[32,64,128]{2,1,0:T(8,128)(2,1)S(1)}, u32[]{:S(2)}, u32[]{:S(2)}) collective-permute-start(bf16[32,64,128]{2,1,0:T(8,128)(2,1)S(1)} %get-tuple-element.58), channel_id=1, source_target_pairs={{0,128},{16,144},{32,160},{48,176},{64,192},{80,208},{96,224},{112... | collective-permute-start | bytes 1572872 | tf_op jit(solution)/shard_map/ppermute | solution.py:326
  73.0 25.8 %collective-permute-start.16 = (bf16[16,64,128]{2,1,0:T(8,128)(2,1)S(1)}, bf16[16,64,128]{2,1,0:T(8,128)(2,1)S(1)}, u32[]{:S(2)}, u32[]{:S(2)}) collective-permute-start(bf16[16,64,128]{2,1,0:T(8,128)(2,1)S(1)} %get-tuple-element.62), channel_id=1, source_target_pairs={{0,32},{16,48},{32,64},{48,80},{64,96},{80,112},{96,0},{112,16},{1... | collective-permute-start | bytes 786440 | tf_op jit(solution)/shard_map/ppermute | solution.py:285
  78.5 20.4 %collective-permute-start.17 = (bf16[16,64,128]{2,1,0:T(8,128)(2,1)S(1)}, bf16[16,64,128]{2,1,0:T(8,128)(2,1)S(1)}, u32[]{:S(2)}, u32[]{:S(2)}) collective-permute-start(bf16[16,64,128]{2,1,0:T(8,128)(2,1)S(1)} %get-tuple-element.61), channel_id=1, source_target_pairs={{0,96},{16,112},{32,0},{48,16},{64,32},{80,48},{96,64},{112,80},{1... | collective-permute-start | bytes 786440 | tf_op jit(solution)/shard_map/ppermute | solution.py:285
  91.3 7.9 %collective-permute-start.18 = (bf16[16,64,128]{2,1,0:T(8,128)(2,1)S(1)}, bf16[16,64,128]{2,1,0:T(8,128)(2,1)S(1)}, u32[]{:S(2)}, u32[]{:S(2)}) collective-permute-start(bf16[16,64,128]{2,1,0:T(8,128)(2,1)S(1)} %get-tuple-element.60), channel_id=1, source_target_pairs={{0,64},{16,80},{32,96},{48,112},{64,0},{80,16},{96,32},{112,48},{1... | collective-permute-start | bytes 786440 | tf_op jit(solution)/shard_map/ppermute | solution.py:285
  93.8 23.2 %collective-permute-start.12 = (bf16[256,256]{1,0:T(8,128)(2,1)S(1)}, bf16[256,256]{1,0:T(8,128)(2,1)S(1)}, u32[]{:S(2)}, u32[]{:S(2)}) collective-permute-start(bf16[256,256]{1,0:T(8,128)(2,1)S(1)} %get-tuple-element.66), channel_id=1, source_target_pairs={{0,1},{1,2},{2,3},{3,0},{4,5},{5,6},{6,7},{7,4},{8,9},{9,10},{10,1... | collective-permute-start | bytes 393224 | tf_op jit(solution)/shard_map/ppermute | solution.py:285
  98.8 18.3 %collective-permute-start.13 = (bf16[256,256]{1,0:T(8,128)(2,1)S(1)}, bf16[256,256]{1,0:T(8,128)(2,1)S(1)}, u32[]{:S(2)}, u32[]{:S(2)}) collective-permute-start(bf16[256,256]{1,0:T(8,128)(2,1)S(1)} %get-tuple-element.65), channel_id=1, source_target_pairs={{0,3},{1,0},{2,1},{3,2},{4,7},{5,4},{6,5},{7,6},{8,11},{9,8},{10,9... | collective-permute-start | bytes 393224 | tf_op jit(solution)/shard_map/ppermute | solution.py:285
  99.2 9.1 %collective-permute-start.20 = (bf16[8,64,128]{2,1,0:T(8,128)(2,1)S(1)}, bf16[8,64,128]{2,1,0:T(8,128)(2,1)S(1)}, u32[]{:S(2)}, u32[]{:S(2)}) collective-permute-start(bf16[8,64,128]{2,1,0:T(8,128)(2,1)S(1)} %add_convert_fusion.10), channel_id=1, source_target_pairs={{0,128},{16,144},{32,160},{48,176},{64,192},{80,208},{96,224},{112... | collective-permute-start | bytes 393224 | tf_op jit(solution)/shard_map/ppermute | solution.py:332
  104.2 6.5 %collective-permute-start.21 = (bf16[8,64,128]{2,1,0:T(8,128)(2,1)S(1)}, bf16[8,64,128]{2,1,0:T(8,128)(2,1)S(1)}, u32[]{:S(2)}, u32[]{:S(2)}) collective-permute-start(bf16[8,64,128]{2,1,0:T(8,128)(2,1)S(1)} %get-tuple-element.68), channel_id=1, source_target_pairs={{0,32},{16,48},{32,64},{48,80},{64,96},{80,112},{96,0},{112,16},{1... | collective-permute-start | bytes 393224 | tf_op jit(solution)/shard_map/ppermute | solution.py:285
  107.2 5.6 %collective-permute-start.22 = (bf16[8,64,128]{2,1,0:T(8,128)(2,1)S(1)}, bf16[8,64,128]{2,1,0:T(8,128)(2,1)S(1)}, u32[]{:S(2)}, u32[]{:S(2)}) collective-permute-start(bf16[8,64,128]{2,1,0:T(8,128)(2,1)S(1)} %get-tuple-element.70), channel_id=1, source_target_pairs={{0,96},{16,112},{32,0},{48,16},{64,32},{80,48},{96,64},{112,80},{1... | collective-permute-start | bytes 393224 | tf_op jit(solution)/shard_map/ppermute | solution.py:285
  108.3 6.5 %collective-permute-start.23 = (bf16[8,64,128]{2,1,0:T(8,128)(2,1)S(1)}, bf16[8,64,128]{2,1,0:T(8,128)(2,1)S(1)}, u32[]{:S(2)}, u32[]{:S(2)}) collective-permute-start(bf16[8,64,128]{2,1,0:T(8,128)(2,1)S(1)} %get-tuple-element.69), channel_id=1, source_target_pairs={{0,64},{16,80},{32,96},{48,112},{64,0},{80,16},{96,32},{112,48},{1... | collective-permute-start | bytes 393224 | tf_op jit(solution)/shard_map/ppermute | solution.py:285
  110.6 9.3 %collective-permute-start.14 = (bf16[256,256]{1,0:T(8,128)(2,1)S(1)}, bf16[256,256]{1,0:T(8,128)(2,1)S(1)}, u32[]{:S(2)}, u32[]{:S(2)}) collective-permute-start(bf16[256,256]{1,0:T(8,128)(2,1)S(1)} %get-tuple-element.64), channel_id=1, source_target_pairs={{0,2},{1,3},{2,0},{3,1},{4,6},{5,7},{6,4},{7,5},{8,10},{9,11},{10,... | collective-permute-start | bytes 393224 | tf_op jit(solution)/shard_map/ppermute | solution.py:285
